TPU v7x, 32 devices: a whole 2x2x4 slice. The times are simulated.
32 devices in a mesh: parts: 2 (over x), tm: 16 (over z, y, core).
Axes of the slice: x: 2, y: 2, z: 4, core: 2. Of those that a mesh axis runs over, the one named last changes fastest.
Arguments:
- currents: bfloat16 [49152, 1024], P('tm', 'parts'), parts along dimension 1, may hold values from -5 to 5
- seed_on_tension: bfloat16 [49152, 1024], P('tm', 'parts'), parts along dimension 1, may hold values from -6 to 6
- mode_diffusivity_factor: float32 [32, 98304], P(None, ('parts', 'tm')), parts along dimension 1, may hold values from 0.25 to 34410
- decay_rates: float32 [32], replicated, may hold values from 6.1035156e-06 to 0.34
- fit_weights: float32 [32], replicated, may hold values from 0.06 to 0.3
- counts: int32 [1024], P('parts'), parts along dimension 0, may hold values from 1 to 16
Outputs:
- tension_at_end: bfloat16 [49152, 1024], P('tm', 'parts'), parts along dimension 1
- gradient_wrt_draw: bfloat16 [49152, 1024], P('tm', 'parts'), parts along dimension 1
- softened_peak_tension: float32 [1024], P('parts'), parts along dimension 0
There are 2 independent parts, one for each index of `parts`. A program takes and returns all parts, laid end to end along the dimension named above; an argument that names none is the same for every part. Nothing has to cross between parts.
All inputs are finite; a program needn't handle non-finite values.
Results may differ from a plain program's by a relative error of at most 0.0053.
Values sent between devices are 32-bit elements; how exact they have to be, the bound alone decides.
No kernel may reach another device: no remote copies, remote signals or barrier semaphores. Data moves between devices by JAX's collectives and lax.ppermute only.
A program may use at most 192 MiB of HBM per device.

v0:
```python
import jax
import jax.numpy as jnp
from jax import lax
from jax.sharding import PartitionSpec as P

KERNEL_SPAN = 768


SHARPNESS = 4.0
FAR_AWAY = 1e30


def entering(part, axis, combine, identity, reverse):
    count = lax.axis_size(axis)
    place = lax.axis_index(axis)
    ahead = count - 1 - place if reverse else place
    gathered = jax.tree.map(lambda a: lax.all_gather(a, axis), part)
    state = jax.tree.map(lambda a, e: jnp.zeros_like(a) + jnp.asarray(e, a.dtype), part, identity)

    def one(hop, state):
        source = count - 1 - hop if reverse else hop
        return combine(
            state, jax.tree.map(lambda a: lax.dynamic_index_in_dim(a, source, 0, False), gathered)
        )

    return lax.fori_loop(0, ahead, one, state)


def combine_states(earlier, latter):
    return (earlier[0] * latter[0], latter[0][:, None] * earlier[1] + latter[1])


def body(currents, seed_on_tension, mode_diffusivity_factor, decay_rates, fit_weights, counts):
    samples, conductor_total = currents.shape
    kernel_spans = samples // KERNEL_SPAN
    mode_count = decay_rates.shape[0]
    mode_gains = fit_weights * jnp.sqrt(decay_rates)
    length_scale = counts.astype(jnp.float32) / 4.0
    prefix = jnp.cumsum(
        mode_diffusivity_factor.reshape(mode_count, kernel_spans, KERNEL_SPAN), axis=2
    ).transpose(1, 0, 2)
    closing_instant = prefix[:, :, -1]
    prefix_rows = prefix.transpose(0, 2, 1)
    row_ids = lax.broadcasted_iota(jnp.int32, (KERNEL_SPAN, KERNEL_SPAN), 0)
    col_ids = lax.broadcasted_iota(jnp.int32, (KERNEL_SPAN, KERNEL_SPAN), 1)
    lower_part = (row_ids >= col_ids)[None]
    kernel_list = []
    for position in range(kernel_spans):
        block_kernel = jnp.zeros((KERNEL_SPAN, KERNEL_SPAN), jnp.float32)
        for first_mode in range(0, mode_count, 8):
            rate_part = decay_rates[first_mode : first_mode + 8]
            gain_part = mode_gains[first_mode : first_mode + 8]
            part_prefix = prefix[position, first_mode : first_mode + 8]
            spread = part_prefix[:, :, None] - part_prefix[:, None, :]
            spread = jnp.where(lower_part, spread, FAR_AWAY)
            block_kernel = block_kernel + jnp.sum(
                gain_part[:, None, None] * jnp.exp(-rate_part[:, None, None] * spread), axis=0
            )
        kernel_list.append(block_kernel.astype(jnp.bfloat16))
    kernel = jnp.stack(kernel_list)
    back_table = jnp.exp(-decay_rates[None, None, :] * (closing_instant[:, None, :] - prefix_rows))
    start_table = mode_gains * jnp.exp(-decay_rates * prefix_rows)
    decays = jnp.exp(-decay_rates[None, :] * closing_instant)
    cur_blocks = currents.reshape(kernel_spans, KERNEL_SPAN, conductor_total)
    cot_blocks = seed_on_tension.reshape(kernel_spans, KERNEL_SPAN, conductor_total)
    local_fwd = jnp.einsum("bts,bsw->btw", kernel, cur_blocks, preferred_element_type=jnp.float32)
    fresh_fwd = jnp.einsum(
        "bsm,bsw->bmw",
        back_table.astype(jnp.bfloat16),
        cur_blocks,
        preferred_element_type=jnp.float32,
    )
    local_adj = jnp.einsum("bts,btw->bsw", kernel, cot_blocks, preferred_element_type=jnp.float32)
    fresh_adj = jnp.einsum(
        "btm,btw->bmw",
        start_table.astype(jnp.bfloat16),
        cot_blocks,
        preferred_element_type=jnp.float32,
    )
    dev_decay = jnp.ones((mode_count,), jnp.float32)
    resident_mode_values = jnp.zeros((mode_count, conductor_total), jnp.float32)
    for position in range(kernel_spans):
        dev_decay = dev_decay * decays[position]
        resident_mode_values = (
            decays[position][:, None] * resident_mode_values + fresh_fwd[position]
        )
    shard_adjoint_rows = jnp.zeros((mode_count, conductor_total), jnp.float32)
    for position in reversed(range(kernel_spans)):
        shard_adjoint_rows = decays[position][:, None] * shard_adjoint_rows + fresh_adj[position]
    no_decay = jnp.ones((mode_count,), jnp.float32)
    no_state = jnp.zeros((mode_count, conductor_total), jnp.float32)
    forward_pair = entering(
        (dev_decay, resident_mode_values), "tm", combine_states, (no_decay, no_state), False
    )
    adjoint_pair = entering(
        (dev_decay, shard_adjoint_rows), "tm", combine_states, (no_decay, no_state), True
    )
    state_in = forward_pair[1]
    adjoint_in = adjoint_pair[1]
    mode_state = state_in
    full_blocks = []
    for position in range(kernel_spans):
        carried_in = jnp.dot(
            start_table[position],
            mode_state,
            precision=lax.Precision.HIGHEST,
            preferred_element_type=jnp.float32,
        )
        full_blocks.append(length_scale[None, :] * (local_fwd[position] + carried_in))
        if position + 1 < kernel_spans:
            mode_state = decays[position][:, None] * mode_state + fresh_fwd[position]
    stress_full = jnp.stack(full_blocks)
    scores = SHARPNESS * stress_full
    local_high = jnp.max(scores, axis=(0, 1))
    highest = lax.pmax(local_high, "tm")
    amount = lax.psum(jnp.sum(jnp.exp(scores - highest), axis=(0, 1)), "tm")
    softened_peak_tension = (highest + jnp.log(amount)) / SHARPNESS
    adjoint_state = adjoint_in
    reversed_blocks = []
    for position in reversed(range(kernel_spans)):
        carried_in = jnp.dot(
            back_table[position],
            adjoint_state,
            precision=lax.Precision.HIGHEST,
            preferred_element_type=jnp.float32,
        )
        reversed_blocks.append(
            (length_scale[None, :] * (local_adj[position] + carried_in)).astype(jnp.bfloat16)
        )
        if position > 0:
            adjoint_state = decays[position][:, None] * adjoint_state + fresh_adj[position]
    gradient_wrt_draw = jnp.stack(reversed_blocks[::-1]).reshape(samples, conductor_total)
    tension_at_end = stress_full.astype(jnp.bfloat16).reshape(samples, conductor_total)
    return (tension_at_end, gradient_wrt_draw, softened_peak_tension)


def solution(mesh):
    placed = (P("tm", "parts"), P("tm", "parts"), P(None, ("parts", "tm")), P(), P(), P("parts"))
    return jax.shard_map(
        body,
        mesh=mesh,
        in_specs=placed,
        out_specs=(P("tm", "parts"), P("tm", "parts"), P("parts")),
        check_vma=False,
    )
```

profile of v0, /device:TPU:0, one launch (start us, length us, event | category | flops | bytes accessed | tf_op | source)
XLA Modules:
  0.0 303.3 jit_solution(5276616047635515305)
XLA Ops:
  7.2 2.1 reshape.270
  9.4 2.0 copy.54
  11.4 12.3 %reduce-window.6 = f32[32,4,6,128]{3,0,1,2:T(8,128)S(1)} reduce-window(f32[32,4,6,128]{3,0,1,2:T(8,128)} %copy.54, f32[]{:T(128)} %constant.65.clone.1), window={size=1x1x1x128 pad=0_0x0_0x0_0x127_0}, to_apply=%region_0.0 | reduce-window | flops 12484608 | bytes 786436 | tf_op jit(solution)/shard_map/reduce-window
  24.4 0.7 fusion.53
  26.0 2.8 fusion.41
  29.4 0.7 copy-done.14
  30.1 0.8 slice_add_fusion
  31.0 0.7 all-gather.6.cloned.1.call-update
  31.7 1.6 slice_bitcast_fusion.27
  33.4 0.6 slice_negate_fusion.3
  34.3 22.8 %multiply_reduce_fusion.15 = (f32[768,768]{1,0:T(8,128)}, f32[768,768]{1,0:T(8,128)}, f32[768,768]{1,0:T(8,128)}, f32[768,768]{1,0:T(8,128)}) fusion(f32[8,768]{1,0:T(8,128)S(1)} %get-tuple-element.194, f32[8]{0:T(128)S(1)} %get-tuple-element.210, f32[8]{0:T(128)S(1)} %get-tuple-element.206, pred[768,768]{1,0:T(8,128)(4,1)S(1)} %iota_compare_fusion, ...), kind=kLoop, calls=%fused_computation.19 | loop fusion | flops 92012544 | bytes 10125376 | tf_op jit(solution)/shard_map/reduce_sum | solution.py:56
  57.0 72.1 %multiply_reduce_fusion.14 = (f32[768,768]{1,0:T(8,128)}, f32[768,768]{1,0:T(8,128)}, f32[768,768]{1,0:T(8,128)}, f32[768,768]{1,0:T(8,128)}, f32[768,768]{1,0:T...) fusion(f32[8,768]{1,0:T(8,128)} %get-tuple-element.193, ...), kind=kLoop, calls=%fused_computation.18 | loop fusion | flops 276037632 | bytes 29196480 | tf_op jit(solution)/shard_map/reduce_sum | solution.py:56
  129.1 9.0 %fusion.28 = (bf16[1,768,768]{2,1,0:T(8,128)(2,1)}, bf16[1,768,768]{2,1,0:T(8,128)(2,1)}) fusion(f32[768,768]{1,0:T(8,128)} %get-tuple-element.156, f32[768,768]{1,0:T(8,128)} %get-tuple-element.152, f32[768,768]{1,0:T(8,128)} %get-tuple-element.137, f32[768,768]{1,0:T(8,128)} %get-tuple-element.133, f32[768,768]{1,0:T(8,128)} %get-tuple-element.155, ...), kind=kLoop, calls=%fused_computation.66 | loop fusion | flops 4718592 | bytes 21233664 | tf_op jit(solution)/shard_map/convert_element_type | solution.py:59
  138.1 7.1 %fusion.30 = (bf16[1,768,768]{2,1,0:T(8,128)(2,1)}, bf16[1,768,768]{2,1,0:T(8,128)(2,1)}) fusion(f32[768,768]{1,0:T(8,128)} %get-tuple-element.154, f32[768,768]{1,0:T(8,128)} %get-tuple-element.150, f32[768,768]{1,0:T(8,128)S(1)} %copy-done.11, f32[768,768]{1,0:T(8,128)S(1)} %copy-done.13, f32[768,768]{1,0:T(8,128)} %get-tuple-element.153, ...), kind=kLoop, calls=%fused_computation.68 | loop fusion | flops 4718592 | bytes 21233664 | tf_op jit(solution)/shard_map/convert_element_type | solution.py:59
  145.3 7.8 %fusion.34 = f32[4,768,512]{2,1,0:T(8,128)} fusion(bf16[4,768,512]{2,1,0:T(8,128)(2,1)S(1)} %bitcast.251, bf16[1,768,768]{2,1,0:T(8,128)(2,1)} %get-tuple-element.217, bf16[1,768,768]{2,1,0:T(8,128)(2,1)} %get-tuple-element.216, bf16[1,768,768]{2,1,0:T(8,128)(2,1)} %get-tuple-element.215, bf16[1,768,768]{2,1,0:T(8,128)(2,1)} %get-tuple-element.214), kind=kOutput, calls=%fused_computation.72 | convolution fusion | flops 2422996992 | bytes 14155776 | tf_op jit(solution)/shard_map/bts,bsw->btw/dot_general | solution.py:66
  153.1 4.8 %fusion.33 = f32[4,768,512]{2,1,0:T(8,128)} fusion(bf16[4,768,512]{2,1,0:T(8,128)(2,1)S(1)} %bitcast.255, bf16[1,768,768]{2,1,0:T(8,128)(2,1)S(1)} %copy-done.19, bf16[1,768,768]{2,1,0:T(8,128)(2,1)S(1)} %copy-done.18, bf16[1,768,768]{2,1,0:T(8,128)(2,1)S(1)} %copy-done.17, bf16[1,768,768]{2,1,0:T(8,128)(2,1)S(1)} %copy-done.16), kind=kOutput, calls=%fused_computation.71 | convolution fusion | flops 2422996992 | bytes 14155776 | tf_op jit(solution)/shard_map/bts,btw->bsw/dot_general | solution.py:73
  157.9 23.1 %all-gather = f32[16,1,32]{2,1,0:T(1,128)S(1)} all-gather(f32[1,1,32]{2,1,0:T(1,128)S(1)} %copy-done.28), channel_id=1, replica_groups=mesh['parts'=2,'tm'=16] {'tm'}, dimensions={0}, use_global_device_ids=true | all-gather | bytes 2176 | tf_op jit(solution)/shard_map/all_gather | solution.py:17
  181.1 4.3 %fusion.23 = f32[1,768,512]{2,1,0:T(8,128)} fusion(f32[4,768,512]{2,1,0:T(8,128)} %fusion.34, f32[32,512]{1,0:T(8,128)S(1)} %get-tuple-element.131, f32[512]{0:T(512)S(1)} %convert_multiply_fusion, f32[4,768,32]{1,2,0:T(8,128)} %copy-done.8), kind=kOutput, calls=%fused_computation.61 | convolution fusion | flops 151781376 | bytes 3311616 | tf_op jit(solution)/shard_map/dot_general | solution.py:103
  185.4 1.0 bitcast_add_fusion.8
  186.3 4.1 %fusion.17 = f32[1,768,512]{2,1,0:T(8,128)} fusion(f32[4,768,512]{2,1,0:T(8,128)} %fusion.34, f32[32,512]{1,0:T(8,128)S(1)} %bitcast_add_fusion.8, f32[512]{0:T(512)S(1)} %convert_multiply_fusion, f32[4,768,32]{1,2,0:T(8,128)} %copy-done.8), kind=kOutput, calls=%fused_computation.53 | convolution fusion | flops 151781376 | bytes 3311616 | tf_op jit(solution)/shard_map/dot_general | solution.py:103
  190.4 3.5 %fusion.20 = f32[1,768,512]{2,1,0:T(8,128)} fusion(f32[4,768,512]{2,1,0:T(8,128)S(1)} %copy-done.5, f32[512]{0:T(512)S(1)} %convert_multiply_fusion, f32[4,768,32]{1,2,0:T(8,128)S(1)} %copy-done.9, f32[32,512]{1,0:T(8,128)S(1)} %get-tuple-element.131, f32[4,32,512]{2,1,0:T(8,128)} %copy-done.14, f32[32]{0:T(128)S(1)} %copy-done.27), kind=kOutput, calls=%fused_computation.57 | convolution fusion | flops 151814144 | bytes 3377664 | tf_op jit(solution)/shard_map/dot_general | solution.py:103
  193.9 3.5 %fusion.14 = f32[1,768,512]{2,1,0:T(8,128)} fusion(f32[4,768,512]{2,1,0:T(8,128)S(1)} %copy-done.5, f32[512]{0:T(512)S(1)} %convert_multiply_fusion, f32[4,768,32]{1,2,0:T(8,128)S(1)} %copy-done.9, f32[32,512]{1,0:T(8,128)S(1)} %bitcast_add_fusion.8, f32[4,32,512]{2,1,0:T(8,128)} %copy-done.14, f32[32]{0:T(128)S(1)} %copy-done.25), kind=kOutput, calls=%fused_computation.49 | convolution fusion | flops 151814144 | bytes 3377664 | tf_op jit(solution)/shard_map/dot_general | solution.py:103
  197.3 14.0 %while.27 = (s32[]{:T(128)}, f32[32,512]{1,0:T(8,128)S(1)}, s32[]{:T(128)}, f32[16,32]{1,0:T(8,128)S(1)}, f32[16,32,512]{2,1,0:T(8,128)}, /*index=5*/s32[]{:T(128)}, s32[]{:T(128)}, s32[]{:T(128)}, s32[]{:T(128)}) while((s32[]{:T(128)}, f32[32,512]{1,0:T(8,128)S(1)}, s32[]{:T(128)}, f32[16,32]{1,0:T(8,128)S(1)}, f32[16,32,512]{2,1,0:T(8,128)}, ...), condition=%wide.region_21.22_spmd, body=%wide.region_20.21_spmd.sunk | while | flops 32774 | bytes 197139 | solution.py:26
  197.4 0.9 bitcast_add_fusion.15
  198.3 0.9 bitcast_add_fusion.15
  199.2 0.9 bitcast_add_fusion.15
  200.2 0.9 bitcast_add_fusion.15
  201.1 0.9 bitcast_add_fusion.15
  202.0 0.9 bitcast_add_fusion.15
  203.0 0.9 bitcast_add_fusion.15
  203.9 0.9 bitcast_add_fusion.15
  204.8 0.9 bitcast_add_fusion.15
  205.8 0.9 bitcast_add_fusion.15
  206.7 0.9 bitcast_add_fusion.15
  207.6 0.9 bitcast_add_fusion.15
  208.6 0.9 bitcast_add_fusion.15
  209.5 0.9 bitcast_add_fusion.15
  210.4 0.9 bitcast_add_fusion.15
  211.5 4.1 %fusion.24 = bf16[1,768,512]{2,1,0:T(8,128)(2,1)} fusion(f32[4,768,512]{2,1,0:T(8,128)} %fusion.33, f32[512]{0:T(512)S(1)} %convert_multiply_fusion, f32[4,768,32]{1,2,0:T(8,128)} %copy-done.6, f32[32,512]{1,0:T(8,128)S(1)} %bitcast_add_fusion.4, f32[4,32,512]{2,1,0:T(8,128)S(1)} %fusion.41, f32[32]{0:T(128)S(1)} %copy-done.23), kind=kOutput, calls=%fused_computation.62 | convolution fusion | flops 152207360 | bytes 2591232 | tf_op jit(solution)/shard_map/dot_general | solution.py:121
  215.5 3.9 %fusion.25 = bf16[1,768,512]{2,1,0:T(8,128)(2,1)} fusion(f32[32,512]{1,0:T(8,128)S(1)} %bitcast_add_fusion.4, f32[4,768,512]{2,1,0:T(8,128)} %fusion.33, f32[512]{0:T(512)S(1)} %convert_multiply_fusion, f32[4,768,32]{1,2,0:T(8,128)} %copy-done.6), kind=kOutput, calls=%fused_computation.63 | convolution fusion | flops 152174592 | bytes 2525184 | tf_op jit(solution)/shard_map/dot_general | solution.py:121
  219.4 3.8 %fusion.26 = bf16[1,768,512]{2,1,0:T(8,128)(2,1)} fusion(f32[4,768,512]{2,1,0:T(8,128)} %fusion.33, f32[512]{0:T(512)S(1)} %convert_multiply_fusion, f32[4,768,32]{1,2,0:T(8,128)S(1)} %copy-done.7, f32[32,512]{1,0:T(8,128)S(1)} %get-tuple-element.132, f32[4,32,512]{2,1,0:T(8,128)S(1)} %fusion.41, f32[32]{0:T(128)S(1)} %get-tuple-element.198), kind=kOutput, calls=%fused_computation.64 | convolution fusion | flops 152207360 | bytes 2591232 | tf_op jit(solution)/shard_map/dot_general | solution.py:121
  223.2 3.8 %fusion.27 = bf16[1,768,512]{2,1,0:T(8,128)(2,1)} fusion(f32[32,512]{1,0:T(8,128)S(1)} %get-tuple-element.132, f32[4,768,512]{2,1,0:T(8,128)} %fusion.33, f32[512]{0:T(512)S(1)} %convert_multiply_fusion, f32[4,768,32]{1,2,0:T(8,128)S(1)} %copy-done.7), kind=kOutput, calls=%fused_computation.65 | convolution fusion | flops 152174592 | bytes 2525184 | tf_op jit(solution)/shard_map/dot_general | solution.py:121
  227.0 0.9 multiply_reduce_fusion.16
  227.9 2.1 fusion.32
  229.9 29.8 %pmax.7 = f32[512]{0:T(512)S(1)} all-reduce(f32[512]{0:T(512)S(1)} %multiply_reduce_fusion.16), channel_id=1, replica_groups=mesh['parts'=2,'tm'=16] {'tm'}, use_global_device_ids=true, to_apply=%region_23.24 | all-reduce | flops 512 | bytes 4096 | tf_op jit(solution)/shard_map/pmax | solution.py:115
  259.7 3.4 %exponential_reduce_fusion = f32[512]{0:T(512)S(1)} fusion(f32[512]{0:T(512)S(1)} %pmax.7, f32[1,768,512]{2,1,0:T(8,128)} %fusion.14, f32[1,768,512]{2,1,0:T(8,128)} %fusion.17, f32[1,768,512]{2,1,0:T(8,128)} %fusion.20, f32[1,768,512]{2,1,0:T(8,128)} %fusion.23), kind=kLoop, calls=%fused_computation.21 | loop fusion | flops 9436672 | bytes 6295552 | tf_op jit(solution)/shard_map/reduce_sum | solution.py:116
  263.1 29.5 %psum.7 = f32[512]{0:T(512)S(1)} all-reduce(f32[512]{0:T(512)S(1)} %exponential_reduce_fusion), channel_id=1, replica_groups=mesh['parts'=2,'tm'=16] {'tm'}, use_global_device_ids=true, to_apply=%region_25.26 | all-reduce | flops 512 | bytes 4096 | tf_op jit(solution)/shard_map/psum | solution.py:116
  293.2 3.2 %pad_maximum_fusion.2 = bf16[4,768,512]{2,1,0:T(8,128)(2,1)} fusion(bf16[1,768,512]{2,1,0:T(8,128)(2,1)} %fusion.27, bf16[1,768,512]{2,1,0:T(8,128)(2,1)} %fusion.26, bf16[1,768,512]{2,1,0:T(8,128)(2,1)} %fusion.25, bf16[1,768,512]{2,1,0:T(8,128)(2,1)} %fusion.24), kind=kLoop, calls=%fused_computation.24 | loop fusion | flops 4718592 | bytes 6291456 | tf_op jit(solution)/shard_map/stack | solution.py:132
  (99 shorter events, 3.4 us)
Async XLA Ops:
  7.2 21.6 %copy-start = (bf16[3072,512]{1,0:T(8,128)(2,1)S(1)}, bf16[3072,512]{1,0:T(8,128)(2,1)}, u32[]{:S(2)}) copy-start(bf16[3072,512]{1,0:T(8,128)(2,1)} %param.10) | copy-start | bytes 9437188
  7.2 173.9 %all-gather.4.cloned.1.call-start = ((), (), s32[]{:S(2)}) async-start(), calls=%async_computation | async-start | bytes 1114112 | tf_op jit(solution)/shard_map/all_gather | solution.py:17
  24.2 1.7 copy-start.15
  25.7 5.2 %copy-start.22 = (f32[32]{0:T(128)}, f32[32]{0:T(128)S(1)}, u32[]{:S(2)}) copy-start(f32[32]{0:T(128)S(1)} %get-tuple-element.201) | copy-start | bytes 388
  25.7 5.2 %copy-start.24 = (f32[32]{0:T(128)}, f32[32]{0:T(128)S(1)}, u32[]{:S(2)}) copy-start(f32[32]{0:T(128)S(1)} %get-tuple-element.200) | copy-start | bytes 388
  25.7 5.2 %copy-start.26 = (f32[32]{0:T(128)}, f32[32]{0:T(128)S(1)}, u32[]{:S(2)}) copy-start(f32[32]{0:T(128)S(1)} %get-tuple-element.197) | copy-start | bytes 388
  25.9 2.9 copy-start.6
  25.9 3.5 %copy-start.8 = (f32[4,768,32]{1,2,0:T(8,128)}, f32[4,768,32]{1,2,0:T(8,128)S(1)}, u32[]{:S(2)}) copy-start(f32[4,768,32]{1,2,0:T(8,128)S(1)} %get-tuple-element.178) | copy-start | bytes 1179652
  25.9 7.5 %copy-start.21 = (f32[32]{0:T(128)S(1)}, f32[32]{0:T(128)}, u32[]{:S(2)}) copy-start(f32[32]{0:T(128)} %param.13) | copy-start | bytes 388
  29.4 0.7 copy-start.14
  30.9 166.4 %all-gather.6.cloned.1.call-start = ((), (), s32[]{:S(2)}) async-start(), calls=%async_computation.1 | async-start | bytes 1114112 | tf_op jit(solution)/shard_map/all_gather | solution.py:17
  34.2 22.8 %copy-start.20 = (pred[768,768]{1,0:T(8,128)(4,1)}, pred[768,768]{1,0:T(8,128)(4,1)S(1)}, u32[]{:S(2)}) copy-start(pred[768,768]{1,0:T(8,128)(4,1)S(1)} %iota_compare_fusion) | copy-start | bytes 1769476
  34.2 22.8 %copy-start.30 = (f32[8]{0:T(128)S(1)}, f32[8]{0:T(128)}, u32[]{:S(2)}) copy-start(f32[8]{0:T(128)} %get-tuple-element.212) | copy-start | bytes 100
  129.1 9.0 %copy-start.11 = (f32[768,768]{1,0:T(8,128)S(1)}, f32[768,768]{1,0:T(8,128)}, u32[]{:S(2)}) copy-start(f32[768,768]{1,0:T(8,128)} %get-tuple-element.139) | copy-start | bytes 7077892
  129.1 9.0 %copy-start.12 = (f32[768,768]{1,0:T(8,128)S(1)}, f32[768,768]{1,0:T(8,128)}, u32[]{:S(2)}) copy-start(f32[768,768]{1,0:T(8,128)} %get-tuple-element.140) | copy-start | bytes 7077892
  129.1 9.0 %copy-start.13 = (f32[768,768]{1,0:T(8,128)S(1)}, f32[768,768]{1,0:T(8,128)}, u32[]{:S(2)}) copy-start(f32[768,768]{1,0:T(8,128)} %get-tuple-element.135) | copy-start | bytes 7077892
  145.2 7.8 %copy-start.10 = (bf16[3072,512]{1,0:T(8,128)(2,1)S(1)}, bf16[3072,512]{1,0:T(8,128)(2,1)}, u32[]{:S(2)}) copy-start(bf16[3072,512]{1,0:T(8,128)(2,1)} %param.11) | copy-start | bytes 9437188
  145.2 7.8 %copy-start.16 = (bf16[1,768,768]{2,1,0:T(8,128)(2,1)S(1)}, bf16[1,768,768]{2,1,0:T(8,128)(2,1)}, u32[]{:S(2)}) copy-start(bf16[1,768,768]{2,1,0:T(8,128)(2,1)} %get-tuple-element.214) | copy-start | bytes 3538948
  145.2 7.8 %copy-start.17 = (bf16[1,768,768]{2,1,0:T(8,128)(2,1)S(1)}, bf16[1,768,768]{2,1,0:T(8,128)(2,1)}, u32[]{:S(2)}) copy-start(bf16[1,768,768]{2,1,0:T(8,128)(2,1)} %get-tuple-element.215) | copy-start | bytes 3538948
  145.2 7.8 %copy-start.18 = (bf16[1,768,768]{2,1,0:T(8,128)(2,1)S(1)}, bf16[1,768,768]{2,1,0:T(8,128)(2,1)}, u32[]{:S(2)}) copy-start(bf16[1,768,768]{2,1,0:T(8,128)(2,1)} %get-tuple-element.216) | copy-start | bytes 3538948
  145.3 7.8 %copy-start.19 = (bf16[1,768,768]{2,1,0:T(8,128)(2,1)S(1)}, bf16[1,768,768]{2,1,0:T(8,128)(2,1)}, u32[]{:S(2)}) copy-start(bf16[1,768,768]{2,1,0:T(8,128)(2,1)} %get-tuple-element.217) | copy-start | bytes 3538948
  153.1 4.9 %copy-start.28 = (f32[1,1,32]{2,1,0:T(1,128)S(1)}, f32[1,1,32]{2,1,0:T(1,128)}, u32[]{:S(2)}) copy-start(f32[1,1,32]{2,1,0:T(1,128)} %get-tuple-element.199) | copy-start | bytes 388
  153.1 28.0 %copy-start.29 = (s32[512]{0:T(512)S(1)}, s32[512]{0:T(512)}, u32[]{:S(2)}) copy-start(s32[512]{0:T(512)} %param.15) | copy-start | bytes 6148
  153.1 32.3 %copy-start.23 = (f32[32]{0:T(128)S(1)}, f32[32]{0:T(128)}, u32[]{:S(2)}) copy-start(f32[32]{0:T(128)} %copy-done.22) | copy-start | bytes 388
  153.1 32.3 %copy-start.27 = (f32[32]{0:T(128)S(1)}, f32[32]{0:T(128)}, u32[]{:S(2)}) copy-start(f32[32]{0:T(128)} %copy-done.26) | copy-start | bytes 388
  181.1 9.3 %copy-start.5 = (f32[4,768,512]{2,1,0:T(8,128)S(1)}, f32[4,768,512]{2,1,0:T(8,128)}, u32[]{:S(2)}) copy-start(f32[4,768,512]{2,1,0:T(8,128)} %fusion.34) | copy-start | bytes 18874372
  181.1 9.3 %copy-start.9 = (f32[4,768,32]{1,2,0:T(8,128)S(1)}, f32[4,768,32]{1,2,0:T(8,128)}, u32[]{:S(2)}) copy-start(f32[4,768,32]{1,2,0:T(8,128)} %copy-done.8) | copy-start | bytes 1179652
  181.1 12.8 %copy-start.25 = (f32[32]{0:T(128)S(1)}, f32[32]{0:T(128)}, u32[]{:S(2)}) copy-start(f32[32]{0:T(128)} %copy-done.24) | copy-start | bytes 388
  211.3 8.1 %copy-start.7 = (f32[4,768,32]{1,2,0:T(8,128)S(1)}, f32[4,768,32]{1,2,0:T(8,128)}, u32[]{:S(2)}) copy-start(f32[4,768,32]{1,2,0:T(8,128)} %copy-done.6) | copy-start | bytes 1179652
  211.4 15.6 %copy-start.1 = (f32[1,768,512]{2,1,0:T(8,128)S(1)}, f32[1,768,512]{2,1,0:T(8,128)}, u32[]{:S(2)}) copy-start(f32[1,768,512]{2,1,0:T(8,128)} %fusion.23) | copy-start | bytes 4718596
  211.4 15.6 %copy-start.2 = (f32[1,768,512]{2,1,0:T(8,128)S(1)}, f32[1,768,512]{2,1,0:T(8,128)}, u32[]{:S(2)}) copy-start(f32[1,768,512]{2,1,0:T(8,128)} %fusion.17) | copy-start | bytes 4718596
  211.5 15.6 %copy-start.3 = (f32[1,768,512]{2,1,0:T(8,128)S(1)}, f32[1,768,512]{2,1,0:T(8,128)}, u32[]{:S(2)}) copy-start(f32[1,768,512]{2,1,0:T(8,128)} %fusion.20) | copy-start | bytes 4718596
  211.5 15.5 %copy-start.4 = (f32[1,768,512]{2,1,0:T(8,128)S(1)}, f32[1,768,512]{2,1,0:T(8,128)}, u32[]{:S(2)}) copy-start(f32[1,768,512]{2,1,0:T(8,128)} %fusion.14) | copy-start | bytes 4718596
Sparse Core Ops, SparseCore 0:
  31.1 40.6 all-gather.3
  73.9 36.8 all-gather.5
where the time goes:
time: 305 us; the launch traced here: 303 us
  other arithmetic  152 us (50%)
  blocking collectives  82.4 us (27%)
  matrix products  46.8 us (15%)
  between operations  14.4 us (5%)
  local copies, waits for them, and re-layouts  7.32 us (2%)
    reduce_sum x2, other arithmetic, body(): jnp.sum(gain_part[:, None, None] * jnp.exp(-rate_part[:, None, None] * sp...  94.9 us
    pmax x1, blocking collectives, body(): highest = lax.pmax(local_high, 'tm')  29.8 us
    psum x1, blocking collectives, body(): amount = lax.psum(jnp.sum(jnp.exp(scores - highest), axis=(0, 1)), 'tm')  29.5 us
    all_gather x1, blocking collectives, entering(): gathered = jax.tree.map(lambda a: lax.all_gather(a, axis), part)  23.1 us
    convert_element_type x2, other arithmetic, body(): kernel_list.append(block_kernel.astype(jnp.bfloat16))  16.1 us
    dot_general x4, matrix products, body(): jnp.dot(back_table[position], adjoint_state, precision=lax.Precision.HIGH...  15.5 us
    dot_general x4, matrix products, body(): jnp.dot(start_table[position], mode_state, precision=lax.Precision.HIGHES...  15.2 us
    add x15, other arithmetic, combine_states(): return (earlier[0] * latter[0], latter[0][:, None] * earlier[1] + latter[1])  13.8 us
  transfers between devices with their start and end apart: 2, of which 0 were waited for; matrix products, arithmetic and copies ran while one was open for 47% of the time, Pallas kernels for 0%

commit v1 on v0

v1 whole, which is shorter than its diff:
```python
import functools
import math

import jax
import jax.numpy as jnp
from jax import lax
from jax.experimental import pallas as pl
from jax.experimental.pallas import tpu as pltpu
from jax.sharding import PartitionSpec as P

CHUNK = 128
LEVELS = 7
SHARPNESS = 4.0
LOG2E = math.log2(math.e)
LN2 = math.log(2.0)
F32 = jnp.float32
BF16 = jnp.bfloat16


def as_column(row):
    m = row.shape[1]
    r = lax.broadcasted_iota(jnp.int32, (m, m), 0)
    c = lax.broadcasted_iota(jnp.int32, (m, m), 1)
    return jnp.sum(jnp.where(r == c, jnp.broadcast_to(row, (m, m)), 0.0), axis=1, keepdims=True)


def rates_and_gains(rates_ref, fit_ref):
    rates = as_column(rates_ref[...])
    gains = as_column(fit_ref[...]) * jnp.sqrt(rates)
    return rates * LOG2E, gains


def doubling(heat, with_levels):
    lane = lax.broadcasted_iota(jnp.int32, heat.shape, 1)
    pre, suf = heat, jnp.zeros_like(heat)
    tables = []
    for level in range(LEVELS):
        half = 1 << level
        second = (lane & half) != 0
        if with_levels:
            tables.append(jnp.exp2(-jnp.where(second, pre, suf)))
        total = pre + suf
        sibling = jnp.where(
            second, pltpu.roll(total, half, 1), pltpu.roll(total, CHUNK - half, 1)
        )
        pre = jnp.where(second, pre + sibling, pre)
        suf = jnp.where(second, suf, suf + sibling)
    return pre, suf, tables


def wide(a, times):
    return jnp.concatenate([a] * times, axis=1)


def totals_kernel(
    heat_ref, rates_ref, fit_ref, cur_ref, cot_ref,
    fresh_f_ref, fresh_a_ref, decay_ref, msg_ref, tf, ta, dc,
):
    step = pl.program_id(0)
    modes = heat_ref.shape[0]
    wires = cur_ref.shape[1]
    reps = wires // CHUNK

    @pl.when(step == 0)
    def _():
        tf[...] = jnp.zeros_like(tf)
        ta[...] = jnp.zeros_like(ta)
        dc[...] = jnp.ones_like(dc)

    speed, gains = rates_and_gains(rates_ref, fit_ref)
    for c in range(heat_ref.shape[1] // CHUNK):
        span = slice(c * CHUNK, (c + 1) * CHUNK)
        rows = slice(c * modes, (c + 1) * modes)
        pre, suf, _ = doubling(heat_ref[:, span] * speed, False)
        start = (gains * jnp.exp2(-pre)).astype(BF16)
        back = jnp.exp2(-suf).astype(BF16)
        decay = jnp.exp2(-(pre + suf))
        fresh_f = jnp.dot(back, cur_ref[span, :], preferred_element_type=F32)
        fresh_a = jnp.dot(start, cot_ref[span, :], preferred_element_type=F32)
        fresh_f_ref[rows, :] = fresh_f
        fresh_a_ref[rows, :] = fresh_a
        decay_ref[rows, :] = decay
        tf[...] = wide(decay, reps) * tf[...] + fresh_f
        ta[...] = ta[...] + wide(dc[...], reps) * fresh_a
        dc[...] = dc[...] * decay

    @pl.when(step == pl.num_programs(0) - 1)
    def _():
        for k in range(reps):
            lanes = slice(k * CHUNK, (k + 1) * CHUNK)
            msg_ref[k] = tf[:, lanes]
            msg_ref[reps + k] = ta[:, lanes]
        msg_ref[2 * reps] = dc[...]


def kernels_kernel(heat_ref, rates_ref, fit_ref, kf_ref, ka_ref, aux_ref):
    modes = heat_ref.shape[0]
    speed, gains = rates_and_gains(rates_ref, fit_ref)
    gain_sum = jnp.sum(gains, axis=0, keepdims=True)
    t = lax.broadcasted_iota(jnp.int32, (CHUNK, CHUNK), 0)
    s = lax.broadcasted_iota(jnp.int32, (CHUNK, CHUNK), 1)
    apart = jnp.where(t >= s, t ^ s, -1)
    base = jnp.where(apart == 0, jnp.broadcast_to(gain_sum, (CHUNK, CHUNK)), 0.0)
    zero = jnp.zeros((modes, CHUNK), BF16)
    for c in range(heat_ref.shape[1] // CHUNK):
        span = slice(c * CHUNK, (c + 1) * CHUNK)
        pre, suf, tables = doubling(heat_ref[:, span] * speed, True)
        left = [gains * e for e in tables]
        right = [e.astype(BF16) for e in tables]
        kernel = base
        for lv in range(0, LEVELS - 1, 2):
            lhs = jnp.concatenate([left[lv], left[lv + 1]], axis=0).T.astype(BF16)
            rhs = jnp.concatenate(
                [
                    jnp.concatenate([right[lv], zero], axis=1),
                    jnp.concatenate([zero, right[lv + 1]], axis=1),
                ],
                axis=0,
            )
            both = jnp.dot(lhs, rhs, preferred_element_type=F32)
            kernel = jnp.where(apart >= (1 << lv), both[:, :CHUNK], kernel)
            kernel = jnp.where(apart >= (2 << lv), both[:, CHUNK:], kernel)
        back = jnp.exp2(-suf)
        aux = jnp.concatenate(
            [left[LEVELS - 1], gains * jnp.exp2(-pre), back, back], axis=0
        ).T.astype(BF16)
        rhs = jnp.concatenate([right[LEVELS - 1], zero, zero, zero], axis=0)
        last = jnp.dot(aux, rhs, preferred_element_type=F32)
        kernel = jnp.where(apart >= (1 << (LEVELS - 1)), last, kernel)
        kf_ref[span, :] = kernel.astype(BF16)
        ka_ref[span, :] = kernel.T.astype(BF16)
        aux_ref[span, :] = aux


def stress_kernel(
    cur_ref, kf_ref, aux_ref, fresh_ref, decay_ref, in_ref, counts_ref,
    out_ref, lse_ref, state, high, amount,
):
    step = pl.program_id(0)
    wires = cur_ref.shape[1]
    reps = wires // CHUNK
    modes = in_ref.shape[1]

    @pl.when(step == 0)
    def _():
        for k in range(reps):
            state[:, k * CHUNK : (k + 1) * CHUNK] = in_ref[k]
        high[...] = jnp.full_like(high, -1e30)
        amount[...] = jnp.zeros_like(amount)

    scale = counts_ref[...].astype(F32) * 0.25
    scale2 = scale * (SHARPNESS * LOG2E)
    zero1 = jnp.zeros((modes, wires), BF16)
    zero2 = jnp.zeros((CHUNK - 2 * modes, wires), BF16)
    for c in range(cur_ref.shape[0] // CHUNK):
        span = slice(c * CHUNK, (c + 1) * CHUNK)
        rows = slice(c * modes, (c + 1) * modes)
        now = state[...]
        lhs = jnp.concatenate([kf_ref[span, :], aux_ref[span, :]], axis=1)
        rhs = jnp.concatenate([cur_ref[span, :], zero1, now.astype(BF16), zero2], axis=0)
        acc = jnp.dot(lhs, rhs, preferred_element_type=F32)
        out_ref[span, :] = (acc * scale).astype(BF16)
        z = (acc * scale2).reshape(CHUNK // 8, 8, wires)
        old = high[...]
        new = jnp.maximum(old, jnp.max(z, axis=0))
        amount[...] = amount[...] * jnp.exp2(old - new) + jnp.sum(jnp.exp2(z - new[None]), axis=0)
        high[...] = new
        state[...] = wide(decay_ref[rows, :], reps) * now + fresh_ref[rows, :]

    @pl.when(step == pl.num_programs(0) - 1)
    def _():
        top = jnp.max(high[...], axis=0, keepdims=True)
        total = jnp.sum(amount[...] * jnp.exp2(high[...] - top), axis=0, keepdims=True)
        value = top + jnp.log(total) * LOG2E
        lse_ref[...] = jnp.broadcast_to(value[None], lse_ref.shape)


def adjoint_kernel(
    cot_ref, ka_ref, aux_ref, fresh_ref, decay_ref, in_ref, counts_ref, out_ref, state
):
    step = pl.program_id(0)
    wires = cot_ref.shape[1]
    reps = wires // CHUNK
    modes = in_ref.shape[1]

    @pl.when(step == 0)
    def _():
        for k in range(reps):
            state[:, k * CHUNK : (k + 1) * CHUNK] = in_ref[k]

    scale = counts_ref[...].astype(F32) * 0.25
    zero2 = jnp.zeros((2 * modes, wires), BF16)
    zero1 = jnp.zeros((CHUNK - 3 * modes, wires), BF16)
    for c in reversed(range(cot_ref.shape[0] // CHUNK)):
        span = slice(c * CHUNK, (c + 1) * CHUNK)
        rows = slice(c * modes, (c + 1) * modes)
        now = state[...]
        lhs = jnp.concatenate([ka_ref[span, :], aux_ref[span, :]], axis=1)
        rhs = jnp.concatenate([cot_ref[span, :], zero2, now.astype(BF16), zero1], axis=0)
        acc = jnp.dot(lhs, rhs, preferred_element_type=F32)
        out_ref[span, :] = (acc * scale).astype(BF16)
        state[...] = wide(decay_ref[rows, :], reps) * now + fresh_ref[rows, :]


def steps_for(chunks):
    for steps in (4, 3, 2):
        if chunks % steps == 0:
            return steps
    return 1


def scan_devices(msg, reps):
    n = lax.axis_size("tm")
    me = lax.axis_index("tm")
    before = jnp.zeros_like(msg[:reps])
    after = jnp.zeros_like(msg[:reps])
    d_before = jnp.ones_like(msg[2 * reps :])
    d_after = jnp.ones_like(msg[2 * reps :])
    hop = 1
    while hop < n:
        pairs = [(i, i ^ hop) for i in range(n)]
        upper = (me & hop) != 0
        mine_f, mine_a, mine_d = msg[:reps], msg[reps : 2 * reps], msg[2 * reps :]
        if 2 * hop < n:
            got = lax.ppermute(msg, "tm", pairs)
            got_f, got_a, got_d = got[:reps], got[reps : 2 * reps], got[2 * reps :]
            next_f = jnp.where(upper, mine_d * got_f + mine_f, got_d * mine_f + got_f)
            next_a = jnp.where(upper, got_d * mine_a + got_a, mine_d * got_a + mine_a)
            msg = jnp.concatenate([next_f, next_a, mine_d * got_d], axis=0)
            before = jnp.where(upper, d_before * got_f + before, before)
            after = jnp.where(upper, after, d_after * got_a + after)
            d_before = jnp.where(upper, d_before * got_d, d_before)
            d_after = jnp.where(upper, d_after, d_after * got_d)
        else:
            got = lax.ppermute(jnp.where(upper, mine_a, mine_f), "tm", pairs)
            before = jnp.where(upper, d_before * got + before, before)
            after = jnp.where(upper, after, d_after * got + after)
        hop *= 2
    return before, after


def body(currents, seed_on_tension, mode_diffusivity_factor, decay_rates, fit_weights, counts):
    samples, wires = currents.shape
    modes = decay_rates.shape[0]
    devices = lax.axis_size("tm")
    chunks = samples // CHUNK
    steps = steps_for(chunks)
    block = samples // steps
    mblock = chunks * modes // steps
    reps = wires // CHUNK
    rates = decay_rates.reshape(1, modes)
    fits = fit_weights.reshape(1, modes)
    counts = counts.reshape(1, wires)
    params = pltpu.CompilerParams(vmem_limit_bytes=48 << 20)
    small = pl.BlockSpec((1, modes), lambda i: (0, 0))
    flops = 2 * samples * wires

    fresh_f, fresh_a, decay, msg = pl.pallas_call(
        totals_kernel,
        name="totals",
        grid=(steps,),
        in_specs=[
            pl.BlockSpec((modes, block), lambda i: (0, i)),
            small,
            small,
            pl.BlockSpec((block, wires), lambda i: (i, 0)),
            pl.BlockSpec((block, wires), lambda i: (i, 0)),
        ],
        out_specs=[
            pl.BlockSpec((mblock, wires), lambda i: (i, 0)),
            pl.BlockSpec((mblock, wires), lambda i: (i, 0)),
            pl.BlockSpec((mblock, CHUNK), lambda i: (i, 0)),
            pl.BlockSpec((2 * reps + 1, modes, CHUNK), lambda i: (0, 0, 0)),
        ],
        out_shape=[
            jax.ShapeDtypeStruct((chunks * modes, wires), F32),
            jax.ShapeDtypeStruct((chunks * modes, wires), F32),
            jax.ShapeDtypeStruct((chunks * modes, CHUNK), F32),
            jax.ShapeDtypeStruct((2 * reps + 1, modes, CHUNK), F32),
        ],
        scratch_shapes=[
            pltpu.VMEM((modes, wires), F32),
            pltpu.VMEM((modes, wires), F32),
            pltpu.VMEM((modes, CHUNK), F32),
        ],
        compiler_params=params,
        cost_estimate=pl.CostEstimate(
            flops=2 * modes * flops, bytes_accessed=14 << 20, transcendentals=0
        ),
    )(mode_diffusivity_factor, rates, fits, currents, seed_on_tension)

    kf, ka, aux = pl.pallas_call(
        kernels_kernel,
        name="kernels",
        grid=(steps,),
        in_specs=[pl.BlockSpec((modes, block), lambda i: (0, i)), small, small],
        out_specs=[pl.BlockSpec((block, CHUNK), lambda i: (i, 0))] * 3,
        out_shape=[jax.ShapeDtypeStruct((samples, CHUNK), BF16)] * 3,
        compiler_params=params,
        cost_estimate=pl.CostEstimate(
            flops=CHUNK * flops, bytes_accessed=16 << 20, transcendentals=0
        ),
    )(mode_diffusivity_factor, rates, fits)

    before, after = scan_devices(msg, reps)

    def common(reverse):
        def at(i):
            return (steps - 1 - i if reverse else i, 0)

        return [
            pl.BlockSpec((block, wires), at),
            pl.BlockSpec((block, CHUNK), at),
            pl.BlockSpec((block, CHUNK), at),
            pl.BlockSpec((mblock, wires), at),
            pl.BlockSpec((mblock, CHUNK), at),
            pl.BlockSpec((reps, modes, CHUNK), lambda i: (0, 0, 0)),
            pl.BlockSpec((1, wires), lambda i: (0, 0)),
        ], pl.BlockSpec((block, wires), at)

    specs, out_spec = common(False)
    tension, lse = pl.pallas_call(
        stress_kernel,
        name="stress",
        grid=(steps,),
        in_specs=specs,
        out_specs=[out_spec, pl.BlockSpec((devices, 1, wires), lambda i: (0, 0, 0))],
        out_shape=[
            jax.ShapeDtypeStruct((samples, wires), BF16),
            jax.ShapeDtypeStruct((devices, 1, wires), F32),
        ],
        scratch_shapes=[
            pltpu.VMEM((modes, wires), F32),
            pltpu.VMEM((8, wires), F32),
            pltpu.VMEM((8, wires), F32),
        ],
        compiler_params=params,
        cost_estimate=pl.CostEstimate(
            flops=2 * CHUNK * flops, bytes_accessed=10 << 20, transcendentals=0
        ),
    )(currents, kf, aux, fresh_f, decay, before, counts)

    all_lse = lax.all_to_all(lse, "tm", 0, 0, tiled=True)

    specs, out_spec = common(True)
    gradient = pl.pallas_call(
        adjoint_kernel,
        name="adjoint",
        grid=(steps,),
        in_specs=specs,
        out_specs=out_spec,
        out_shape=jax.ShapeDtypeStruct((samples, wires), BF16),
        scratch_shapes=[pltpu.VMEM((modes, wires), F32)],
        compiler_params=params,
        cost_estimate=pl.CostEstimate(
            flops=2 * CHUNK * flops, bytes_accessed=10 << 20, transcendentals=0
        ),
    )(seed_on_tension, ka, aux, fresh_a, decay, after, counts)

    top = jnp.max(all_lse, axis=0)
    total = jnp.sum(jnp.exp2(all_lse - top[None]), axis=0)
    softened = ((top * LN2 + jnp.log(total)) / SHARPNESS).reshape(wires)
    return (tension, gradient, softened)


def solution(mesh):
    placed = (P("tm", "parts"), P("tm", "parts"), P(None, ("parts", "tm")), P(), P(), P("parts"))
    return jax.shard_map(
        body,
        mesh=mesh,
        in_specs=placed,
        out_specs=(P("tm", "parts"), P("tm", "parts"), P("parts")),
        check_vma=False,
    )
```

time: 305 us -> 56 us (0.18)
  other arithmetic: 152 us -> 2.54 us
  blocking collectives: 82.4 us -> 0 us
  matrix products: 46.8 us -> 0 us
  Pallas kernels: 0 us -> 23.7 us
  between operations: 14.4 us -> 0.76 us
  starting transfers between devices: 0.08 us -> 11.7 us
  waiting for transfers between devices: 0.71 us -> 8.76 us
    reduce_sum x3 -> x1, other arithmetic: 98.2 us -> 0.08 us  [body(): total = jnp.sum(jnp.exp2(all_lse - top[None]), axis=0)]
    dot_general x12 -> x0, matrix products: 46.8 us -> none  [the longest x4 15.5 us: body(): jnp.dot(back_table[position], adjoint_state, precision=lax.Precision.HIGH...]
    pmax x1 -> x0, blocking collectives: 29.8 us -> none  [body(): highest = lax.pmax(local_high, 'tm')]
    psum x1 -> x0, blocking collectives: 29.5 us -> none  [body(): amount = lax.psum(jnp.sum(jnp.exp(scores - highest), axis=(0, 1)), 'tm')]
    pallas_call x0 -> x4, Pallas kernels: none -> 23.7 us  [the longest x1 7.22 us: body(): pl.pallas_call(kernels_kernel, name='kernels', grid=(steps,), in_specs=[p...]
    all_gather x1 -> x0, blocking collectives: 23.1 us -> none  [entering(): gathered = jax.tree.map(lambda a: lax.all_gather(a, axis), part)]
    convert_element_type x3 -> x0, other arithmetic: 18.2 us -> none  [the longest x2 16.1 us: body(): kernel_list.append(block_kernel.astype(jnp.bfloat16))]
    add x18 -> x0, other arithmetic: 15.6 us -> none  [the longest x15 13.8 us: combine_states(): return (earlier[0] * latter[0], latter[0][:, None] * earlier[1] + latter[1])]
  transfers between devices with their start and end apart: 2 -> 5, of which waited for: 0 -> 3; matrix products, arithmetic and copies ran while one was open for 47% -> 0% of each run, Pallas kernels for 0% -> 22%
where the time goes in v1:
time: 56 us; the launch traced here: 55.4 us
  Pallas kernels  23.7 us (42%)
  starting transfers between devices  11.7 us (21%)
  waiting for transfers between devices  8.76 us (16%)
  local copies, waits for them, and re-layouts  7.88 us (14%)
  other arithmetic  2.54 us (5%)
  between operations  0.76 us (1%)
    ppermute x3, waiting for transfers between devices, scan_devices(): got = lax.ppermute(msg, 'tm', pairs)  8.75 us
    unnamed x28, local copies, waits for them, and re-layouts  7.88 us
    pallas_call x1, Pallas kernels, body(): pl.pallas_call(kernels_kernel, name='kernels', grid=(steps,), in_specs=[p...  7.22 us
    pallas_call x1, Pallas kernels, body(): pl.pallas_call(totals_kernel, name='totals', grid=(steps,), in_specs=[pl....  6.19 us
    pallas_call x1, Pallas kernels, body(): pl.pallas_call(stress_kernel, name='stress', grid=(steps,), in_specs=spec...  5.43 us
    ppermute x3, starting transfers between devices, scan_devices(): got = lax.ppermute(msg, 'tm', pairs)  5.26 us
    pallas_call x1, Pallas kernels, body(): pl.pallas_call(adjoint_kernel, name='adjoint', grid=(steps,), in_specs=sp...  4.9 us
    all_to_all x1, starting transfers between devices, body(): all_lse = lax.all_to_all(lse, 'tm', 0, 0, tiled=True)  3.91 us
  transfers between devices with their start and end apart: 5, of which 3 were waited for; matrix products, arithmetic and copies ran while one was open for 0% of the time, Pallas kernels for 22%

profile of v1, /device:TPU:0, one launch (start us, length us, event | category | flops | bytes accessed | tf_op | source)
XLA Modules:
  0.0 55.4 jit_solution(3211930394866722985)
XLA Ops:
  0.6 0.0 copy-start.2
  0.6 1.0 %copy-done.2 = f32[32,3072]{1,0:T(8,128)S(1)} copy-done((f32[32,3072]{1,0:T(8,128)S(1)}, f32[32,3072]{1,0:T(8,128)}, u32[]{:S(2)}) %copy-start.2) | copy-done | bytes 393240
  1.6 0.0 copy-start.7
  1.6 0.7 %copy-done.7 = f32[32]{0:T(128)S(1)} copy-done((f32[32]{0:T(128)S(1)}, f32[32]{0:T(128)}, u32[]{:S(2)}) %copy-start.7) | copy-done | bytes 152
  2.3 0.0 copy-start.9
  2.3 0.7 %copy-done.9 = f32[32]{0:T(128)S(1)} copy-done((f32[32]{0:T(128)S(1)}, f32[32]{0:T(128)}, u32[]{:S(2)}) %copy-start.9) | copy-done | bytes 152
  2.9 0.0 copy-start.8
  2.9 0.0 copy-start.10
  2.9 6.2 %totals.1 = (f32[768,512]{1,0:T(8,128)S(1)}, f32[768,512]{1,0:T(8,128)S(1)}, f32[768,128]{1,0:T(8,128)S(1)}, f32[9,32,128]{2,1,0:T(8,128)S(1)}) custom-call(f32[32,3072]{1,0:T(8,128)S(1)} %copy-done.2, f32[1,32]{1,0:T(1,128)S(1)} %bitcast.27, f32[1,32]{1,0:T(1,128)S(1)} %bitcast.29, bf16[3072,512]{1,0:T(8,128)(2,1)} %cur_ref.3, bf16[3072,512]{1,0:T(8,128)(2,1)} %cot_ref.3), custom_call_target="tpu_custom_call" | custom-call | flops 201326592 | bytes 14680064 | tf_op jit(solution)/shard_map/totals/pallas_call | solution.py:258
  9.1 0.0 copy-start
  9.2 1.1 %copy-done = f32[768,512]{1,0:T(8,128)} copy-done((f32[768,512]{1,0:T(8,128)}, f32[768,512]{1,0:T(8,128)S(1)}, u32[]{:S(2)}) %copy-start) | copy-done | bytes 1572888
  10.3 0.0 copy-start.6
  10.3 0.5 collective-permute-start
  10.7 1.0 %collective-permute-done = f32[9,32,128]{2,1,0:T(8,128)S(1)} collective-permute-done((f32[9,32,128]{2,1,0:T(8,128)S(1)}, f32[9,32,128]{2,1,0:T(8,128)S(1)}, u32[]{:S(2)}, u32[]{:S(2)}) %collective-permute-start) | collective-permute-done | bytes 147488 | tf_op jit(solution)/shard_map/ppermute | solution.py:225
  11.8 0.0 copy-start.11
  11.8 2.9 %collective-permute-start.1 = (f32[9,32,128]{2,1,0:T(8,128)S(1)}, f32[9,32,128]{2,1,0:T(8,128)S(1)}, u32[]{:S(2)}, u32[]{:S(2)}) collective-permute-start(f32[9,32,128]{2,1,0:T(8,128)S(1)} %pad_maximum_fusion), channel_id=1, source_target_pairs={{0,2},{1,3},{2,0},{3,1},{4,6},{5,7},{6,4},{7,5},{8,10},{9,11},{10,... | collective-permute-start | bytes 442376 | tf_op jit(solution)/shard_map/ppermute | solution.py:225
  14.8 4.2 %collective-permute-done.1 = f32[9,32,128]{2,1,0:T(8,128)S(1)} collective-permute-done((f32[9,32,128]{2,1,0:T(8,128)S(1)}, f32[9,32,128]{2,1,0:T(8,128)S(1)}, u32[]{:S(2)}, u32[]{:S(2)}) %collective-permute-start.1) | collective-permute-done | bytes 147488 | tf_op jit(solution)/shard_map/ppermute | solution.py:225
  18.9 0.0 copy-start.12
  19.0 1.9 %collective-permute-start.2 = (f32[9,32,128]{2,1,0:T(8,128)S(1)}, f32[9,32,128]{2,1,0:T(8,128)S(1)}, u32[]{:S(2)}, u32[]{:S(2)}) collective-permute-start(f32[9,32,128]{2,1,0:T(8,128)S(1)} %pad_maximum_fusion.1), channel_id=1, source_target_pairs={{0,4},{1,5},{2,6},{3,7},{4,0},{5,1},{6,2},{7,3},{8,12},{9,13},{10,... | collective-permute-start | bytes 442376 | tf_op jit(solution)/shard_map/ppermute | solution.py:225
  20.8 3.6 %collective-permute-done.2 = f32[9,32,128]{2,1,0:T(8,128)S(1)} collective-permute-done((f32[9,32,128]{2,1,0:T(8,128)S(1)}, f32[9,32,128]{2,1,0:T(8,128)S(1)}, u32[]{:S(2)}, u32[]{:S(2)}) %collective-permute-start.2) | collective-permute-done | bytes 147488 | tf_op jit(solution)/shard_map/ppermute | solution.py:225
  24.4 0.0 copy-start.13
  24.5 0.0 copy-done.11
  24.5 0.0 copy-done.12
  24.5 0.6 %copy-done.13 = f32[9,32,128]{2,1,0:T(8,128)} copy-done((f32[9,32,128]{2,1,0:T(8,128)}, f32[9,32,128]{2,1,0:T(8,128)S(1)}, u32[]{:S(2)}) %copy-start.13) | copy-done | bytes 147480
  25.1 2.6 %collective-permute-start.3 = (f32[4,32,128]{2,1,0:T(8,128)S(1)}, f32[4,32,128]{2,1,0:T(8,128)S(1)}, u32[]{:S(2)}, u32[]{:S(2)}) collective-permute-start(f32[4,32,128]{2,1,0:T(8,128)S(1)} %select_select_fusion), channel_id=1, source_target_pairs={{0,8},{1,9},{2,10},{3,11},{4,12},{5,13},{6,14},{7,15},{8,0},{9,1},... | collective-permute-start | bytes 196616 | tf_op jit(solution)/shard_map/ppermute | solution.py:235
  27.7 0.0 copy-done.8
  27.7 0.0 copy-done.10
  27.7 0.0 copy-start.3
  27.7 1.0 %copy-done.3 = f32[32,3072]{1,0:T(8,128)S(1)} copy-done((f32[32,3072]{1,0:T(8,128)S(1)}, f32[32,3072]{1,0:T(8,128)}, u32[]{:S(2)}) %copy-start.3) | copy-done | bytes 393240
  28.7 7.2 %kernels.1 = (bf16[3072,128]{1,0:T(8,128)(2,1)S(1)}, bf16[3072,128]{1,0:T(8,128)(2,1)S(1)}, bf16[3072,128]{1,0:T(8,128)(2,1)S(1)}) custom-call(f32[32,3072]{1,0:T(8,128)S(1)} %copy-done.3, f32[1,32]{1,0:T(1,128)S(1)} %bitcast.28, f32[1,32]{1,0:T(1,128)S(1)} %bitcast.30), custom_call_target="tpu_custom_call" | custom-call | flops 402653184 | bytes 16777216 | tf_op jit(solution)/shard_map/kernels/pallas_call | solution.py:292
  35.9 0.0 collective-permute-done.3
  35.9 1.7 %add_select_fusion = (f32[4,32,128]{2,1,0:T(8,128)}, f32[4,32,128]{2,1,0:T(8,128)S(1)}) fusion(f32[4,32,128]{2,1,0:T(8,128)S(1)} %collective-permute-done.3, f32[9,32,128]{2,1,0:T(8,128)} %copy-done.13, f32[9,32,128]{2,1,0:T(8,128)} %copy-done.12, f32[9,32,128]{2,1,0:T(8,128)} %copy-done.11, f32[32,128]{1,0:T(8,128)S(1)} %get-tuple-element.23, ...), kind=kLoop, calls=%fused_computation.2 | loop fusion | flops 327680 | bytes 688132 | tf_op jit(solution)/shard_map/jit(_where)/select_n | solution.py:237
  37.6 0.0 copy-done.6
  37.6 5.4 %stress.1 = (bf16[3072,512]{1,0:T(8,128)(2,1)}, f32[16,1,512]{2,1,0:T(1,128)S(1)}) custom-call(bf16[3072,512]{1,0:T(8,128)(2,1)} %cur_ref.3, bf16[3072,128]{1,0:T(8,128)(2,1)S(1)} %get-tuple-element.12.kf_ref, bf16[3072,128]{1,0:T(8,128)(2,1)S(1)} %get-tuple-element.13.aux_ref, f32[768,512]{1,0:T(8,128)S(1)} %get-tuple-element.14.fresh_ref, ...), custom_call_target="tpu_custom_call" | custom-call | flops 805306368 | bytes 10485760 | tf_op jit(solution)/shard_map/stress/pallas_call | solution.py:322
  43.0 0.0 copy-start.5
  43.0 0.6 %copy-done.5 = f32[16,1,512]{2,1,0:T(1,128)} copy-done((f32[16,1,512]{2,1,0:T(1,128)}, f32[16,1,512]{2,1,0:T(1,128)S(1)}, u32[]{:S(2)}) %copy-start.5) | copy-done | bytes 32792
  43.6 3.9 %all-to-all-start = ((f32[16,1,512]{2,1,0:T(1,128)}), f32[16,1,512]{2,1,0:T(1,128)S(1)}, u32[]{:S(2)}, u32[]{:S(2)}) async-start(f32[16,1,512]{2,1,0:T(1,128)} %copy-done.5), calls=%async_computation | async-start | bytes 65536 | tf_op jit(solution)/shard_map/all_to_all | solution.py:343
  47.6 0.0 copy-start.1
  47.6 1.4 %copy-done.1 = f32[768,512]{1,0:T(8,128)S(1)} copy-done((f32[768,512]{1,0:T(8,128)S(1)}, f32[768,512]{1,0:T(8,128)}, u32[]{:S(2)}) %copy-start.1) | copy-done | bytes 1572888
  49.0 0.0 copy-start.4
  49.0 0.8 %copy-done.4 = f32[4,32,128]{2,1,0:T(8,128)S(1)} copy-done((f32[4,32,128]{2,1,0:T(8,128)S(1)}, f32[4,32,128]{2,1,0:T(8,128)}, u32[]{:S(2)}) %copy-start.4) | copy-done | bytes 65560
  49.8 4.9 %adjoint.1 = bf16[3072,512]{1,0:T(8,128)(2,1)} custom-call(bf16[3072,512]{1,0:T(8,128)(2,1)} %cot_ref.3, bf16[3072,128]{1,0:T(8,128)(2,1)S(1)} %get-tuple-element.18.ka_ref, bf16[3072,128]{1,0:T(8,128)(2,1)S(1)} %get-tuple-element.13.aux_ref, f32[768,512]{1,0:T(8,128)S(1)} %copy-done.1, f32[768,128]{1,0:T(8,128)S(1)} %get-tuple-element.15.decay_ref, ...), custom_call_target="tpu_custom_call" | custom-call | flops 805306368 | bytes 10485760 | tf_op jit(solution)/shard_map/adjoint/pallas_call | solution.py:346
  54.7 0.0 all-to-all-done
  54.8 0.1 exponential_reduce_fusion
  54.8 0.6 %add_multiply_fusion = f32[512]{0:T(512)} fusion(f32[512]{0:T(512)S(1)} %exponential_reduce_fusion, f32[512]{0:T(512)S(1)} %reduce_max.9), kind=kLoop, calls=%fused_computation.30 | loop fusion | flops 1536 | bytes 6144 | tf_op jit(solution)/shard_map/div | solution.py:362
  (9 shorter events, 0.2 us)
Async XLA Ops:
  0.6 1.0 %copy-start.2 = (f32[32,3072]{1,0:T(8,128)S(1)}, f32[32,3072]{1,0:T(8,128)}, u32[]{:S(2)}) copy-start(f32[32,3072]{1,0:T(8,128)} %heat_ref.3) | copy-start | bytes 1179652
  1.6 0.7 %copy-start.7 = (f32[32]{0:T(128)S(1)}, f32[32]{0:T(128)}, u32[]{:S(2)}) copy-start(f32[32]{0:T(128)} %param.9) | copy-start | bytes 388
  2.3 0.7 %copy-start.9 = (f32[32]{0:T(128)S(1)}, f32[32]{0:T(128)}, u32[]{:S(2)}) copy-start(f32[32]{0:T(128)} %param.10) | copy-start | bytes 388
  2.9 24.7 %copy-start.8 = (f32[32]{0:T(128)S(1)}, f32[32]{0:T(128)}, u32[]{:S(2)}) copy-start(f32[32]{0:T(128)} %param.9) | copy-start | bytes 388
  2.9 24.7 %copy-start.10 = (f32[32]{0:T(128)S(1)}, f32[32]{0:T(128)}, u32[]{:S(2)}) copy-start(f32[32]{0:T(128)} %param.10) | copy-start | bytes 388
  9.1 1.1 %copy-start = (f32[768,512]{1,0:T(8,128)}, f32[768,512]{1,0:T(8,128)S(1)}, u32[]{:S(2)}) copy-start(f32[768,512]{1,0:T(8,128)S(1)} %get-tuple-element.19.fresh_ref) | copy-start | bytes 4718596
  10.3 27.3 %copy-start.6 = (s32[512]{0:T(512)S(1)}, s32[512]{0:T(512)}, u32[]{:S(2)}) copy-start(s32[512]{0:T(512)} %param.11) | copy-start | bytes 6148
  10.3 1.5 %collective-permute-start = (f32[9,32,128]{2,1,0:T(8,128)S(1)}, f32[9,32,128]{2,1,0:T(8,128)S(1)}, u32[]{:S(2)}, u32[]{:S(2)}) collective-permute-start(f32[9,32,128]{2,1,0:T(8,128)S(1)} %get-tuple-element.16), channel_id=1, source_target_pairs={{0,1},{1,0},{2,3},{3,2},{4,5},{5,4},{6,7},{7,6},{8,9},{9,8},{10,11... | collective-permute-start | bytes 442376 | tf_op jit(solution)/shard_map/ppermute | solution.py:225
  11.8 12.7 %copy-start.11 = (f32[9,32,128]{2,1,0:T(8,128)}, f32[9,32,128]{2,1,0:T(8,128)S(1)}, u32[]{:S(2)}) copy-start(f32[9,32,128]{2,1,0:T(8,128)S(1)} %collective-permute-done) | copy-start | bytes 442372
  11.8 7.1 %collective-permute-start.1 = (f32[9,32,128]{2,1,0:T(8,128)S(1)}, f32[9,32,128]{2,1,0:T(8,128)S(1)}, u32[]{:S(2)}, u32[]{:S(2)}) collective-permute-start(f32[9,32,128]{2,1,0:T(8,128)S(1)} %pad_maximum_fusion), channel_id=1, source_target_pairs={{0,2},{1,3},{2,0},{3,1},{4,6},{5,7},{6,4},{7,5},{8,10},{9,11},{10,... | collective-permute-start | bytes 442376 | tf_op jit(solution)/shard_map/ppermute | solution.py:225
  18.9 5.6 %copy-start.12 = (f32[9,32,128]{2,1,0:T(8,128)}, f32[9,32,128]{2,1,0:T(8,128)S(1)}, u32[]{:S(2)}) copy-start(f32[9,32,128]{2,1,0:T(8,128)S(1)} %collective-permute-done.1) | copy-start | bytes 442372
  19.0 5.5 %collective-permute-start.2 = (f32[9,32,128]{2,1,0:T(8,128)S(1)}, f32[9,32,128]{2,1,0:T(8,128)S(1)}, u32[]{:S(2)}, u32[]{:S(2)}) collective-permute-start(f32[9,32,128]{2,1,0:T(8,128)S(1)} %pad_maximum_fusion.1), channel_id=1, source_target_pairs={{0,4},{1,5},{2,6},{3,7},{4,0},{5,1},{6,2},{7,3},{8,12},{9,13},{10,... | collective-permute-start | bytes 442376 | tf_op jit(solution)/shard_map/ppermute | solution.py:225
  24.4 0.7 %copy-start.13 = (f32[9,32,128]{2,1,0:T(8,128)}, f32[9,32,128]{2,1,0:T(8,128)S(1)}, u32[]{:S(2)}) copy-start(f32[9,32,128]{2,1,0:T(8,128)S(1)} %collective-permute-done.2) | copy-start | bytes 442372
  25.1 10.8 %collective-permute-start.3 = (f32[4,32,128]{2,1,0:T(8,128)S(1)}, f32[4,32,128]{2,1,0:T(8,128)S(1)}, u32[]{:S(2)}, u32[]{:S(2)}) collective-permute-start(f32[4,32,128]{2,1,0:T(8,128)S(1)} %select_select_fusion), channel_id=1, source_target_pairs={{0,8},{1,9},{2,10},{3,11},{4,12},{5,13},{6,14},{7,15},{8,0},{9,1},... | collective-permute-start | bytes 196616 | tf_op jit(solution)/shard_map/ppermute | solution.py:235
  27.7 1.0 %copy-start.3 = (f32[32,3072]{1,0:T(8,128)S(1)}, f32[32,3072]{1,0:T(8,128)}, u32[]{:S(2)}) copy-start(f32[32,3072]{1,0:T(8,128)} %heat_ref.3) | copy-start | bytes 1179652
  43.0 0.6 %copy-start.5 = (f32[16,1,512]{2,1,0:T(1,128)}, f32[16,1,512]{2,1,0:T(1,128)S(1)}, u32[]{:S(2)}) copy-start(f32[16,1,512]{2,1,0:T(1,128)S(1)} %get-tuple-element.20) | copy-start | bytes 98308
  43.6 11.1 %all-to-all-start = ((f32[16,1,512]{2,1,0:T(1,128)}), f32[16,1,512]{2,1,0:T(1,128)S(1)}, u32[]{:S(2)}, u32[]{:S(2)}) async-start(f32[16,1,512]{2,1,0:T(1,128)} %copy-done.5), calls=%async_computation | async-start | bytes 65536 | tf_op jit(solution)/shard_map/all_to_all | solution.py:343
  47.6 1.4 %copy-start.1 = (f32[768,512]{1,0:T(8,128)S(1)}, f32[768,512]{1,0:T(8,128)}, u32[]{:S(2)}) copy-start(f32[768,512]{1,0:T(8,128)} %copy-done) | copy-start | bytes 4718596
  49.0 0.8 %copy-start.4 = (f32[4,32,128]{2,1,0:T(8,128)S(1)}, f32[4,32,128]{2,1,0:T(8,128)}, u32[]{:S(2)}) copy-start(f32[4,32,128]{2,1,0:T(8,128)} %get-tuple-element.21.in_ref) | copy-start | bytes 196612

commit v2 on v1

v2 whole, which is shorter than its diff:
```python
import functools
import math

import jax
import jax.numpy as jnp
from jax import lax
from jax.experimental import pallas as pl
from jax.experimental.pallas import tpu as pltpu
from jax.sharding import PartitionSpec as P

CHUNK = 128
LEVELS = 7
SHARPNESS = 4.0
LOG2E = math.log2(math.e)
LN2 = math.log(2.0)
F32 = jnp.float32
BF16 = jnp.bfloat16


def as_column(row):
    m = row.shape[1]
    r = lax.broadcasted_iota(jnp.int32, (m, m), 0)
    c = lax.broadcasted_iota(jnp.int32, (m, m), 1)
    return jnp.sum(jnp.where(r == c, jnp.broadcast_to(row, (m, m)), 0.0), axis=1, keepdims=True)


def rates_and_gains(rates_ref, fit_ref):
    rates = as_column(rates_ref[...])
    gains = as_column(fit_ref[...]) * jnp.sqrt(rates)
    return rates * LOG2E, gains


def doubling(heat, with_levels):
    lane = lax.broadcasted_iota(jnp.int32, heat.shape, 1)
    pre, suf = heat, jnp.zeros_like(heat)
    tables = []
    for level in range(LEVELS):
        half = 1 << level
        second = (lane & half) != 0
        if with_levels:
            tables.append(jnp.exp2(-jnp.where(second, pre, suf)))
        total = pre + suf
        sibling = jnp.where(
            second, pltpu.roll(total, half, 1), pltpu.roll(total, CHUNK - half, 1)
        )
        pre = jnp.where(second, pre + sibling, pre)
        suf = jnp.where(second, suf, suf + sibling)
    return pre, suf, tables


def wide(a, times):
    return jnp.concatenate([a] * times, axis=1)


def stacked(heat_ref, speed, first, count):
    return jnp.concatenate(
        [
            heat_ref[:, c * CHUNK : (c + 1) * CHUNK] * speed
            for c in range(first, first + count)
        ],
        axis=0,
    )


def group_of(chunks, most):
    return max(g for g in range(1, most + 1) if chunks % g == 0)


def totals_kernel(
    heat_ref, rates_ref, fit_ref, cur_ref, cot_ref,
    fresh_f_ref, fresh_a_ref, decay_ref, msg_ref, tf_ref, ta_ref, dc_ref,
):
    step = pl.program_id(0)
    modes = heat_ref.shape[0]
    wires = cur_ref.shape[1]
    reps = wires // CHUNK
    chunks = heat_ref.shape[1] // CHUNK
    group = group_of(chunks, 3)

    @pl.when(step == 0)
    def _():
        tf_ref[...] = jnp.zeros_like(tf_ref)
        ta_ref[...] = jnp.zeros_like(ta_ref)
        dc_ref[...] = jnp.ones_like(dc_ref)

    speed, gains = rates_and_gains(rates_ref, fit_ref)
    gain_stack = jnp.concatenate([gains] * group, axis=0)
    tf, ta, dc = tf_ref[...], ta_ref[...], dc_ref[...]
    for first in range(0, chunks, group):
        pre, suf, _ = doubling(stacked(heat_ref, speed, first, group), False)
        starts = (gain_stack * jnp.exp2(-pre)).astype(BF16)
        backs = jnp.exp2(-suf).astype(BF16)
        decays = jnp.exp2(-(pre + suf))
        for c in range(group):
            part = slice(c * modes, (c + 1) * modes)
            span = slice((first + c) * CHUNK, (first + c + 1) * CHUNK)
            rows = slice((first + c) * modes, (first + c + 1) * modes)
            decay = decays[part]
            fresh_f = jnp.dot(backs[part], cur_ref[span, :], preferred_element_type=F32)
            fresh_a = jnp.dot(starts[part], cot_ref[span, :], preferred_element_type=F32)
            fresh_f_ref[rows, :] = fresh_f
            fresh_a_ref[rows, :] = fresh_a
            decay_ref[rows, :] = decay
            tf = wide(decay, reps) * tf + fresh_f
            ta = ta + wide(dc, reps) * fresh_a
            dc = dc * decay
    tf_ref[...], ta_ref[...], dc_ref[...] = tf, ta, dc

    @pl.when(step == pl.num_programs(0) - 1)
    def _():
        for k in range(reps):
            lanes = slice(k * CHUNK, (k + 1) * CHUNK)
            msg_ref[k] = tf[:, lanes]
            msg_ref[reps + k] = ta[:, lanes]
        msg_ref[2 * reps] = dc


def kernels_kernel(heat_ref, rates_ref, fit_ref, *refs):
    kf_ref, ka_ref, aux_ref = refs[-3:]
    modes = heat_ref.shape[0]
    chunks = heat_ref.shape[1] // CHUNK
    group = group_of(chunks, 2)
    speed, gains = rates_and_gains(rates_ref, fit_ref)
    gain_sum = jnp.sum(gains, axis=0, keepdims=True)
    t = lax.broadcasted_iota(jnp.int32, (CHUNK, CHUNK), 0)
    s = lax.broadcasted_iota(jnp.int32, (CHUNK, CHUNK), 1)
    apart = jnp.where(t >= s, t ^ s, -1)
    base = jnp.where(apart == 0, jnp.broadcast_to(gain_sum, (CHUNK, CHUNK)), 0.0)
    zero = jnp.zeros((modes, CHUNK), BF16)
    for first in range(0, chunks, group):
        pres, sufs, stacks = doubling(stacked(heat_ref, speed, first, group), True)
        for c in range(group):
            part = slice(c * modes, (c + 1) * modes)
            span = slice((first + c) * CHUNK, (first + c + 1) * CHUNK)
            pre, suf = pres[part], sufs[part]
            tables = [e[part] for e in stacks]
            left = [gains * e for e in tables]
            right = [e.astype(BF16) for e in tables]
            kernel = base
            for lv in range(0, LEVELS - 1, 2):
                lhs = jnp.concatenate([left[lv], left[lv + 1]], axis=0).T.astype(BF16)
                rhs = jnp.concatenate(
                    [
                        jnp.concatenate([right[lv], zero], axis=1),
                        jnp.concatenate([zero, right[lv + 1]], axis=1),
                    ],
                    axis=0,
                )
                both = jnp.dot(lhs, rhs, preferred_element_type=F32)
                kernel = jnp.where(apart >= (1 << lv), both[:, :CHUNK], kernel)
                kernel = jnp.where(apart >= (2 << lv), both[:, CHUNK:], kernel)
            back = jnp.exp2(-suf)
            aux = jnp.concatenate(
                [left[LEVELS - 1], gains * jnp.exp2(-pre), back, back], axis=0
            ).T.astype(BF16)
            rhs = jnp.concatenate([right[LEVELS - 1], zero, zero, zero], axis=0)
            last = jnp.dot(aux, rhs, preferred_element_type=F32)
            kernel = jnp.where(apart >= (1 << (LEVELS - 1)), last, kernel)
            kf_ref[span, :] = kernel.astype(BF16)
            ka_ref[span, :] = kernel.T.astype(BF16)
            aux_ref[span, :] = aux


def stress_kernel(
    cur_ref, kf_ref, aux_ref, fresh_ref, decay_ref, in_ref, counts_ref,
    out_ref, lse_ref, state_ref, high_ref, amount_ref,
):
    step = pl.program_id(0)
    wires = cur_ref.shape[1]
    reps = wires // CHUNK
    modes = in_ref.shape[1]

    @pl.when(step == 0)
    def _():
        for k in range(reps):
            state_ref[:, k * CHUNK : (k + 1) * CHUNK] = in_ref[k]
        high_ref[...] = jnp.full_like(high_ref, -1e30)
        amount_ref[...] = jnp.zeros_like(amount_ref)

    scale = counts_ref[...].astype(F32) * 0.25
    scale2 = scale * (SHARPNESS * LOG2E)
    zero1 = jnp.zeros((modes, wires), BF16)
    zero2 = jnp.zeros((CHUNK - 2 * modes, wires), BF16)
    state, high, amount = state_ref[...], high_ref[...], amount_ref[...]
    for c in range(cur_ref.shape[0] // CHUNK):
        span = slice(c * CHUNK, (c + 1) * CHUNK)
        rows = slice(c * modes, (c + 1) * modes)
        lhs = jnp.concatenate([kf_ref[span, :], aux_ref[span, :]], axis=1)
        rhs = jnp.concatenate([cur_ref[span, :], zero1, state.astype(BF16), zero2], axis=0)
        acc = jnp.dot(lhs, rhs, preferred_element_type=F32)
        out_ref[span, :] = (acc * scale).astype(BF16)
        z = (acc * scale2).reshape(CHUNK // 8, 8, wires)
        new = jnp.maximum(high, jnp.max(z, axis=0))
        amount = amount * jnp.exp2(high - new) + jnp.sum(jnp.exp2(z - new[None]), axis=0)
        high = new
        state = wide(decay_ref[rows, :], reps) * state + fresh_ref[rows, :]
    state_ref[...], high_ref[...], amount_ref[...] = state, high, amount

    @pl.when(step == pl.num_programs(0) - 1)
    def _():
        top = jnp.max(high, axis=0, keepdims=True)
        total = jnp.sum(amount * jnp.exp2(high - top), axis=0, keepdims=True)
        value = top + jnp.log(total) * LOG2E
        lse_ref[...] = jnp.broadcast_to(value[None], lse_ref.shape)


def adjoint_kernel(
    cot_ref, ka_ref, aux_ref, fresh_ref, decay_ref, in_ref, counts_ref, out_ref, state_ref
):
    step = pl.program_id(0)
    wires = cot_ref.shape[1]
    reps = wires // CHUNK
    modes = in_ref.shape[1]

    @pl.when(step == 0)
    def _():
        for k in range(reps):
            state_ref[:, k * CHUNK : (k + 1) * CHUNK] = in_ref[k]

    scale = counts_ref[...].astype(F32) * 0.25
    zero2 = jnp.zeros((2 * modes, wires), BF16)
    zero1 = jnp.zeros((CHUNK - 3 * modes, wires), BF16)
    state = state_ref[...]
    for c in reversed(range(cot_ref.shape[0] // CHUNK)):
        span = slice(c * CHUNK, (c + 1) * CHUNK)
        rows = slice(c * modes, (c + 1) * modes)
        lhs = jnp.concatenate([ka_ref[span, :], aux_ref[span, :]], axis=1)
        rhs = jnp.concatenate([cot_ref[span, :], zero2, state.astype(BF16), zero1], axis=0)
        acc = jnp.dot(lhs, rhs, preferred_element_type=F32)
        out_ref[span, :] = (acc * scale).astype(BF16)
        state = wide(decay_ref[rows, :], reps) * state + fresh_ref[rows, :]
    state_ref[...] = state


def on_hbm(a):
    return pltpu.with_memory_space_constraint(a, pltpu.HBM)


def steps_for(chunks):
    for steps in (4, 3, 2):
        if chunks % steps == 0:
            return steps
    return 1


def scan_devices(msg, reps, run_part, parts):
    n = lax.axis_size("tm")
    me = lax.axis_index("tm")
    before = jnp.zeros_like(msg[:reps])
    after = jnp.zeros_like(msg[:reps])
    d_before = jnp.ones_like(msg[2 * reps :])
    d_after = jnp.ones_like(msg[2 * reps :])
    hops = [1 << k for k in range(n.bit_length() - 1)]
    for index, hop in enumerate(hops):
        pairs = [(i, i ^ hop) for i in range(n)]
        upper = (me & hop) != 0
        mine_f, mine_a, mine_d = msg[:reps], msg[reps : 2 * reps], msg[2 * reps :]
        part = index - len(hops) + parts
        final = index == len(hops) - 1
        sent = jnp.where(upper, mine_a, mine_f) if final else msg
        sent = run_part.gate(part, sent)
        got = lax.ppermute(sent, "tm", pairs)
        got = run_part(part, got)
        if final:
            before = jnp.where(upper, d_before * got + before, before)
            after = jnp.where(upper, after, d_after * got + after)
        else:
            got_f, got_a, got_d = got[:reps], got[reps : 2 * reps], got[2 * reps :]
            next_f = jnp.where(upper, mine_d * got_f + mine_f, got_d * mine_f + got_f)
            next_a = jnp.where(upper, got_d * mine_a + got_a, mine_d * got_a + mine_a)
            msg = jnp.concatenate([next_f, next_a, mine_d * got_d], axis=0)
            before = jnp.where(upper, d_before * got_f + before, before)
            after = jnp.where(upper, after, d_after * got_a + after)
            d_before = jnp.where(upper, d_before * got_d, d_before)
            d_after = jnp.where(upper, d_after, d_after * got_d)
            msg, before, after, d_before, d_after = lax.optimization_barrier(
                (msg, before, after, d_before, d_after)
            )
    return before, after


class KernelParts:
    def __init__(self, heat, rates, fits, parts, params):
        self.heat, self.rates, self.fits, self.parts = heat, rates, fits, parts
        self.params, self.arrays = params, ()

    def gate(self, part, sent):
        if part >= 0:
            sent, self.rates = lax.optimization_barrier((sent, self.rates))
        return sent

    def __call__(self, part, got):
        if part < 0:
            return got
        modes, samples = self.heat.shape
        length = samples // self.parts
        inner = 2 if (length // CHUNK) % 2 == 0 else 1
        block = length // inner
        small = pl.BlockSpec((1, modes), lambda i: (0, 0))
        rest = len(self.arrays)
        self.arrays = tuple(
            pl.pallas_call(
                kernels_kernel,
                name="kernels",
                grid=(inner,),
                in_specs=[
                    pl.BlockSpec((modes, block), lambda i: (0, part * inner + i)),
                    small,
                    small,
                ]
                + [pl.BlockSpec(memory_space=pl.ANY)] * rest,
                out_specs=[pl.BlockSpec((block, CHUNK), lambda i: (part * inner + i, 0))] * 3,
                out_shape=[jax.ShapeDtypeStruct((samples, CHUNK), BF16)] * 3,
                input_output_aliases={3 + k: k for k in range(rest)},
                compiler_params=self.params,
                cost_estimate=pl.CostEstimate(
                    flops=20 * length * CHUNK * CHUNK, bytes_accessed=8 << 20, transcendentals=0
                ),
            )(on_hbm(self.heat), on_hbm(self.rates), on_hbm(self.fits), *self.arrays)
        )
        got, arrays = lax.optimization_barrier((got, self.arrays))
        self.arrays = arrays
        return got


def body(currents, seed_on_tension, mode_diffusivity_factor, decay_rates, fit_weights, counts):
    samples, wires = currents.shape
    modes = decay_rates.shape[0]
    devices = lax.axis_size("tm")
    chunks = samples // CHUNK
    steps = steps_for(chunks)
    block = samples // steps
    mblock = chunks * modes // steps
    reps = wires // CHUNK
    rates = decay_rates.reshape(1, modes)
    fits = fit_weights.reshape(1, modes)
    counts = counts.reshape(1, wires)
    params = pltpu.CompilerParams(vmem_limit_bytes=24 << 20)
    small = pl.BlockSpec((1, modes), lambda i: (0, 0))
    flops = 2 * samples * wires

    fresh_f, fresh_a, decay, msg = pl.pallas_call(
        totals_kernel,
        name="totals",
        grid=(steps,),
        in_specs=[
            pl.BlockSpec((modes, block), lambda i: (0, i)),
            small,
            small,
            pl.BlockSpec((block, wires), lambda i: (i, 0)),
            pl.BlockSpec((block, wires), lambda i: (i, 0)),
        ],
        out_specs=[
            pl.BlockSpec((mblock, wires), lambda i: (i, 0)),
            pl.BlockSpec((mblock, wires), lambda i: (i, 0)),
            pl.BlockSpec((mblock, CHUNK), lambda i: (i, 0)),
            pl.BlockSpec((2 * reps + 1, modes, CHUNK), lambda i: (0, 0, 0)),
        ],
        out_shape=[
            pltpu.HBM((chunks * modes, wires), F32),
            pltpu.HBM((chunks * modes, wires), F32),
            pltpu.HBM((chunks * modes, CHUNK), F32),
            jax.ShapeDtypeStruct((2 * reps + 1, modes, CHUNK), F32),
        ],
        scratch_shapes=[
            pltpu.VMEM((modes, wires), F32),
            pltpu.VMEM((modes, wires), F32),
            pltpu.VMEM((modes, CHUNK), F32),
        ],
        compiler_params=params,
        cost_estimate=pl.CostEstimate(
            flops=2 * modes * flops, bytes_accessed=14 << 20, transcendentals=0
        ),
    )(
        on_hbm(mode_diffusivity_factor),
        on_hbm(rates),
        on_hbm(fits),
        on_hbm(currents),
        on_hbm(seed_on_tension),
    )

    parts = 3 if chunks % 3 == 0 else 1
    covered = KernelParts(mode_diffusivity_factor, rates, fits, parts, params)
    before, after = scan_devices(msg, reps, covered, parts)
    kf, ka, aux = covered.arrays

    def common(reverse):
        def at(i):
            return (steps - 1 - i if reverse else i, 0)

        return [
            pl.BlockSpec((block, wires), at),
            pl.BlockSpec((block, CHUNK), at),
            pl.BlockSpec((block, CHUNK), at),
            pl.BlockSpec((mblock, wires), at),
            pl.BlockSpec((mblock, CHUNK), at),
            pl.BlockSpec((reps, modes, CHUNK), lambda i: (0, 0, 0)),
            pl.BlockSpec((1, wires), lambda i: (0, 0)),
        ], pl.BlockSpec((block, wires), at)

    specs, out_spec = common(False)
    tension, lse = pl.pallas_call(
        stress_kernel,
        name="stress",
        grid=(steps,),
        in_specs=specs,
        out_specs=[out_spec, pl.BlockSpec((devices, 1, wires), lambda i: (0, 0, 0))],
        out_shape=[
            jax.ShapeDtypeStruct((samples, wires), BF16),
            pltpu.HBM((devices, 1, wires), F32),
        ],
        scratch_shapes=[
            pltpu.VMEM((modes, wires), F32),
            pltpu.VMEM((8, wires), F32),
            pltpu.VMEM((8, wires), F32),
        ],
        compiler_params=params,
        cost_estimate=pl.CostEstimate(
            flops=2 * CHUNK * flops, bytes_accessed=10 << 20, transcendentals=0
        ),
    )(on_hbm(currents), kf, aux, on_hbm(fresh_f), on_hbm(decay), before, on_hbm(counts))

    all_lse = lax.all_to_all(lse, "tm", 0, 0, tiled=True)

    specs, out_spec = common(True)
    gradient = pl.pallas_call(
        adjoint_kernel,
        name="adjoint",
        grid=(steps,),
        in_specs=specs,
        out_specs=out_spec,
        out_shape=jax.ShapeDtypeStruct((samples, wires), BF16),
        scratch_shapes=[pltpu.VMEM((modes, wires), F32)],
        compiler_params=params,
        cost_estimate=pl.CostEstimate(
            flops=2 * CHUNK * flops, bytes_accessed=10 << 20, transcendentals=0
        ),
    )(on_hbm(seed_on_tension), ka, aux, on_hbm(fresh_a), on_hbm(decay), after, on_hbm(counts))

    top = jnp.max(all_lse, axis=0)
    total = jnp.sum(jnp.exp2(all_lse - top[None]), axis=0)
    softened = ((top * LN2 + jnp.log(total)) / SHARPNESS).reshape(wires)
    return (tension, gradient, softened)


def solution(mesh):
    placed = (P("tm", "parts"), P("tm", "parts"), P(None, ("parts", "tm")), P(), P(), P("parts"))
    return jax.shard_map(
        body,
        mesh=mesh,
        in_specs=placed,
        out_specs=(P("tm", "parts"), P("tm", "parts"), P("parts")),
        check_vma=False,
    )
```

time: 56 us -> 47.9 us (0.86)
  local copies, waits for them, and re-layouts: 7.88 us -> 0 us
  waiting for transfers between devices: 8.76 us -> 3.48 us
  Pallas kernels: 23.7 us -> 28.6 us
  starting transfers between devices: 11.7 us -> 13.6 us
  other arithmetic: 2.54 us -> 0.92 us
    unnamed x28 -> x0, local copies, waits for them, and re-layouts: 7.88 us -> none
    ppermute x4, waiting for transfers between devices: 8.75 us -> 2.04 us  [scan_devices(): got = lax.ppermute(sent, 'tm', pairs)]
    pallas_call x1 -> x3, Pallas kernels: 7.22 us -> 10.1 us  [__call__(): pl.pallas_call(kernels_kernel, name='kernels', grid=(inner,), in_specs=[p...]
    all_to_all x1, starting transfers between devices: 3.91 us -> 5.72 us  [body(): all_lse = lax.all_to_all(lse, 'tm', 0, 0, tiled=True)]
    select_n x1, other arithmetic: 1.7 us -> 0.02 us  [scan_devices(): after = jnp.where(upper, after, d_after * got + after)]
    pallas_call x1, Pallas kernels: 6.19 us -> 7.63 us  [body(): pl.pallas_call(totals_kernel, name='totals', grid=(steps,), in_specs=[pl....]
    all_to_all x1, waiting for transfers between devices: 0.01 us -> 1.44 us  [body(): all_lse = lax.all_to_all(lse, 'tm', 0, 0, tiled=True)]
  transfers between devices with their start and end apart: 5 -> 5, of which waited for: 3 -> 4; matrix products, arithmetic and copies ran while one was open for 0% -> 0% of each run, Pallas kernels for 22% -> 32%
where the time goes in v2:
time: 47.9 us; the launch traced here: 47.4 us
  Pallas kernels  28.6 us (60%)
  starting transfers between devices  13.6 us (28%)
  waiting for transfers between devices  3.48 us (7%)
  other arithmetic  0.92 us (2%)
  between operations  0.74 us (2%)
    pallas_call x3, Pallas kernels, __call__(): pl.pallas_call(kernels_kernel, name='kernels', grid=(inner,), in_specs=[p...  10.1 us
    ppermute x4, starting transfers between devices, scan_devices(): got = lax.ppermute(sent, 'tm', pairs)  7.89 us
    pallas_call x1, Pallas kernels, body(): pl.pallas_call(totals_kernel, name='totals', grid=(steps,), in_specs=[pl....  7.63 us
    pallas_call x1, Pallas kernels, body(): pl.pallas_call(stress_kernel, name='stress', grid=(steps,), in_specs=spec...  5.72 us
    all_to_all x1, starting transfers between devices, body(): all_lse = lax.all_to_all(lse, 'tm', 0, 0, tiled=True)  5.72 us
    pallas_call x1, Pallas kernels, body(): pl.pallas_call(adjoint_kernel, name='adjoint', grid=(steps,), in_specs=sp...  5.19 us
    ppermute x4, waiting for transfers between devices, scan_devices(): got = lax.ppermute(sent, 'tm', pairs)  2.04 us
    all_to_all x1, waiting for transfers between devices, body(): all_lse = lax.all_to_all(lse, 'tm', 0, 0, tiled=True)  1.44 us
  transfers between devices with their start and end apart: 5, of which 4 were waited for; matrix products, arithmetic and copies ran while one was open for 0% of the time, Pallas kernels for 32%

profile of v2, /device:TPU:0, one launch (start us, length us, event | category | flops | bytes accessed | tf_op | source)
XLA Modules:
  0.0 47.4 jit_solution(6919824698987861650)
XLA Ops:
  0.6 7.6 %totals.1 = (f32[768,512]{1,0:T(8,128)}, f32[768,512]{1,0:T(8,128)}, f32[768,128]{1,0:T(8,128)}, f32[9,32,128]{2,1,0:T(8,128)S(1)}) custom-call(f32[32,3072]{1,0:T(8,128)} %heat_ref.7, f32[1,32]{1,0:T(1,128)} %bitcast.29, f32[1,32]{1,0:T(1,128)} %bitcast.33, bf16[3072,512]{1,0:T(8,128)(2,1)} %cur_ref.3, bf16[3072,512]{1,0:T(8,128)(2,1)} %cot_ref.3), custom_call_target="tpu_custom_call" | custom-call | flops 201326592 | bytes 14680064 | tf_op jit(solution)/shard_map/totals/pallas_call | solution.py:342
  8.3 0.5 collective-permute-start
  8.7 1.0 %collective-permute-done = f32[9,32,128]{2,1,0:T(8,128)S(1)} collective-permute-done((f32[9,32,128]{2,1,0:T(8,128)S(1)}, f32[9,32,128]{2,1,0:T(8,128)S(1)}, u32[]{:S(2)}, u32[]{:S(2)}) %collective-permute-start) | collective-permute-done | bytes 147488 | tf_op jit(solution)/shard_map/ppermute | solution.py:262
  9.8 2.9 %collective-permute-start.1 = (f32[9,32,128]{2,1,0:T(8,128)S(1)}, f32[9,32,128]{2,1,0:T(8,128)S(1)}, u32[]{:S(2)}, u32[]{:S(2)}) collective-permute-start(f32[9,32,128]{2,1,0:T(8,128)S(1)} %pad_maximum_fusion), channel_id=1, source_target_pairs={{0,2},{1,3},{2,0},{3,1},{4,6},{5,7},{6,4},{7,5},{8,10},{9,11},{10,... | collective-permute-start | bytes 442376 | tf_op jit(solution)/shard_map/ppermute | solution.py:262
  12.7 3.3 %kernels.3 = (bf16[3072,128]{1,0:T(8,128)(2,1)S(1)}, bf16[3072,128]{1,0:T(8,128)(2,1)S(1)}, bf16[3072,128]{1,0:T(8,128)(2,1)S(1)}) custom-call(f32[32,3072]{1,0:T(8,128)} %heat_ref.7, f32[1,32]{1,0:T(1,128)} %bitcast.30, f32[1,32]{1,0:T(1,128)} %bitcast.34), custom_call_target="tpu_custom_call" | custom-call | flops 335544320 | bytes 8388608 | tf_op jit(solution)/shard_map/kernels/pallas_call | solution.py:302
  16.1 0.8 %collective-permute-done.1 = f32[9,32,128]{2,1,0:T(8,128)S(1)} collective-permute-done((f32[9,32,128]{2,1,0:T(8,128)S(1)}, f32[9,32,128]{2,1,0:T(8,128)S(1)}, u32[]{:S(2)}, u32[]{:S(2)}) %collective-permute-start.1) | collective-permute-done | bytes 147488 | tf_op jit(solution)/shard_map/ppermute | solution.py:262
  17.0 1.9 %collective-permute-start.2 = (f32[9,32,128]{2,1,0:T(8,128)S(1)}, f32[9,32,128]{2,1,0:T(8,128)S(1)}, u32[]{:S(2)}, u32[]{:S(2)}) collective-permute-start(f32[9,32,128]{2,1,0:T(8,128)S(1)} %pad_maximum_fusion.1), channel_id=1, source_target_pairs={{0,4},{1,5},{2,6},{3,7},{4,0},{5,1},{6,2},{7,3},{8,12},{9,13},{10,... | collective-permute-start | bytes 442376 | tf_op jit(solution)/shard_map/ppermute | solution.py:262
  18.8 3.4 %kernels.4 = (bf16[3072,128]{1,0:T(8,128)(2,1)S(1)}, bf16[3072,128]{1,0:T(8,128)(2,1)S(1)}, bf16[3072,128]{1,0:T(8,128)(2,1)S(1)}) custom-call(f32[32,3072]{1,0:T(8,128)} %heat_ref.7, f32[1,32]{1,0:T(1,128)} %bitcast.31, f32[1,32]{1,0:T(1,128)} %bitcast.35, ...), custom_call_target="tpu_custom_call", output_to_operand_aliasing={{0}: (3, {}), {1}: (4, {}), {2}: (5, {})} | custom-call | flops 335544320 | bytes 8388608 | tf_op jit(solution)/shard_map/kernels/pallas_call | solution.py:302
  22.2 0.2 collective-permute-done.2
  22.5 2.6 %collective-permute-start.3 = (f32[4,32,128]{2,1,0:T(8,128)S(1)}, f32[4,32,128]{2,1,0:T(8,128)S(1)}, u32[]{:S(2)}, u32[]{:S(2)}) collective-permute-start(f32[4,32,128]{2,1,0:T(8,128)S(1)} %slice_select_fusion), channel_id=1, source_target_pairs={{0,8},{1,9},{2,10},{3,11},{4,12},{5,13},{6,14},{7,15},{8,0},{9,1},... | collective-permute-start | bytes 196616 | tf_op jit(solution)/shard_map/ppermute | solution.py:262
  25.2 3.4 %kernels.5 = (bf16[3072,128]{1,0:T(8,128)(2,1)S(1)}, bf16[3072,128]{1,0:T(8,128)(2,1)S(1)}, bf16[3072,128]{1,0:T(8,128)(2,1)S(1)}) custom-call(f32[32,3072]{1,0:T(8,128)} %heat_ref.7, f32[1,32]{1,0:T(1,128)} %bitcast.32, f32[1,32]{1,0:T(1,128)} %bitcast.36, ...), custom_call_target="tpu_custom_call", output_to_operand_aliasing={{0}: (3, {}), {1}: (4, {}), {2}: (5, {})} | custom-call | flops 335544320 | bytes 8388608 | tf_op jit(solution)/shard_map/kernels/pallas_call | solution.py:302
  28.5 0.0 collective-permute-done.3
  28.6 5.7 %stress.1 = (bf16[3072,512]{1,0:T(8,128)(2,1)}, f32[16,1,512]{2,1,0:T(1,128)}) custom-call(bf16[3072,512]{1,0:T(8,128)(2,1)} %cur_ref.3, bf16[3072,128]{1,0:T(8,128)(2,1)S(1)} %get-tuple-element.86.kf_ref, bf16[3072,128]{1,0:T(8,128)(2,1)S(1)} %get-tuple-element.87.aux_ref, f32[768,512]{1,0:T(8,128)} %get-tuple-element.88.fresh_ref, ...), custom_call_target="tpu_custom_call" | custom-call | flops 805306368 | bytes 10485760 | tf_op jit(solution)/shard_map/stress/pallas_call | solution.py:402
  34.3 5.7 %all-to-all-start = ((f32[16,1,512]{2,1,0:T(1,128)}), f32[16,1,512]{2,1,0:T(1,128)S(1)}, u32[]{:S(2)}, u32[]{:S(2)}) async-start(f32[16,1,512]{2,1,0:T(1,128)} %get-tuple-element.98), calls=%async_computation | async-start | bytes 65536 | tf_op jit(solution)/shard_map/all_to_all | solution.py:423
  40.0 5.2 %adjoint.1 = bf16[3072,512]{1,0:T(8,128)(2,1)} custom-call(bf16[3072,512]{1,0:T(8,128)(2,1)} %cot_ref.3, bf16[3072,128]{1,0:T(8,128)(2,1)S(1)} %get-tuple-element.94.ka_ref, bf16[3072,128]{1,0:T(8,128)(2,1)S(1)} %get-tuple-element.87.aux_ref, f32[768,512]{1,0:T(8,128)} %get-tuple-element.95.fresh_ref, f32[768,128]{1,0:T(8,128)} %get-tuple-element.89.decay_ref, ...), custom_call_target="tpu_custom_call" | custom-call | flops 805306368 | bytes 10485760 | tf_op jit(solution)/shard_map/adjoint/pallas_call | solution.py:426
  45.2 1.4 %all-to-all-done = f32[16,1,512]{2,1,0:T(1,128)S(1)} async-done(((f32[16,1,512]{2,1,0:T(1,128)}), f32[16,1,512]{2,1,0:T(1,128)S(1)}, u32[]{:S(2)}, u32[]{:S(2)}) %all-to-all-start) | async-done | bytes 32800 | tf_op jit(solution)/shard_map/all_to_all | solution.py:423
  46.7 0.1 exponential_reduce_fusion
  46.8 0.6 %add_multiply_fusion = f32[512]{0:T(512)} fusion(f32[512]{0:T(512)S(1)} %exponential_reduce_fusion, f32[512]{0:T(512)S(1)} %reduce_max.9), kind=kLoop, calls=%fused_computation.34 | loop fusion | flops 1536 | bytes 6144 | tf_op jit(solution)/shard_map/div | solution.py:442
  (12 shorter events, 0.3 us)
Async XLA Ops:
  8.3 1.5 %collective-permute-start = (f32[9,32,128]{2,1,0:T(8,128)S(1)}, f32[9,32,128]{2,1,0:T(8,128)S(1)}, u32[]{:S(2)}, u32[]{:S(2)}) collective-permute-start(f32[9,32,128]{2,1,0:T(8,128)S(1)} %get-tuple-element.51), channel_id=1, source_target_pairs={{0,1},{1,0},{2,3},{3,2},{4,5},{5,4},{6,7},{7,6},{8,9},{9,8},{10,11... | collective-permute-start | bytes 442376 | tf_op jit(solution)/shard_map/ppermute | solution.py:262
  9.8 7.1 %collective-permute-start.1 = (f32[9,32,128]{2,1,0:T(8,128)S(1)}, f32[9,32,128]{2,1,0:T(8,128)S(1)}, u32[]{:S(2)}, u32[]{:S(2)}) collective-permute-start(f32[9,32,128]{2,1,0:T(8,128)S(1)} %pad_maximum_fusion), channel_id=1, source_target_pairs={{0,2},{1,3},{2,0},{3,1},{4,6},{5,7},{6,4},{7,5},{8,10},{9,11},{10,... | collective-permute-start | bytes 442376 | tf_op jit(solution)/shard_map/ppermute | solution.py:262
  17.0 5.5 %collective-permute-start.2 = (f32[9,32,128]{2,1,0:T(8,128)S(1)}, f32[9,32,128]{2,1,0:T(8,128)S(1)}, u32[]{:S(2)}, u32[]{:S(2)}) collective-permute-start(f32[9,32,128]{2,1,0:T(8,128)S(1)} %pad_maximum_fusion.1), channel_id=1, source_target_pairs={{0,4},{1,5},{2,6},{3,7},{4,0},{5,1},{6,2},{7,3},{8,12},{9,13},{10,... | collective-permute-start | bytes 442376 | tf_op jit(solution)/shard_map/ppermute | solution.py:262
  22.5 6.0 %collective-permute-start.3 = (f32[4,32,128]{2,1,0:T(8,128)S(1)}, f32[4,32,128]{2,1,0:T(8,128)S(1)}, u32[]{:S(2)}, u32[]{:S(2)}) collective-permute-start(f32[4,32,128]{2,1,0:T(8,128)S(1)} %slice_select_fusion), channel_id=1, source_target_pairs={{0,8},{1,9},{2,10},{3,11},{4,12},{5,13},{6,14},{7,15},{8,0},{9,1},... | collective-permute-start | bytes 196616 | tf_op jit(solution)/shard_map/ppermute | solution.py:262
  34.3 12.4 %all-to-all-start = ((f32[16,1,512]{2,1,0:T(1,128)}), f32[16,1,512]{2,1,0:T(1,128)S(1)}, u32[]{:S(2)}, u32[]{:S(2)}) async-start(f32[16,1,512]{2,1,0:T(1,128)} %get-tuple-element.98), calls=%async_computation | async-start | bytes 65536 | tf_op jit(solution)/shard_map/all_to_all | solution.py:423

commit v3 on v2

v3 whole, which is shorter than its diff:
```python
import functools
import math

import jax
import jax.numpy as jnp
from jax import lax
from jax.experimental import pallas as pl
from jax.experimental.pallas import tpu as pltpu
from jax.sharding import PartitionSpec as P

CHUNK = 128
LEVELS = 7
SHARPNESS = 4.0
LOG2E = math.log2(math.e)
LN2 = math.log(2.0)
F32 = jnp.float32
BF16 = jnp.bfloat16


def as_column(row):
    m = row.shape[1]
    r = lax.broadcasted_iota(jnp.int32, (m, m), 0)
    c = lax.broadcasted_iota(jnp.int32, (m, m), 1)
    return jnp.sum(jnp.where(r == c, jnp.broadcast_to(row, (m, m)), 0.0), axis=1, keepdims=True)


def rates_and_gains(rates_ref, fit_ref):
    rates = as_column(rates_ref[...])
    gains = as_column(fit_ref[...]) * jnp.sqrt(rates)
    return rates * LOG2E, gains


def doubling(heat, with_levels):
    lane = lax.broadcasted_iota(jnp.int32, heat.shape, 1)
    pre, suf = heat, jnp.zeros_like(heat)
    tables = []
    for level in range(LEVELS):
        half = 1 << level
        second = (lane & half) != 0
        if with_levels:
            tables.append(jnp.exp2(-jnp.where(second, pre, suf)))
        total = pre + suf
        sibling = jnp.where(
            second, pltpu.roll(total, half, 1), pltpu.roll(total, CHUNK - half, 1)
        )
        pre = jnp.where(second, pre + sibling, pre)
        suf = jnp.where(second, suf, suf + sibling)
    return pre, suf, tables


def wide(a, times):
    return jnp.concatenate([a] * times, axis=1)


def stacked(heat_ref, speed, first, count):
    return jnp.concatenate(
        [
            heat_ref[:, c * CHUNK : (c + 1) * CHUNK] * speed
            for c in range(first, first + count)
        ],
        axis=0,
    )


def group_of(chunks, most):
    return max(g for g in range(1, most + 1) if chunks % g == 0)


def pieces_of(chunks):
    if chunks % 8:
        return [1] * chunks
    unit = chunks // 8
    return [3 * unit, 2 * unit, 2 * unit, unit]


def prefixes(heat):
    high = heat.astype(BF16)
    rest = heat - high.astype(F32)
    middle = rest.astype(BF16)
    low = (rest - middle.astype(F32)).astype(BF16)
    v = lax.broadcasted_iota(jnp.int32, (CHUNK, CHUNK), 0)
    u = lax.broadcasted_iota(jnp.int32, (CHUNK, CHUNK), 1)
    ones = jnp.concatenate(
        [jnp.where(v <= u, 1.0, 0.0).astype(BF16), jnp.where(v > u, 1.0, 0.0).astype(BF16)],
        axis=1,
    )
    both = jnp.dot(
        jnp.concatenate([high, middle, low], axis=1),
        jnp.concatenate([ones] * 3, axis=0),
        preferred_element_type=F32,
    )
    return both[:, :CHUNK], both[:, CHUNK:]


def totals_kernel(
    heat_hbm, rates_hbm, fits_hbm, cur_hbm, cot_hbm,
    cur_ref, fresh_f_ref, fresh_a_ref, decay_ref, msg_ref,
    cot_ref, heat_ref, rates_ref, fits_ref, start_ref, back_ref, small_sem, cur_sem, cot_sem,
):
    modes = heat_ref.shape[0]
    samples, wires = cur_ref.shape
    reps = wires // CHUNK
    chunks = samples // CHUNK
    group = group_of(chunks, 3)

    small = [
        pltpu.make_async_copy(heat_hbm, heat_ref, small_sem.at[0]),
        pltpu.make_async_copy(rates_hbm, rates_ref, small_sem.at[1]),
        pltpu.make_async_copy(fits_hbm, fits_ref, small_sem.at[2]),
    ]
    for copy in small:
        copy.start()
    loads = []
    at = 0
    for k, piece in enumerate(pieces_of(chunks)):
        rows = pl.ds(at * CHUNK, piece * CHUNK)
        pair = (
            pltpu.make_async_copy(cur_hbm.at[rows], cur_ref.at[rows], cur_sem.at[k]),
            pltpu.make_async_copy(cot_hbm.at[rows], cot_ref.at[rows], cot_sem.at[k]),
        )
        for copy in pair:
            copy.start()
        loads.append((at, piece, pair))
        at += piece
    for copy in small:
        copy.wait()

    speed, gains = rates_and_gains(rates_ref, fits_ref)
    gain_stack = jnp.concatenate([gains] * group, axis=0)
    for first in range(0, chunks, group):
        rows = slice(first * modes, (first + group) * modes)
        pre, suf = prefixes(stacked(heat_ref, speed, first, group))
        start_ref[rows, :] = (gain_stack * jnp.exp2(-pre)).astype(BF16)
        back_ref[rows, :] = jnp.exp2(-suf).astype(BF16)
        decay_ref[rows, :] = jnp.exp2(-(pre + suf))

    tf = jnp.zeros((modes, wires), F32)
    ta = jnp.zeros((modes, wires), F32)
    dc = jnp.ones((modes, CHUNK), F32)
    for first, piece, pair in loads:
        for copy in pair:
            copy.wait()
        for c in range(first, first + piece):
            span = slice(c * CHUNK, (c + 1) * CHUNK)
            rows = slice(c * modes, (c + 1) * modes)
            decay = decay_ref[rows, :]
            fresh_f = jnp.dot(back_ref[rows, :], cur_ref[span, :], preferred_element_type=F32)
            fresh_a = jnp.dot(start_ref[rows, :], cot_ref[span, :], preferred_element_type=F32)
            fresh_f_ref[rows, :] = fresh_f
            fresh_a_ref[rows, :] = fresh_a.astype(BF16)
            tf = wide(decay, reps) * tf + fresh_f
            ta = ta + wide(dc, reps) * fresh_a
            dc = dc * decay
    for k in range(reps):
        lanes = slice(k * CHUNK, (k + 1) * CHUNK)
        msg_ref[k] = tf[:, lanes]
        msg_ref[reps + k] = ta[:, lanes]
    msg_ref[2 * reps] = dc


def kernels_kernel(heat_ref, rates_ref, fit_ref, *refs):
    kf_ref, ka_ref, aux_ref = refs[-3:]
    modes = heat_ref.shape[0]
    chunks = heat_ref.shape[1] // CHUNK
    group = group_of(chunks, 2)
    speed, gains = rates_and_gains(rates_ref, fit_ref)
    gain_sum = jnp.sum(gains, axis=0, keepdims=True)
    t = lax.broadcasted_iota(jnp.int32, (CHUNK, CHUNK), 0)
    s = lax.broadcasted_iota(jnp.int32, (CHUNK, CHUNK), 1)
    apart = jnp.where(t >= s, t ^ s, -1)
    base = jnp.where(apart == 0, jnp.broadcast_to(gain_sum, (CHUNK, CHUNK)), 0.0)
    zero = jnp.zeros((modes, CHUNK), BF16)
    for first in range(0, chunks, group):
        pres, sufs, stacks = doubling(stacked(heat_ref, speed, first, group), True)
        for c in range(group):
            part = slice(c * modes, (c + 1) * modes)
            span = slice((first + c) * CHUNK, (first + c + 1) * CHUNK)
            pre, suf = pres[part], sufs[part]
            tables = [e[part] for e in stacks]
            left = [gains * e for e in tables]
            right = [e.astype(BF16) for e in tables]
            kernel = base
            for lv in range(0, LEVELS - 1, 2):
                lhs = jnp.concatenate([left[lv], left[lv + 1]], axis=0).T.astype(BF16)
                rhs = jnp.concatenate(
                    [
                        jnp.concatenate([right[lv], zero], axis=1),
                        jnp.concatenate([zero, right[lv + 1]], axis=1),
                    ],
                    axis=0,
                )
                both = jnp.dot(lhs, rhs, preferred_element_type=F32)
                kernel = jnp.where(apart >= (1 << lv), both[:, :CHUNK], kernel)
                kernel = jnp.where(apart >= (2 << lv), both[:, CHUNK:], kernel)
            back = jnp.exp2(-suf)
            aux = jnp.concatenate(
                [gains * jnp.exp2(-pre), back, left[LEVELS - 1], back], axis=0
            ).T.astype(BF16)
            rhs = jnp.concatenate([zero, zero, right[LEVELS - 1], zero], axis=0)
            last = jnp.dot(aux, rhs, preferred_element_type=F32)
            kernel = jnp.where(apart >= (1 << (LEVELS - 1)), last, kernel)
            kf_ref[span, :] = kernel.astype(BF16)
            ka_ref[span, :] = kernel.T.astype(BF16)
            aux_ref[span, :] = aux


def stress_kernel(
    cur_ref, kf_ref, aux_ref, fresh_ref, decay_ref, in_ref, counts_ref,
    out_hbm, lse_ref, out_ref, sem,
):
    samples, wires = cur_ref.shape
    reps = wires // CHUNK
    modes = in_ref.shape[1]
    scale = counts_ref[...].astype(F32) * 0.25
    scale2 = scale * (SHARPNESS * LOG2E)
    state = jnp.concatenate([in_ref[k] for k in range(reps)], axis=1)
    high = jnp.full((8, wires), -1e30, F32)
    amount = jnp.zeros((8, wires), F32)
    stores = []
    first = 0
    for k, piece in enumerate(pieces_of(samples // CHUNK)):
        for c in range(first, first + piece):
            span = slice(c * CHUNK, (c + 1) * CHUNK)
            rows = slice(c * modes, (c + 1) * modes)
            acc = jnp.dot(kf_ref[span, :], cur_ref[span, :], preferred_element_type=F32) + jnp.dot(
                aux_ref[span, :modes], state.astype(BF16), preferred_element_type=F32
            )
            out_ref[span, :] = (acc * scale).astype(BF16)
            z = (acc * scale2).reshape(CHUNK // 8, 8, wires)
            new = jnp.maximum(high, jnp.max(z, axis=0))
            amount = amount * jnp.exp2(high - new) + jnp.sum(jnp.exp2(z - new[None]), axis=0)
            high = new
            state = wide(decay_ref[rows, :], reps) * state + fresh_ref[rows, :]
        done = pl.ds(first * CHUNK, piece * CHUNK)
        copy = pltpu.make_async_copy(out_ref.at[done], out_hbm.at[done], sem.at[k])
        copy.start()
        stores.append(copy)
        first += piece
    top = jnp.max(high, axis=0, keepdims=True)
    total = jnp.sum(amount * jnp.exp2(high - top), axis=0, keepdims=True)
    value = top + jnp.log(total) * LOG2E
    lse_ref[...] = jnp.broadcast_to(value[None], lse_ref.shape)
    for copy in stores:
        copy.wait()


def adjoint_kernel(
    cot_hbm, ka_ref, aux_ref, fresh_ref, decay_ref, in_ref, counts_ref,
    out_hbm, cot_ref, out_ref, load_sem, sem,
):
    samples, wires = cot_ref.shape
    reps = wires // CHUNK
    chunks = samples // CHUNK
    modes = in_ref.shape[1]
    scale = counts_ref[...].astype(F32) * 0.25
    zero = jnp.zeros((modes, wires), BF16)
    state = jnp.concatenate([in_ref[k] for k in range(reps)], axis=1)
    loads = []
    end = chunks
    for k, piece in enumerate(pieces_of(chunks)):
        rows = pl.ds((end - piece) * CHUNK, piece * CHUNK)
        copy = pltpu.make_async_copy(cot_hbm.at[rows], cot_ref.at[rows], load_sem.at[k])
        copy.start()
        loads.append(copy)
        end -= piece
    stores = []
    end = chunks
    for k, piece in enumerate(pieces_of(chunks)):
        loads[k].wait()
        for c in reversed(range(end - piece, end)):
            span = slice(c * CHUNK, (c + 1) * CHUNK)
            rows = slice(c * modes, (c + 1) * modes)
            carried = jnp.concatenate([zero, state.astype(BF16)], axis=0)
            acc = jnp.dot(ka_ref[span, :], cot_ref[span, :], preferred_element_type=F32) + jnp.dot(
                aux_ref[span, : 2 * modes], carried, preferred_element_type=F32
            )
            out_ref[span, :] = (acc * scale).astype(BF16)
            state = wide(decay_ref[rows, :], reps) * state + fresh_ref[rows, :].astype(F32)
        done = pl.ds((end - piece) * CHUNK, piece * CHUNK)
        copy = pltpu.make_async_copy(out_ref.at[done], out_hbm.at[done], sem.at[k])
        copy.start()
        stores.append(copy)
        end -= piece
    for copy in stores:
        copy.wait()


def on_vmem(a):
    return pltpu.with_memory_space_constraint(a, pltpu.VMEM)


def on_hbm(a):
    return pltpu.with_memory_space_constraint(a, pltpu.HBM)


def hops_of(n):
    return [1 << k for k in range(n.bit_length() - 1)]


def scan_devices(msg, uppers, reps, run_part, parts):
    n = lax.axis_size("tm")
    before = jnp.zeros_like(msg[:reps])
    after = jnp.zeros_like(msg[:reps])
    d_before = jnp.ones_like(msg[2 * reps :])
    d_after = jnp.ones_like(msg[2 * reps :])
    hops = hops_of(n)
    for index, hop in enumerate(hops):
        pairs = [(i, i ^ hop) for i in range(n)]
        upper = uppers[index]
        mine_f, mine_a, mine_d = msg[:reps], msg[reps : 2 * reps], msg[2 * reps :]
        part = index - len(hops) + parts
        final = index == len(hops) - 1
        sent = jnp.where(upper, mine_a, mine_f) if final else msg
        sent = run_part.gate(part, sent)
        got = lax.ppermute(sent, "tm", pairs)
        got = run_part(part, got)
        if final:
            before = jnp.where(upper, d_before * got + before, before)
            after = jnp.where(upper, after, d_after * got + after)
        else:
            got_f, got_a, got_d = got[:reps], got[reps : 2 * reps], got[2 * reps :]
            next_f = jnp.where(upper, mine_d * got_f + mine_f, got_d * mine_f + got_f)
            next_a = jnp.where(upper, got_d * mine_a + got_a, mine_d * got_a + mine_a)
            msg = jnp.concatenate([next_f, next_a, mine_d * got_d], axis=0)
            before = jnp.where(upper, d_before * got_f + before, before)
            after = jnp.where(upper, after, d_after * got_a + after)
            d_before = jnp.where(upper, d_before * got_d, d_before)
            d_after = jnp.where(upper, d_after, d_after * got_d)
            msg, before, after, d_before, d_after = lax.optimization_barrier(
                (msg, before, after, d_before, d_after)
            )
    return before, after


class KernelParts:
    def __init__(self, heat, rates, fits, parts, params):
        self.heat, self.rates, self.fits, self.parts = heat, rates, fits, parts
        self.params, self.arrays = params, ()

    def gate(self, part, sent):
        if part >= 0:
            sent, self.rates = lax.optimization_barrier((sent, self.rates))
        return sent

    def __call__(self, part, got):
        if part < 0:
            return got
        modes, samples = self.heat.shape
        length = samples // self.parts
        inner = 2 if (length // CHUNK) % 2 == 0 else 1
        block = length // inner
        small = pl.BlockSpec((1, modes), lambda i: (0, 0))
        rest = len(self.arrays)
        self.arrays = tuple(
            pl.pallas_call(
                kernels_kernel,
                name="kernels",
                grid=(inner,),
                in_specs=[
                    pl.BlockSpec((modes, block), lambda i: (0, part * inner + i)),
                    small,
                    small,
                ]
                + [pl.BlockSpec(memory_space=pl.ANY)] * rest,
                out_specs=[pl.BlockSpec((block, CHUNK), lambda i: (part * inner + i, 0))] * 3,
                out_shape=[jax.ShapeDtypeStruct((samples, CHUNK), BF16)] * 3,
                input_output_aliases={3 + k: k for k in range(rest)},
                compiler_params=self.params,
                cost_estimate=pl.CostEstimate(
                    flops=20 * length * CHUNK * CHUNK, bytes_accessed=8 << 20, transcendentals=0
                ),
            )(on_hbm(self.heat), on_hbm(self.rates), on_hbm(self.fits), *self.arrays)
        )
        got, arrays = lax.optimization_barrier((got, self.arrays))
        self.arrays = arrays
        return got


def body(currents, seed_on_tension, mode_diffusivity_factor, decay_rates, fit_weights, counts):
    samples, wires = currents.shape
    modes = decay_rates.shape[0]
    devices = lax.axis_size("tm")
    chunks = samples // CHUNK
    reps = wires // CHUNK
    me = lax.axis_index("tm")
    uppers = tuple((me & hop) != 0 for hop in hops_of(devices))
    rates, uppers = lax.optimization_barrier((decay_rates.reshape(1, modes), uppers))
    fits = fit_weights.reshape(1, modes)
    counts = counts.reshape(1, wires)
    params = pltpu.CompilerParams(vmem_limit_bytes=16 << 20)
    apart = pl.BlockSpec(memory_space=pl.ANY)
    whole = pl.BlockSpec(memory_space=pltpu.VMEM)
    flops = 2 * samples * wires
    copies = len(pieces_of(chunks))

    cur, fresh_f, fresh_a, decay, msg = pl.pallas_call(
        totals_kernel,
        name="totals",
        in_specs=[apart] * 5,
        out_specs=[whole] * 5,
        out_shape=[
            pltpu.VMEM((samples, wires), BF16),
            pltpu.VMEM((chunks * modes, wires), F32),
            pltpu.VMEM((chunks * modes, wires), BF16),
            pltpu.VMEM((chunks * modes, CHUNK), F32),
            pltpu.VMEM((2 * reps + 1, modes, CHUNK), F32),
        ],
        scratch_shapes=[
            pltpu.VMEM((samples, wires), BF16),
            pltpu.VMEM((modes, samples), F32),
            pltpu.VMEM((1, modes), F32),
            pltpu.VMEM((1, modes), F32),
            pltpu.VMEM((chunks * modes, CHUNK), BF16),
            pltpu.VMEM((chunks * modes, CHUNK), BF16),
            pltpu.SemaphoreType.DMA((3,)),
            pltpu.SemaphoreType.DMA((copies,)),
            pltpu.SemaphoreType.DMA((copies,)),
        ],
        compiler_params=params,
        cost_estimate=pl.CostEstimate(
            flops=2 * modes * flops, bytes_accessed=14 << 20, transcendentals=0
        ),
    )(
        on_hbm(mode_diffusivity_factor),
        on_hbm(rates),
        on_hbm(fits),
        on_hbm(currents),
        on_hbm(seed_on_tension),
    )

    parts = 3 if chunks % 3 == 0 else 1
    covered = KernelParts(mode_diffusivity_factor, rates, fits, parts, params)
    before, after = scan_devices(msg, uppers, reps, covered, parts)
    kf, ka, aux = covered.arrays

    tension, lse = pl.pallas_call(
        stress_kernel,
        name="stress",
        in_specs=[whole] * 7,
        out_specs=[apart, whole],
        out_shape=[
            pltpu.HBM((samples, wires), BF16),
            pltpu.HBM((devices, 1, wires), F32),
        ],
        scratch_shapes=[pltpu.VMEM((samples, wires), BF16), pltpu.SemaphoreType.DMA((copies,))],
        compiler_params=params,
        cost_estimate=pl.CostEstimate(
            flops=2 * CHUNK * flops, bytes_accessed=10 << 20, transcendentals=0
        ),
    )(*map(on_vmem, (cur, kf, aux, fresh_f, decay, before, counts)))

    all_lse = lax.all_to_all(lse, "tm", 0, 0, tiled=True)

    gradient = pl.pallas_call(
        adjoint_kernel,
        name="adjoint",
        in_specs=[apart] + [whole] * 6,
        out_specs=apart,
        out_shape=pltpu.HBM((samples, wires), BF16),
        scratch_shapes=[
            pltpu.VMEM((samples, wires), BF16),
            pltpu.VMEM((samples, wires), BF16),
            pltpu.SemaphoreType.DMA((copies,)),
            pltpu.SemaphoreType.DMA((copies,)),
        ],
        compiler_params=params,
        cost_estimate=pl.CostEstimate(
            flops=2 * CHUNK * flops, bytes_accessed=10 << 20, transcendentals=0
        ),
    )(
        on_hbm(seed_on_tension),
        *map(on_vmem, (ka, aux, fresh_a, decay, after, counts)),
    )

    top = jnp.max(all_lse, axis=0)
    total = jnp.sum(jnp.exp2(all_lse - top[None]), axis=0)
    softened = ((top * LN2 + jnp.log(total)) / SHARPNESS).reshape(wires)
    return (tension, gradient, softened)


def solution(mesh):
    placed = (P("tm", "parts"), P("tm", "parts"), P(None, ("parts", "tm")), P(), P(), P("parts"))
    return jax.shard_map(
        body,
        mesh=mesh,
        in_specs=placed,
        out_specs=(P("tm", "parts"), P("tm", "parts"), P("parts")),
        check_vma=False,
    )
```

time: 47.9 us -> 42.3 us (0.88)
  Pallas kernels: 28.6 us -> 23.2 us
    pallas_call x3, Pallas kernels: 18.5 us -> 12.1 us  [the longest x1 4.45 us: body(): pl.pallas_call(totals_kernel, name='totals', in_specs=[apart] * 5, out_sp...]
    pallas_call x3, Pallas kernels: 10.1 us -> 11.1 us  [__call__(): pl.pallas_call(kernels_kernel, name='kernels', grid=(inner,), in_specs=[p...]
    all_to_all x1, waiting for transfers between devices: 1.44 us -> 2.32 us  [body(): all_lse = lax.all_to_all(lse, 'tm', 0, 0, tiled=True)]
    ppermute x4, waiting for transfers between devices: 2.04 us -> 1.45 us  [scan_devices(): got = lax.ppermute(sent, 'tm', pairs)]
  transfers between devices with their start and end apart: 5 -> 5, of which waited for: 4 -> 3; matrix products, arithmetic and copies ran while one was open for 0% -> 0% of each run, Pallas kernels for 32% -> 37%
where the time goes in v3:
time: 42.3 us; the launch traced here: 42 us
  Pallas kernels  23.2 us (55%)
  starting transfers between devices  13.3 us (31%)
  waiting for transfers between devices  3.77 us (9%)
  other arithmetic  0.93 us (2%)
  between operations  0.81 us (2%)
    pallas_call x3, Pallas kernels, __call__(): pl.pallas_call(kernels_kernel, name='kernels', grid=(inner,), in_specs=[p...  11.1 us
    ppermute x4, starting transfers between devices, scan_devices(): got = lax.ppermute(sent, 'tm', pairs)  7.97 us
    all_to_all x1, starting transfers between devices, body(): all_lse = lax.all_to_all(lse, 'tm', 0, 0, tiled=True)  5.32 us
    pallas_call x1, Pallas kernels, body(): pl.pallas_call(totals_kernel, name='totals', in_specs=[apart] * 5, out_sp...  4.45 us
    pallas_call x1, Pallas kernels, body(): pl.pallas_call(adjoint_kernel, name='adjoint', in_specs=[apart] + [whole]...  4.31 us
    pallas_call x1, Pallas kernels, body(): pl.pallas_call(stress_kernel, name='stress', in_specs=[whole] * 7, out_sp...  3.31 us
    all_to_all x1, waiting for transfers between devices, body(): all_lse = lax.all_to_all(lse, 'tm', 0, 0, tiled=True)  2.32 us
    ppermute x4, waiting for transfers between devices, scan_devices(): got = lax.ppermute(sent, 'tm', pairs)  1.45 us
  transfers between devices with their start and end apart: 5, of which 3 were waited for; matrix products, arithmetic and copies ran while one was open for 0% of the time, Pallas kernels for 37%

profile of v3, /device:TPU:0, one launch (start us, length us, event | category | flops | bytes accessed | tf_op | source)
XLA Modules:
  0.0 42.0 jit_solution(16866261538569891957)
XLA Ops:
  0.6 4.4 %totals.1 = (bf16[3072,512]{1,0:T(8,128)(2,1)S(1)}, f32[768,512]{1,0:T(8,128)S(1)}, bf16[768,512]{1,0:T(8,128)(2,1)S(1)}, f32[768,128]{1,0:T(8,128)S(1)}, f32[9,32,128]{2,1,0:T(8,128)S(1)}) custom-call(f32[32,3072]{1,0:T(8,128)} %heat_ref.5, f32[1,32]{1,0:T(1,128)} %bitcast.29, f32[1,32]{1,0:T(1,128)} %bitcast.33, bf16[3072,512]{1,0:T(8,128)(2,1)} %cur_hbm.1, ...), custom_call_target="tpu_custom_call" | custom-call | flops 201326592 | bytes 14680064 | tf_op jit(solution)/shard_map/totals/pallas_call | solution.py:396
  5.1 0.5 %collective-permute-start = (f32[9,32,128]{2,1,0:T(8,128)S(1)}, f32[9,32,128]{2,1,0:T(8,128)S(1)}, u32[]{:S(2)}, u32[]{:S(2)}) collective-permute-start(f32[9,32,128]{2,1,0:T(8,128)S(1)} %get-tuple-element.63), channel_id=1, source_target_pairs={{0,1},{1,0},{2,3},{3,2},{4,5},{5,4},{6,7},{7,6},{8,9},{9,8},{10,11... | collective-permute-start | bytes 442376 | tf_op jit(solution)/shard_map/ppermute | solution.py:315
  5.6 1.0 %collective-permute-done = f32[9,32,128]{2,1,0:T(8,128)S(1)} collective-permute-done((f32[9,32,128]{2,1,0:T(8,128)S(1)}, f32[9,32,128]{2,1,0:T(8,128)S(1)}, u32[]{:S(2)}, u32[]{:S(2)}) %collective-permute-start) | collective-permute-done | bytes 147488 | tf_op jit(solution)/shard_map/ppermute | solution.py:315
  6.7 2.9 %collective-permute-start.1 = (f32[9,32,128]{2,1,0:T(8,128)S(1)}, f32[9,32,128]{2,1,0:T(8,128)S(1)}, u32[]{:S(2)}, u32[]{:S(2)}) collective-permute-start(f32[9,32,128]{2,1,0:T(8,128)S(1)} %pad_maximum_fusion), channel_id=1, source_target_pairs={{0,2},{1,3},{2,0},{3,1},{4,6},{5,7},{6,4},{7,5},{8,10},{9,11},{10,... | collective-permute-start | bytes 442376 | tf_op jit(solution)/shard_map/ppermute | solution.py:315
  9.6 3.7 %kernels.3 = (bf16[3072,128]{1,0:T(8,128)(2,1)S(1)}, bf16[3072,128]{1,0:T(8,128)(2,1)S(1)}, bf16[3072,128]{1,0:T(8,128)(2,1)S(1)}) custom-call(f32[32,3072]{1,0:T(8,128)} %heat_ref.5, f32[1,32]{1,0:T(1,128)} %bitcast.30, f32[1,32]{1,0:T(1,128)} %bitcast.34), custom_call_target="tpu_custom_call" | custom-call | flops 335544320 | bytes 8388608 | tf_op jit(solution)/shard_map/kernels/pallas_call | solution.py:355
  13.4 0.4 %collective-permute-done.1 = f32[9,32,128]{2,1,0:T(8,128)S(1)} collective-permute-done((f32[9,32,128]{2,1,0:T(8,128)S(1)}, f32[9,32,128]{2,1,0:T(8,128)S(1)}, u32[]{:S(2)}, u32[]{:S(2)}) %collective-permute-start.1) | collective-permute-done | bytes 147488 | tf_op jit(solution)/shard_map/ppermute | solution.py:315
  13.9 0.0 copy-start
  13.9 1.9 %collective-permute-start.2 = (f32[9,32,128]{2,1,0:T(8,128)S(1)}, f32[9,32,128]{2,1,0:T(8,128)S(1)}, u32[]{:S(2)}, u32[]{:S(2)}) collective-permute-start(f32[9,32,128]{2,1,0:T(8,128)S(1)} %pad_maximum_fusion.1), channel_id=1, source_target_pairs={{0,4},{1,5},{2,6},{3,7},{4,0},{5,1},{6,2},{7,3},{8,12},{9,13},{10,... | collective-permute-start | bytes 442376 | tf_op jit(solution)/shard_map/ppermute | solution.py:315
  15.8 3.7 %kernels.4 = (bf16[3072,128]{1,0:T(8,128)(2,1)S(1)}, bf16[3072,128]{1,0:T(8,128)(2,1)S(1)}, bf16[3072,128]{1,0:T(8,128)(2,1)S(1)}) custom-call(f32[32,3072]{1,0:T(8,128)} %heat_ref.5, f32[1,32]{1,0:T(1,128)} %bitcast.31, f32[1,32]{1,0:T(1,128)} %bitcast.35, ...), custom_call_target="tpu_custom_call", output_to_operand_aliasing={{0}: (3, {}), {1}: (4, {}), {2}: (5, {})} | custom-call | flops 335544320 | bytes 8388608 | tf_op jit(solution)/shard_map/kernels/pallas_call | solution.py:355
  19.5 0.0 collective-permute-done.2
  19.6 2.6 %collective-permute-start.3 = (f32[4,32,128]{2,1,0:T(8,128)S(1)}, f32[4,32,128]{2,1,0:T(8,128)S(1)}, u32[]{:S(2)}, u32[]{:S(2)}) collective-permute-start(f32[4,32,128]{2,1,0:T(8,128)S(1)} %slice_select_fusion), channel_id=1, source_target_pairs={{0,8},{1,9},{2,10},{3,11},{4,12},{5,13},{6,14},{7,15},{8,0},{9,1},... | collective-permute-start | bytes 196616 | tf_op jit(solution)/shard_map/ppermute | solution.py:315
  22.2 3.7 %kernels.5 = (bf16[3072,128]{1,0:T(8,128)(2,1)S(1)}, bf16[3072,128]{1,0:T(8,128)(2,1)S(1)}, bf16[3072,128]{1,0:T(8,128)(2,1)S(1)}) custom-call(f32[32,3072]{1,0:T(8,128)} %heat_ref.5, f32[1,32]{1,0:T(1,128)} %bitcast.32, f32[1,32]{1,0:T(1,128)} %bitcast.36, ...), custom_call_target="tpu_custom_call", output_to_operand_aliasing={{0}: (3, {}), {1}: (4, {}), {2}: (5, {})} | custom-call | flops 335544320 | bytes 8388608 | tf_op jit(solution)/shard_map/kernels/pallas_call | solution.py:355
  26.0 0.0 collective-permute-done.3
  26.0 0.0 copy-done
  26.0 3.3 %stress.1 = (bf16[3072,512]{1,0:T(8,128)(2,1)}, f32[16,1,512]{2,1,0:T(1,128)}) custom-call(bf16[3072,512]{1,0:T(8,128)(2,1)S(1)} %get-tuple-element.58.cur_ref, bf16[3072,128]{1,0:T(8,128)(2,1)S(1)} %get-tuple-element.98.kf_ref, bf16[3072,128]{1,0:T(8,128)(2,1)S(1)} %get-tuple-element.99.aux_ref, f32[768,512]{1,0:T(8,128)S(1)} %get-tuple-element.100.fresh_ref, ...), custom_call_target="tpu_custom_call" | custom-call | flops 805306368 | bytes 10485760 | tf_op jit(solution)/shard_map/stress/pallas_call | solution.py:436
  29.3 5.3 %all-to-all-start = ((f32[16,1,512]{2,1,0:T(1,128)}), f32[16,1,512]{2,1,0:T(1,128)S(1)}, u32[]{:S(2)}, u32[]{:S(2)}) async-start(f32[16,1,512]{2,1,0:T(1,128)} %get-tuple-element.110), calls=%async_computation | async-start | bytes 65536 | tf_op jit(solution)/shard_map/all_to_all | solution.py:452
  34.7 4.3 %adjoint.1 = bf16[3072,512]{1,0:T(8,128)(2,1)} custom-call(bf16[3072,512]{1,0:T(8,128)(2,1)} %cot_hbm.3, bf16[3072,128]{1,0:T(8,128)(2,1)S(1)} %get-tuple-element.106.ka_ref, bf16[3072,128]{1,0:T(8,128)(2,1)S(1)} %get-tuple-element.99.aux_ref, bf16[768,512]{1,0:T(8,128)(2,1)S(1)} %get-tuple-element.107.fresh_ref, ...), custom_call_target="tpu_custom_call" | custom-call | flops 805306368 | bytes 10485760 | tf_op jit(solution)/shard_map/adjoint/pallas_call | solution.py:454
  39.0 2.3 %all-to-all-done = f32[16,1,512]{2,1,0:T(1,128)S(1)} async-done(((f32[16,1,512]{2,1,0:T(1,128)}), f32[16,1,512]{2,1,0:T(1,128)S(1)}, u32[]{:S(2)}, u32[]{:S(2)}) %all-to-all-start) | async-done | bytes 32800 | tf_op jit(solution)/shard_map/all_to_all | solution.py:452
  41.3 0.1 exponential_reduce_fusion
  41.4 0.6 %add_multiply_fusion = f32[512]{0:T(512)} fusion(f32[512]{0:T(512)S(1)} %exponential_reduce_fusion, f32[512]{0:T(512)S(1)} %reduce_max.9), kind=kLoop, calls=%fused_computation.34 | loop fusion | flops 1536 | bytes 6144 | tf_op jit(solution)/shard_map/div | solution.py:477
  (12 shorter events, 0.3 us)
Async XLA Ops:
  5.1 1.5 %collective-permute-start = (f32[9,32,128]{2,1,0:T(8,128)S(1)}, f32[9,32,128]{2,1,0:T(8,128)S(1)}, u32[]{:S(2)}, u32[]{:S(2)}) collective-permute-start(f32[9,32,128]{2,1,0:T(8,128)S(1)} %get-tuple-element.63), channel_id=1, source_target_pairs={{0,1},{1,0},{2,3},{3,2},{4,5},{5,4},{6,7},{7,6},{8,9},{9,8},{10,11... | collective-permute-start | bytes 442376 | tf_op jit(solution)/shard_map/ppermute | solution.py:315
  6.7 7.1 %collective-permute-start.1 = (f32[9,32,128]{2,1,0:T(8,128)S(1)}, f32[9,32,128]{2,1,0:T(8,128)S(1)}, u32[]{:S(2)}, u32[]{:S(2)}) collective-permute-start(f32[9,32,128]{2,1,0:T(8,128)S(1)} %pad_maximum_fusion), channel_id=1, source_target_pairs={{0,2},{1,3},{2,0},{3,1},{4,6},{5,7},{6,4},{7,5},{8,10},{9,11},{10,... | collective-permute-start | bytes 442376 | tf_op jit(solution)/shard_map/ppermute | solution.py:315
  13.9 12.1 %copy-start = (s32[512]{0:T(512)S(1)}, s32[512]{0:T(512)}, u32[]{:S(2)}) copy-start(s32[512]{0:T(512)} %param.11) | copy-start | bytes 6148
  13.9 5.6 %collective-permute-start.2 = (f32[9,32,128]{2,1,0:T(8,128)S(1)}, f32[9,32,128]{2,1,0:T(8,128)S(1)}, u32[]{:S(2)}, u32[]{:S(2)}) collective-permute-start(f32[9,32,128]{2,1,0:T(8,128)S(1)} %pad_maximum_fusion.1), channel_id=1, source_target_pairs={{0,4},{1,5},{2,6},{3,7},{4,0},{5,1},{6,2},{7,3},{8,12},{9,13},{10,... | collective-permute-start | bytes 442376 | tf_op jit(solution)/shard_map/ppermute | solution.py:315
  19.6 6.4 %collective-permute-start.3 = (f32[4,32,128]{2,1,0:T(8,128)S(1)}, f32[4,32,128]{2,1,0:T(8,128)S(1)}, u32[]{:S(2)}, u32[]{:S(2)}) collective-permute-start(f32[4,32,128]{2,1,0:T(8,128)S(1)} %slice_select_fusion), channel_id=1, source_target_pairs={{0,8},{1,9},{2,10},{3,11},{4,12},{5,13},{6,14},{7,15},{8,0},{9,1},... | collective-permute-start | bytes 196616 | tf_op jit(solution)/shard_map/ppermute | solution.py:315
  29.3 12.0 %all-to-all-start = ((f32[16,1,512]{2,1,0:T(1,128)}), f32[16,1,512]{2,1,0:T(1,128)S(1)}, u32[]{:S(2)}, u32[]{:S(2)}) async-start(f32[16,1,512]{2,1,0:T(1,128)} %get-tuple-element.110), calls=%async_computation | async-start | bytes 65536 | tf_op jit(solution)/shard_map/all_to_all | solution.py:452

commit v4 on v3

--- a/solution.py
+++ b/solution.py
@@ -30,22 +30,17 @@
     return rates * LOG2E, gains
 
 
-def doubling(heat, with_levels):
-    lane = lax.broadcasted_iota(jnp.int32, heat.shape, 1)
-    pre, suf = heat, jnp.zeros_like(heat)
+def level_sums():
+    v = lax.broadcasted_iota(jnp.int32, (CHUNK, CHUNK), 0)
+    u = lax.broadcasted_iota(jnp.int32, (CHUNK, CHUNK), 1)
+    apart = v ^ u
     tables = []
     for level in range(LEVELS):
         half = 1 << level
-        second = (lane & half) != 0
-        if with_levels:
-            tables.append(jnp.exp2(-jnp.where(second, pre, suf)))
-        total = pre + suf
-        sibling = jnp.where(
-            second, pltpu.roll(total, half, 1), pltpu.roll(total, CHUNK - half, 1)
-        )
-        pre = jnp.where(second, pre + sibling, pre)
-        suf = jnp.where(second, suf, suf + sibling)
-    return pre, suf, tables
+        near = apart < half
+        inside = jnp.where((u & half) != 0, jnp.where(v <= u, -1.0, 0.0), jnp.where(v > u, -1.0, 0.0))
+        tables.append(jnp.where(near, inside, 0.0).astype(BF16))
+    return jnp.concatenate(tables, axis=1)
 
 
 def wide(a, times):
@@ -89,13 +84,14 @@
         jnp.concatenate([ones] * 3, axis=0),
         preferred_element_type=F32,
     )
-    return both[:, :CHUNK], both[:, CHUNK:]
+    return both[:, :CHUNK], both[:, CHUNK:], jnp.concatenate([high, middle], axis=1)
 
 
 def totals_kernel(
     heat_hbm, rates_hbm, fits_hbm, cur_hbm, cot_hbm,
     cur_ref, fresh_f_ref, fresh_a_ref, decay_ref, msg_ref,
-    cot_ref, heat_ref, rates_ref, fits_ref, start_ref, back_ref, small_sem, cur_sem, cot_sem,
+    split_ref, start_ref, back_ref, gains_ref, sums_ref,
+    cot_ref, heat_ref, rates_ref, fits_ref, small_sem, cur_sem, cot_sem,
 ):
     modes = heat_ref.shape[0]
     samples, wires = cur_ref.shape
@@ -122,14 +118,19 @@
             copy.start()
         loads.append((at, piece, pair))
         at += piece
+    sums_ref[...] = level_sums()
     for copy in small:
         copy.wait()
 
     speed, gains = rates_and_gains(rates_ref, fits_ref)
     gain_stack = jnp.concatenate([gains] * group, axis=0)
+    gains_ref[...] = jnp.broadcast_to(
+        jnp.concatenate([gains] * (CHUNK // modes), axis=0), gains_ref.shape
+    )
     for first in range(0, chunks, group):
         rows = slice(first * modes, (first + group) * modes)
-        pre, suf = prefixes(stacked(heat_ref, speed, first, group))
+        pre, suf, split = prefixes(stacked(heat_ref, speed, first, group))
+        split_ref[rows, :] = split
         start_ref[rows, :] = (gain_stack * jnp.exp2(-pre)).astype(BF16)
         back_ref[rows, :] = jnp.exp2(-suf).astype(BF16)
         decay_ref[rows, :] = jnp.exp2(-(pre + suf))
@@ -158,56 +159,67 @@
     msg_ref[2 * reps] = dc
 
 
-def kernels_kernel(heat_ref, rates_ref, fit_ref, *refs):
-    kf_ref, ka_ref, aux_ref = refs[-3:]
-    modes = heat_ref.shape[0]
-    chunks = heat_ref.shape[1] // CHUNK
-    group = group_of(chunks, 2)
-    speed, gains = rates_and_gains(rates_ref, fit_ref)
-    gain_sum = jnp.sum(gains, axis=0, keepdims=True)
+def kernels_kernel(modes, first, split_ref, gains_ref, sums_ref, kf_ref, ka_ref):
+    group = CHUNK // modes
     t = lax.broadcasted_iota(jnp.int32, (CHUNK, CHUNK), 0)
     s = lax.broadcasted_iota(jnp.int32, (CHUNK, CHUNK), 1)
     apart = jnp.where(t >= s, t ^ s, -1)
+    gains = gains_ref[...]
+    gain_sum = jnp.sum(gains[:modes], axis=0, keepdims=True)
     base = jnp.where(apart == 0, jnp.broadcast_to(gain_sum, (CHUNK, CHUNK)), 0.0)
-    zero = jnp.zeros((modes, CHUNK), BF16)
-    for first in range(0, chunks, group):
-        pres, sufs, stacks = doubling(stacked(heat_ref, speed, first, group), True)
+    for g in range(kf_ref.shape[0] // (CHUNK * group)):
+        rows = slice((first + g) * CHUNK, (first + g + 1) * CHUNK)
+        sums = jnp.dot(
+            split_ref[rows, :],
+            jnp.concatenate([sums_ref[...]] * 2, axis=0),
+            preferred_element_type=F32,
+        )
+        kernels = [base] * group
+        for level in range(LEVELS):
+            table = jnp.exp2(sums[:, level * CHUNK : (level + 1) * CHUNK])
+            left = (gains * table).astype(BF16).T
+            right = table.astype(BF16)
+            columns = []
+            for c in range(group):
+                parts = []
+                if c > 0:
+                    parts.append(jnp.zeros((c * modes, CHUNK), BF16))
+                parts.append(right[c * modes : (c + 1) * modes])
+                if c + 1 < group:
+                    parts.append(jnp.zeros(((group - 1 - c) * modes, CHUNK), BF16))
+                columns.append(jnp.concatenate(parts, axis=0))
+            both = jnp.dot(left, jnp.concatenate(columns, axis=1), preferred_element_type=F32)
+            keep = apart >= (1 << level)
+            kernels = [
+                jnp.where(keep, both[:, c * CHUNK : (c + 1) * CHUNK], kernels[c])
+                for c in range(group)
+            ]
         for c in range(group):
-            part = slice(c * modes, (c + 1) * modes)
-            span = slice((first + c) * CHUNK, (first + c + 1) * CHUNK)
-            pre, suf = pres[part], sufs[part]
-            tables = [e[part] for e in stacks]
-            left = [gains * e for e in tables]
-            right = [e.astype(BF16) for e in tables]
-            kernel = base
-            for lv in range(0, LEVELS - 1, 2):
-                lhs = jnp.concatenate([left[lv], left[lv + 1]], axis=0).T.astype(BF16)
-                rhs = jnp.concatenate(
-                    [
-                        jnp.concatenate([right[lv], zero], axis=1),
-                        jnp.concatenate([zero, right[lv + 1]], axis=1),
-                    ],
-                    axis=0,
-                )
-                both = jnp.dot(lhs, rhs, preferred_element_type=F32)
-                kernel = jnp.where(apart >= (1 << lv), both[:, :CHUNK], kernel)
-                kernel = jnp.where(apart >= (2 << lv), both[:, CHUNK:], kernel)
-            back = jnp.exp2(-suf)
-            aux = jnp.concatenate(
-                [gains * jnp.exp2(-pre), back, left[LEVELS - 1], back], axis=0
-            ).T.astype(BF16)
-            rhs = jnp.concatenate([zero, zero, right[LEVELS - 1], zero], axis=0)
-            last = jnp.dot(aux, rhs, preferred_element_type=F32)
-            kernel = jnp.where(apart >= (1 << (LEVELS - 1)), last, kernel)
-            kf_ref[span, :] = kernel.astype(BF16)
-            ka_ref[span, :] = kernel.T.astype(BF16)
-            aux_ref[span, :] = aux
+            span = slice((g * group + c) * CHUNK, (g * group + c + 1) * CHUNK)
+            kernel = kernels[c].astype(BF16)
+            kf_ref[span, :] = kernel
+            ka_ref[span, :] = kernel.T
+
+
+def carry(table, state):
+    return lax.dot_general(
+        table, state, (((0,), (0,)), ((), ())), preferred_element_type=F32
+    )
+
+
+def part_of(refs, c):
+    for ref in refs:
+        chunks = ref.shape[0] // CHUNK
+        if c < chunks:
+            return ref[c * CHUNK : (c + 1) * CHUNK, :]
+        c -= chunks
 
 
 def stress_kernel(
-    cur_ref, kf_ref, aux_ref, fresh_ref, decay_ref, in_ref, counts_ref,
-    out_hbm, lse_ref, out_ref, sem,
+    cur_ref, start_ref, fresh_ref, decay_ref, in_ref, counts_ref, *refs
 ):
+    kf_refs = refs[:-4]
+    out_hbm, lse_ref, out_ref, sem = refs[-4:]
     samples, wires = cur_ref.shape
     reps = wires // CHUNK
     modes = in_ref.shape[1]
@@ -222,9 +234,8 @@
         for c in range(first, first + piece):
             span = slice(c * CHUNK, (c + 1) * CHUNK)
             rows = slice(c * modes, (c + 1) * modes)
-            acc = jnp.dot(kf_ref[span, :], cur_ref[span, :], preferred_element_type=F32) + jnp.dot(
-                aux_ref[span, :modes], state.astype(BF16), preferred_element_type=F32
-            )
+            acc = jnp.dot(part_of(kf_refs, c), cur_ref[span, :], preferred_element_type=F32)
+            acc = acc + carry(start_ref[rows, :], state.astype(BF16))
             out_ref[span, :] = (acc * scale).astype(BF16)
             z = (acc * scale2).reshape(CHUNK // 8, 8, wires)
             new = jnp.maximum(high, jnp.max(z, axis=0))
@@ -245,15 +256,15 @@
 
 
 def adjoint_kernel(
-    cot_hbm, ka_ref, aux_ref, fresh_ref, decay_ref, in_ref, counts_ref,
-    out_hbm, cot_ref, out_ref, load_sem, sem,
+    cot_hbm, back_ref, fresh_ref, decay_ref, in_ref, counts_ref, *refs
 ):
+    ka_refs = refs[:-5]
+    out_hbm, cot_ref, out_ref, load_sem, sem = refs[-5:]
     samples, wires = cot_ref.shape
     reps = wires // CHUNK
     chunks = samples // CHUNK
     modes = in_ref.shape[1]
     scale = counts_ref[...].astype(F32) * 0.25
-    zero = jnp.zeros((modes, wires), BF16)
     state = jnp.concatenate([in_ref[k] for k in range(reps)], axis=1)
     loads = []
     end = chunks
@@ -270,10 +281,8 @@
         for c in reversed(range(end - piece, end)):
             span = slice(c * CHUNK, (c + 1) * CHUNK)
             rows = slice(c * modes, (c + 1) * modes)
-            carried = jnp.concatenate([zero, state.astype(BF16)], axis=0)
-            acc = jnp.dot(ka_ref[span, :], cot_ref[span, :], preferred_element_type=F32) + jnp.dot(
-                aux_ref[span, : 2 * modes], carried, preferred_element_type=F32
-            )
+            acc = jnp.dot(part_of(ka_refs, c), cot_ref[span, :], preferred_element_type=F32)
+            acc = acc + carry(back_ref[rows, :], state.astype(BF16))
             out_ref[span, :] = (acc * scale).astype(BF16)
             state = wide(decay_ref[rows, :], reps) * state + fresh_ref[rows, :].astype(F32)
         done = pl.ds((end - piece) * CHUNK, piece * CHUNK)
@@ -299,26 +308,53 @@
 
 def scan_devices(msg, uppers, reps, run_part, parts):
     n = lax.axis_size("tm")
-    before = jnp.zeros_like(msg[:reps])
-    after = jnp.zeros_like(msg[:reps])
-    d_before = jnp.ones_like(msg[2 * reps :])
-    d_after = jnp.ones_like(msg[2 * reps :])
+    half = reps // 2
     hops = hops_of(n)
+    late = uppers[0]
+    pairs = [(i, i ^ 1) for i in range(n)]
+
+    low_f, high_f = msg[:half], msg[half:reps]
+    low_a, high_a = msg[reps : reps + half], msg[reps + half : 2 * reps]
+    mine_d = msg[2 * reps :]
+    sent = jnp.concatenate(
+        [jnp.where(late, low_f, high_f), jnp.where(late, low_a, high_a), mine_d], axis=0
+    )
+    mine_f, mine_a = jnp.where(late, high_f, low_f), jnp.where(late, high_a, low_a)
+    got = lax.ppermute(sent, "tm", pairs)
+    got_f, got_a, got_d = got[:half], got[half : 2 * half], got[2 * half :]
+    first_f, last_a = jnp.where(late, got_f, mine_f), jnp.where(late, mine_a, got_a)
+    first_d, last_d = jnp.where(late, got_d, mine_d), jnp.where(late, mine_d, got_d)
+    msg = jnp.concatenate(
+        [
+            last_d * first_f + jnp.where(late, mine_f, got_f),
+            jnp.where(late, got_a, mine_a) + first_d * last_a,
+            mine_d * got_d,
+        ],
+        axis=0,
+    )
+    before = jnp.zeros_like(mine_f)
+    after = jnp.zeros_like(mine_f)
+    d_before = jnp.ones_like(mine_d)
+    d_after = jnp.ones_like(mine_d)
+    msg, first_f, last_a, first_d, last_d = lax.optimization_barrier(
+        (msg, first_f, last_a, first_d, last_d)
+    )
     for index, hop in enumerate(hops):
-        pairs = [(i, i ^ hop) for i in range(n)]
+        if index == 0:
+            continue
         upper = uppers[index]
-        mine_f, mine_a, mine_d = msg[:reps], msg[reps : 2 * reps], msg[2 * reps :]
+        mine_f, mine_a, mine_d = msg[:half], msg[half : 2 * half], msg[2 * half :]
         part = index - len(hops) + parts
         final = index == len(hops) - 1
         sent = jnp.where(upper, mine_a, mine_f) if final else msg
         sent = run_part.gate(part, sent)
-        got = lax.ppermute(sent, "tm", pairs)
+        got = lax.ppermute(sent, "tm", [(i, i ^ hop) for i in range(n)])
         got = run_part(part, got)
         if final:
             before = jnp.where(upper, d_before * got + before, before)
             after = jnp.where(upper, after, d_after * got + after)
         else:
-            got_f, got_a, got_d = got[:reps], got[reps : 2 * reps], got[2 * reps :]
+            got_f, got_a, got_d = got[:half], got[half : 2 * half], got[2 * half :]
             next_f = jnp.where(upper, mine_d * got_f + mine_f, got_d * mine_f + got_f)
             next_a = jnp.where(upper, got_d * mine_a + got_a, mine_d * got_a + mine_a)
             msg = jnp.concatenate([next_f, next_a, mine_d * got_d], axis=0)
@@ -329,50 +365,53 @@
             msg, before, after, d_before, d_after = lax.optimization_barrier(
                 (msg, before, after, d_before, d_after)
             )
+    second_f = first_d * before + first_f
+    first_a = last_d * after + last_a
+    mine_f, mine_a = jnp.where(late, second_f, before), jnp.where(late, after, first_a)
+    sent = jnp.concatenate(
+        [jnp.where(late, before, second_f), jnp.where(late, first_a, after)], axis=0
+    )
+    got = lax.ppermute(sent, "tm", pairs)
+    got_f, got_a = got[:half], got[half:]
+    before = jnp.concatenate(
+        [jnp.where(late, got_f, mine_f), jnp.where(late, mine_f, got_f)], axis=0
+    )
+    after = jnp.concatenate(
+        [jnp.where(late, got_a, mine_a), jnp.where(late, mine_a, got_a)], axis=0
+    )
     return before, after
 
 
 class KernelParts:
-    def __init__(self, heat, rates, fits, parts, params):
-        self.heat, self.rates, self.fits, self.parts = heat, rates, fits, parts
-        self.params, self.arrays = params, ()
+    def __init__(self, split, gains, sums, modes, counts, params):
+        self.split, self.gains, self.sums = split, gains, sums
+        self.modes, self.counts, self.params = modes, counts, params
+        self.kf, self.ka = [], []
 
     def gate(self, part, sent):
         if part >= 0:
-            sent, self.rates = lax.optimization_barrier((sent, self.rates))
+            sent, self.gains = lax.optimization_barrier((sent, self.gains))
         return sent
 
     def __call__(self, part, got):
         if part < 0:
             return got
-        modes, samples = self.heat.shape
-        length = samples // self.parts
-        inner = 2 if (length // CHUNK) % 2 == 0 else 1
-        block = length // inner
-        small = pl.BlockSpec((1, modes), lambda i: (0, 0))
-        rest = len(self.arrays)
-        self.arrays = tuple(
-            pl.pallas_call(
-                kernels_kernel,
-                name="kernels",
-                grid=(inner,),
-                in_specs=[
-                    pl.BlockSpec((modes, block), lambda i: (0, part * inner + i)),
-                    small,
-                    small,
-                ]
-                + [pl.BlockSpec(memory_space=pl.ANY)] * rest,
-                out_specs=[pl.BlockSpec((block, CHUNK), lambda i: (part * inner + i, 0))] * 3,
-                out_shape=[jax.ShapeDtypeStruct((samples, CHUNK), BF16)] * 3,
-                input_output_aliases={3 + k: k for k in range(rest)},
-                compiler_params=self.params,
-                cost_estimate=pl.CostEstimate(
-                    flops=20 * length * CHUNK * CHUNK, bytes_accessed=8 << 20, transcendentals=0
-                ),
-            )(on_hbm(self.heat), on_hbm(self.rates), on_hbm(self.fits), *self.arrays)
-        )
-        got, arrays = lax.optimization_barrier((got, self.arrays))
-        self.arrays = arrays
+        length = self.counts[part] * CHUNK * (CHUNK // self.modes)
+        whole = pl.BlockSpec(memory_space=pltpu.VMEM)
+        kf, ka = pl.pallas_call(
+            functools.partial(kernels_kernel, self.modes, sum(self.counts[:part])),
+            name="kernels",
+            in_specs=[whole] * 3,
+            out_specs=[whole] * 2,
+            out_shape=[pltpu.VMEM((length, CHUNK), BF16)] * 2,
+            compiler_params=self.params,
+            cost_estimate=pl.CostEstimate(
+                flops=20 * length * CHUNK * CHUNK, bytes_accessed=8 << 20, transcendentals=0
+            ),
+        )(on_vmem(self.split), on_vmem(self.gains), on_vmem(self.sums))
+        got, kf, ka = lax.optimization_barrier((got, kf, ka))
+        self.kf.append(kf)
+        self.ka.append(ka)
         return got
 
 
@@ -393,25 +432,28 @@
     flops = 2 * samples * wires
     copies = len(pieces_of(chunks))
 
-    cur, fresh_f, fresh_a, decay, msg = pl.pallas_call(
+    cur, fresh_f, fresh_a, decay, msg, split, start, back, gains, sums = pl.pallas_call(
         totals_kernel,
         name="totals",
         in_specs=[apart] * 5,
-        out_specs=[whole] * 5,
+        out_specs=[whole] * 10,
         out_shape=[
             pltpu.VMEM((samples, wires), BF16),
             pltpu.VMEM((chunks * modes, wires), F32),
             pltpu.VMEM((chunks * modes, wires), BF16),
             pltpu.VMEM((chunks * modes, CHUNK), F32),
             pltpu.VMEM((2 * reps + 1, modes, CHUNK), F32),
+            pltpu.VMEM((chunks * modes, 2 * CHUNK), BF16),
+            pltpu.VMEM((chunks * modes, CHUNK), BF16),
+            pltpu.VMEM((chunks * modes, CHUNK), BF16),
+            pltpu.VMEM((CHUNK, CHUNK), F32),
+            pltpu.VMEM((CHUNK, LEVELS * CHUNK), BF16),
         ],
         scratch_shapes=[
             pltpu.VMEM((samples, wires), BF16),
             pltpu.VMEM((modes, samples), F32),
             pltpu.VMEM((1, modes), F32),
             pltpu.VMEM((1, modes), F32),
-            pltpu.VMEM((chunks * modes, CHUNK), BF16),
-            pltpu.VMEM((chunks * modes, CHUNK), BF16),
             pltpu.SemaphoreType.DMA((3,)),
             pltpu.SemaphoreType.DMA((copies,)),
             pltpu.SemaphoreType.DMA((copies,)),
@@ -428,15 +470,16 @@
         on_hbm(seed_on_tension),
     )
 
-    parts = 3 if chunks % 3 == 0 else 1
-    covered = KernelParts(mode_diffusivity_factor, rates, fits, parts, params)
+    groups = chunks * modes // CHUNK
+    parts = 3
+    shares = [groups * (k + 1) // parts - groups * k // parts for k in range(parts)]
+    covered = KernelParts(split, gains, sums, modes, shares, params)
     before, after = scan_devices(msg, uppers, reps, covered, parts)
-    kf, ka, aux = covered.arrays
 
     tension, lse = pl.pallas_call(
         stress_kernel,
         name="stress",
-        in_specs=[whole] * 7,
+        in_specs=[whole] * (6 + parts),
         out_specs=[apart, whole],
         out_shape=[
             pltpu.HBM((samples, wires), BF16),
@@ -447,14 +490,14 @@
         cost_estimate=pl.CostEstimate(
             flops=2 * CHUNK * flops, bytes_accessed=10 << 20, transcendentals=0
         ),
-    )(*map(on_vmem, (cur, kf, aux, fresh_f, decay, before, counts)))
+    )(*map(on_vmem, (cur, start, fresh_f, decay, before, counts, *covered.kf)))
 
     all_lse = lax.all_to_all(lse, "tm", 0, 0, tiled=True)
 
     gradient = pl.pallas_call(
         adjoint_kernel,
         name="adjoint",
-        in_specs=[apart] + [whole] * 6,
+        in_specs=[apart] + [whole] * (5 + parts),
         out_specs=apart,
         out_shape=pltpu.HBM((samples, wires), BF16),
         scratch_shapes=[
@@ -469,7 +512,7 @@
         ),
     )(
         on_hbm(seed_on_tension),
-        *map(on_vmem, (ka, aux, fresh_a, decay, after, counts)),
+        *map(on_vmem, (back, fresh_a, decay, after, counts, *covered.ka)),
     )
 
     top = jnp.max(all_lse, axis=0)

time: 42.3 us -> 40.6 us (0.960)
  Pallas kernels: 23.2 us -> 15.7 us
  waiting for transfers between devices: 3.77 us -> 8.24 us
  starting transfers between devices: 13.3 us -> 14.7 us
    ppermute x0 -> x3, starting transfers between devices: none -> 7.68 us  [scan_devices(): got = lax.ppermute(sent, 'tm', [(i, i ^ hop) for i in range(n)])]
    pallas_call x4, Pallas kernels: 14.5 us -> 6.77 us  [the longest x3 3.41 us: __call__(): pl.pallas_call(functools.partial(kernels_kernel, self.modes, sum(self.cou...]
    ppermute x4 -> x2, starting transfers between devices: 7.97 us -> 0.59 us  [scan_devices(): got = lax.ppermute(sent, 'tm', pairs)]
    ppermute x0 -> x3, waiting for transfers between devices: none -> 3.96 us  [scan_devices(): got = lax.ppermute(sent, 'tm', [(i, i ^ hop) for i in range(n)])]
    all_to_all x1, starting transfers between devices: 5.32 us -> 6.42 us  [body(): all_lse = lax.all_to_all(lse, 'tm', 0, 0, tiled=True)]
    ppermute x4 -> x2, waiting for transfers between devices: 1.45 us -> 2.16 us  [scan_devices(): got = lax.ppermute(sent, 'tm', pairs)]
  transfers between devices with their start and end apart: 5 -> 6, of which waited for: 3 -> 6; matrix products, arithmetic and copies ran while one was open for 0% -> 0% of each run, Pallas kernels for 37% -> 20%
where the time goes in v4:
time: 40.6 us; the launch traced here: 40.4 us
  Pallas kernels  15.7 us (39%)
  starting transfers between devices  14.7 us (36%)
  waiting for transfers between devices  8.24 us (20%)
  other arithmetic  0.9 us (2%)
  between operations  0.83 us (2%)
    ppermute x3, starting transfers between devices, scan_devices(): got = lax.ppermute(sent, 'tm', [(i, i ^ hop) for i in range(n)])  7.68 us
    all_to_all x1, starting transfers between devices, body(): all_lse = lax.all_to_all(lse, 'tm', 0, 0, tiled=True)  6.42 us
    pallas_call x1, Pallas kernels, body(): pl.pallas_call(adjoint_kernel, name='adjoint', in_specs=[apart] + [whole]...  4.49 us
    pallas_call x1, Pallas kernels, body(): pl.pallas_call(totals_kernel, name='totals', in_specs=[apart] * 5, out_sp...  4.49 us
    ppermute x3, waiting for transfers between devices, scan_devices(): got = lax.ppermute(sent, 'tm', [(i, i ^ hop) for i in range(n)])  3.96 us
    pallas_call x3, Pallas kernels, __call__(): pl.pallas_call(functools.partial(kernels_kernel, self.modes, sum(self.cou...  3.41 us
    pallas_call x1, Pallas kernels, body(): pl.pallas_call(stress_kernel, name='stress', in_specs=[whole] * (6 + part...  3.36 us
    ppermute x2, waiting for transfers between devices, scan_devices(): got = lax.ppermute(sent, 'tm', pairs)  2.16 us
  transfers between devices with their start and end apart: 6, of which 6 were waited for; matrix products, arithmetic and copies ran while one was open for 0% of the time, Pallas kernels for 20%

profile of v4, /device:TPU:0, one launch (start us, length us, event | category | flops | bytes accessed | tf_op | source)
XLA Modules:
  0.0 40.4 jit_solution(14723729228041220378)
XLA Ops:
  0.6 4.5 %totals.1 = (bf16[3072,512]{1,0:T(8,128)(2,1)S(1)}, f32[768,512]{1,0:T(8,128)S(1)}, bf16[768,512]{1,0:T(8,128)(2,1)S(1)}, f32[768,128]{1,0:T(8,128)S(1)}, f32[9,...) custom-call(f32[32,3072]{1,0:T(8,128)} %heat_hbm.1, ...), custom_call_target="tpu_custom_call" | custom-call | flops 201326592 | bytes 14680064 | tf_op jit(solution)/shard_map/totals/pallas_call | solution.py:435
  5.2 0.5 %collective-permute-start = (f32[5,32,128]{2,1,0:T(8,128)S(1)}, f32[5,32,128]{2,1,0:T(8,128)S(1)}, u32[]{:S(2)}, u32[]{:S(2)}) collective-permute-start(f32[5,32,128]{2,1,0:T(8,128)S(1)} %pad_maximum_fusion), channel_id=1, source_target_pairs={{0,1},{1,0},{2,3},{3,2},{4,5},{5,4},{6,7},{7,6},{8,9},{9,8},{10,11... | collective-permute-start | bytes 245768 | tf_op jit(solution)/shard_map/ppermute | solution.py:323
  5.7 0.9 %collective-permute-done = f32[5,32,128]{2,1,0:T(8,128)S(1)} collective-permute-done((f32[5,32,128]{2,1,0:T(8,128)S(1)}, f32[5,32,128]{2,1,0:T(8,128)S(1)}, u32[]{:S(2)}, u32[]{:S(2)}) %collective-permute-start) | collective-permute-done | bytes 81952 | tf_op jit(solution)/shard_map/ppermute | solution.py:323
  6.7 0.0 copy-start
  6.7 2.9 %collective-permute-start.1 = (f32[5,32,128]{2,1,0:T(8,128)S(1)}, f32[5,32,128]{2,1,0:T(8,128)S(1)}, u32[]{:S(2)}, u32[]{:S(2)}) collective-permute-start(f32[5,32,128]{2,1,0:T(8,128)S(1)} %pad_maximum_fusion.1), channel_id=1, source_target_pairs={{0,2},{1,3},{2,0},{3,1},{4,6},{5,7},{6,4},{7,5},{8,10},{9,11},{10,... | collective-permute-start | bytes 245768 | tf_op jit(solution)/shard_map/ppermute | solution.py:351
  9.6 1.1 %kernels.3 = (bf16[1024,128]{1,0:T(8,128)(2,1)S(1)}, bf16[1024,128]{1,0:T(8,128)(2,1)S(1)}) custom-call(bf16[768,256]{1,0:T(8,128)(2,1)S(1)} %get-tuple-element.69.split_ref, f32[128,128]{1,0:T(8,128)S(1)} %get-tuple-element.88.gains_ref, bf16[128,896]{1,0:T(8,128)(2,1)S(1)} %get-tuple-element.71.sums_ref), custom_call_target="tpu_custom_call" | custom-call | flops 335544320 | bytes 8388608 | tf_op jit(solution)/shard_map/kernels/pallas_call | solution.py:401
  10.8 1.6 %collective-permute-done.1 = f32[5,32,128]{2,1,0:T(8,128)S(1)} collective-permute-done((f32[5,32,128]{2,1,0:T(8,128)S(1)}, f32[5,32,128]{2,1,0:T(8,128)S(1)}, u32[]{:S(2)}, u32[]{:S(2)}) %collective-permute-start.1) | collective-permute-done | bytes 81952 | tf_op jit(solution)/shard_map/ppermute | solution.py:351
  12.4 1.9 %collective-permute-start.2 = (f32[5,32,128]{2,1,0:T(8,128)S(1)}, f32[5,32,128]{2,1,0:T(8,128)S(1)}, u32[]{:S(2)}, u32[]{:S(2)}) collective-permute-start(f32[5,32,128]{2,1,0:T(8,128)S(1)} %pad_maximum_fusion.2), channel_id=1, source_target_pairs={{0,4},{1,5},{2,6},{3,7},{4,0},{5,1},{6,2},{7,3},{8,12},{9,13},{10,... | collective-permute-start | bytes 245768 | tf_op jit(solution)/shard_map/ppermute | solution.py:351
  14.3 1.1 %kernels.4 = (bf16[1024,128]{1,0:T(8,128)(2,1)S(1)}, bf16[1024,128]{1,0:T(8,128)(2,1)S(1)}) custom-call(bf16[768,256]{1,0:T(8,128)(2,1)S(1)} %get-tuple-element.69.split_ref, f32[128,128]{1,0:T(8,128)S(1)} %get-tuple-element.88.gains_ref, bf16[128,896]{1,0:T(8,128)(2,1)S(1)} %get-tuple-element.71.sums_ref), custom_call_target="tpu_custom_call" | custom-call | flops 335544320 | bytes 8388608 | tf_op jit(solution)/shard_map/kernels/pallas_call | solution.py:401
  15.4 1.5 %collective-permute-done.2 = f32[5,32,128]{2,1,0:T(8,128)S(1)} collective-permute-done((f32[5,32,128]{2,1,0:T(8,128)S(1)}, f32[5,32,128]{2,1,0:T(8,128)S(1)}, u32[]{:S(2)}, u32[]{:S(2)}) %collective-permute-start.2) | collective-permute-done | bytes 81952 | tf_op jit(solution)/shard_map/ppermute | solution.py:351
  17.0 2.9 %collective-permute-start.3 = (f32[2,32,128]{2,1,0:T(8,128)S(1)}, f32[2,32,128]{2,1,0:T(8,128)S(1)}, u32[]{:S(2)}, u32[]{:S(2)}) collective-permute-start(f32[2,32,128]{2,1,0:T(8,128)S(1)} %slice_select_fusion), channel_id=1, source_target_pairs={{0,8},{1,9},{2,10},{3,11},{4,12},{5,13},{6,14},{7,15},{8,0},{9,1},... | collective-permute-start | bytes 98312 | tf_op jit(solution)/shard_map/ppermute | solution.py:351
  19.9 1.1 %kernels.5 = (bf16[1024,128]{1,0:T(8,128)(2,1)S(1)}, bf16[1024,128]{1,0:T(8,128)(2,1)S(1)}) custom-call(bf16[768,256]{1,0:T(8,128)(2,1)S(1)} %get-tuple-element.69.split_ref, f32[128,128]{1,0:T(8,128)S(1)} %get-tuple-element.88.gains_ref, bf16[128,896]{1,0:T(8,128)(2,1)S(1)} %get-tuple-element.71.sums_ref), custom_call_target="tpu_custom_call" | custom-call | flops 335544320 | bytes 8388608 | tf_op jit(solution)/shard_map/kernels/pallas_call | solution.py:401
  21.0 0.9 %collective-permute-done.3 = f32[2,32,128]{2,1,0:T(8,128)S(1)} collective-permute-done((f32[2,32,128]{2,1,0:T(8,128)S(1)}, f32[2,32,128]{2,1,0:T(8,128)S(1)}, u32[]{:S(2)}, u32[]{:S(2)}) %collective-permute-start.3) | collective-permute-done | bytes 32800 | tf_op jit(solution)/shard_map/ppermute | solution.py:351
  21.9 0.1 collective-permute-start.4
  22.0 1.2 %collective-permute-done.4 = f32[4,32,128]{2,1,0:T(8,128)S(1)} collective-permute-done((f32[4,32,128]{2,1,0:T(8,128)S(1)}, f32[4,32,128]{2,1,0:T(8,128)S(1)}, u32[]{:S(2)}, u32[]{:S(2)}) %collective-permute-start.4) | collective-permute-done | bytes 65568 | tf_op jit(solution)/shard_map/ppermute | solution.py:374
  23.3 0.0 copy-done
  23.3 3.4 %stress.1 = (bf16[3072,512]{1,0:T(8,128)(2,1)}, f32[16,1,512]{2,1,0:T(1,128)}) custom-call(bf16[3072,512]{1,0:T(8,128)(2,1)S(1)} %get-tuple-element.57.cur_ref, bf16[768,128]{1,0:T(8,128)(2,1)S(1)} %get-tuple-element.58.start_ref, f32[768,512]{1,0:T(8,128)S(1)} %get-tuple-element.59.fresh_ref, f32[768,128]{1,0:T(8,128)S(1)} %get-tuple-element.60.decay_ref, ...), custom_call_target="tpu_custom_call" | custom-call | flops 805306368 | bytes 10485760 | tf_op jit(solution)/shard_map/stress/pallas_call | solution.py:479
  26.7 6.4 %all-to-all-start = ((f32[16,1,512]{2,1,0:T(1,128)}), f32[16,1,512]{2,1,0:T(1,128)S(1)}, u32[]{:S(2)}, u32[]{:S(2)}) async-start(f32[16,1,512]{2,1,0:T(1,128)} %get-tuple-element.108), calls=%async_computation | async-start | bytes 65536 | tf_op jit(solution)/shard_map/all_to_all | solution.py:495
  33.1 4.5 %adjoint.1 = bf16[3072,512]{1,0:T(8,128)(2,1)} custom-call(bf16[3072,512]{1,0:T(8,128)(2,1)} %cot_hbm.3, bf16[768,128]{1,0:T(8,128)(2,1)S(1)} %get-tuple-element.103.back_ref, bf16[768,512]{1,0:T(8,128)(2,1)S(1)} %get-tuple-element.104.fresh_ref, f32[768,128]{1,0:T(8,128)S(1)} %get-tuple-element.60.decay_ref, f32[4,32,128]{2,1,0:T(8,128)S(1)} %pad_maximum_fusion.6.in_ref, ...), custom_call_target="tpu_custom_call" | custom-call | flops 805306368 | bytes 10485760 | tf_op jit(solution)/shard_map/adjoint/pallas_call | solution.py:497
  37.6 2.1 %all-to-all-done = f32[16,1,512]{2,1,0:T(1,128)S(1)} async-done(((f32[16,1,512]{2,1,0:T(1,128)}), f32[16,1,512]{2,1,0:T(1,128)S(1)}, u32[]{:S(2)}, u32[]{:S(2)}) %all-to-all-start) | async-done | bytes 32800 | tf_op jit(solution)/shard_map/all_to_all | solution.py:495
  39.8 0.1 exponential_reduce_fusion
  39.8 0.6 %add_multiply_fusion = f32[512]{0:T(512)} fusion(f32[512]{0:T(512)S(1)} %exponential_reduce_fusion, f32[512]{0:T(512)S(1)} %reduce_max.9), kind=kLoop, calls=%fused_computation.50 | loop fusion | flops 1536 | bytes 6144 | tf_op jit(solution)/shard_map/div | solution.py:520
  (19 shorter events, 0.2 us)
Async XLA Ops:
  5.2 1.4 %collective-permute-start = (f32[5,32,128]{2,1,0:T(8,128)S(1)}, f32[5,32,128]{2,1,0:T(8,128)S(1)}, u32[]{:S(2)}, u32[]{:S(2)}) collective-permute-start(f32[5,32,128]{2,1,0:T(8,128)S(1)} %pad_maximum_fusion), channel_id=1, source_target_pairs={{0,1},{1,0},{2,3},{3,2},{4,5},{5,4},{6,7},{7,6},{8,9},{9,8},{10,11... | collective-permute-start | bytes 245768 | tf_op jit(solution)/shard_map/ppermute | solution.py:323
  6.7 16.6 %copy-start = (s32[512]{0:T(512)S(1)}, s32[512]{0:T(512)}, u32[]{:S(2)}) copy-start(s32[512]{0:T(512)} %param.11) | copy-start | bytes 6148
  6.7 5.7 %collective-permute-start.1 = (f32[5,32,128]{2,1,0:T(8,128)S(1)}, f32[5,32,128]{2,1,0:T(8,128)S(1)}, u32[]{:S(2)}, u32[]{:S(2)}) collective-permute-start(f32[5,32,128]{2,1,0:T(8,128)S(1)} %pad_maximum_fusion.1), channel_id=1, source_target_pairs={{0,2},{1,3},{2,0},{3,1},{4,6},{5,7},{6,4},{7,5},{8,10},{9,11},{10,... | collective-permute-start | bytes 245768 | tf_op jit(solution)/shard_map/ppermute | solution.py:351
  12.4 4.5 %collective-permute-start.2 = (f32[5,32,128]{2,1,0:T(8,128)S(1)}, f32[5,32,128]{2,1,0:T(8,128)S(1)}, u32[]{:S(2)}, u32[]{:S(2)}) collective-permute-start(f32[5,32,128]{2,1,0:T(8,128)S(1)} %pad_maximum_fusion.2), channel_id=1, source_target_pairs={{0,4},{1,5},{2,6},{3,7},{4,0},{5,1},{6,2},{7,3},{8,12},{9,13},{10,... | collective-permute-start | bytes 245768 | tf_op jit(solution)/shard_map/ppermute | solution.py:351
  17.0 4.9 %collective-permute-start.3 = (f32[2,32,128]{2,1,0:T(8,128)S(1)}, f32[2,32,128]{2,1,0:T(8,128)S(1)}, u32[]{:S(2)}, u32[]{:S(2)}) collective-permute-start(f32[2,32,128]{2,1,0:T(8,128)S(1)} %slice_select_fusion), channel_id=1, source_target_pairs={{0,8},{1,9},{2,10},{3,11},{4,12},{5,13},{6,14},{7,15},{8,0},{9,1},... | collective-permute-start | bytes 98312 | tf_op jit(solution)/shard_map/ppermute | solution.py:351
  21.9 1.3 %collective-permute-start.4 = (f32[4,32,128]{2,1,0:T(8,128)S(1)}, f32[4,32,128]{2,1,0:T(8,128)S(1)}, u32[]{:S(2)}, u32[]{:S(2)}) collective-permute-start(f32[4,32,128]{2,1,0:T(8,128)S(1)} %pad_maximum_fusion.4), channel_id=1, source_target_pairs={{0,1},{1,0},{2,3},{3,2},{4,5},{5,4},{6,7},{7,6},{8,9},{9,8},{10,11... | collective-permute-start | bytes 196616 | tf_op jit(solution)/shard_map/ppermute | solution.py:374
  26.7 13.1 %all-to-all-start = ((f32[16,1,512]{2,1,0:T(1,128)}), f32[16,1,512]{2,1,0:T(1,128)S(1)}, u32[]{:S(2)}, u32[]{:S(2)}) async-start(f32[16,1,512]{2,1,0:T(1,128)} %get-tuple-element.108), calls=%async_computation | async-start | bytes 65536 | tf_op jit(solution)/shard_map/all_to_all | solution.py:495

commit v5 on v4

--- a/solution.py
+++ b/solution.py
@@ -215,11 +215,18 @@
         c -= chunks
 
 
+def stress_pieces(chunks):
+    if chunks % 8:
+        return [1] * chunks
+    unit = chunks // 8
+    return [2 * unit, 2 * unit, unit, unit, 2 * unit]
+
+
 def stress_kernel(
     cur_ref, start_ref, fresh_ref, decay_ref, in_ref, counts_ref, *refs
 ):
-    kf_refs = refs[:-4]
-    out_hbm, lse_ref, out_ref, sem = refs[-4:]
+    kf_refs = refs[:-5]
+    out_hbm, tail_ref, lse_ref, out_ref, sem = refs[-5:]
     samples, wires = cur_ref.shape
     reps = wires // CHUNK
     modes = in_ref.shape[1]
@@ -230,22 +237,29 @@
     amount = jnp.zeros((8, wires), F32)
     stores = []
     first = 0
-    for k, piece in enumerate(pieces_of(samples // CHUNK)):
+    pieces = stress_pieces(samples // CHUNK)
+    for k, piece in enumerate(pieces):
+        last = k == len(pieces) - 1
         for c in range(first, first + piece):
             span = slice(c * CHUNK, (c + 1) * CHUNK)
             rows = slice(c * modes, (c + 1) * modes)
             acc = jnp.dot(part_of(kf_refs, c), cur_ref[span, :], preferred_element_type=F32)
             acc = acc + carry(start_ref[rows, :], state.astype(BF16))
-            out_ref[span, :] = (acc * scale).astype(BF16)
+            stress = (acc * scale).astype(BF16)
+            if last:
+                tail_ref[(c - first) * CHUNK : (c - first + 1) * CHUNK, :] = stress
+            else:
+                out_ref[span, :] = stress
             z = (acc * scale2).reshape(CHUNK // 8, 8, wires)
             new = jnp.maximum(high, jnp.max(z, axis=0))
             amount = amount * jnp.exp2(high - new) + jnp.sum(jnp.exp2(z - new[None]), axis=0)
             high = new
             state = wide(decay_ref[rows, :], reps) * state + fresh_ref[rows, :]
-        done = pl.ds(first * CHUNK, piece * CHUNK)
-        copy = pltpu.make_async_copy(out_ref.at[done], out_hbm.at[done], sem.at[k])
-        copy.start()
-        stores.append(copy)
+        if not last:
+            done = pl.ds(first * CHUNK, piece * CHUNK)
+            copy = pltpu.make_async_copy(out_ref.at[done], out_hbm.at[done], sem.at[k])
+            copy.start()
+            stores.append(copy)
         first += piece
     top = jnp.max(high, axis=0, keepdims=True)
     total = jnp.sum(amount * jnp.exp2(high - top), axis=0, keepdims=True)
@@ -256,10 +270,10 @@
 
 
 def adjoint_kernel(
-    cot_hbm, back_ref, fresh_ref, decay_ref, in_ref, counts_ref, *refs
+    cot_hbm, early_hbm, tail_ref, back_ref, fresh_ref, decay_ref, in_ref, counts_ref, *refs
 ):
-    ka_refs = refs[:-5]
-    out_hbm, cot_ref, out_ref, load_sem, sem = refs[-5:]
+    ka_refs = refs[:-7]
+    out_hbm, stress_hbm, cot_ref, out_ref, load_sem, sem, tail_sem = refs[-7:]
     samples, wires = cot_ref.shape
     reps = wires // CHUNK
     chunks = samples // CHUNK
@@ -274,7 +288,10 @@
         copy.start()
         loads.append(copy)
         end -= piece
-    stores = []
+    tail = tail_ref.shape[0]
+    copy = pltpu.make_async_copy(tail_ref, stress_hbm.at[pl.ds(samples - tail, tail)], tail_sem)
+    copy.start()
+    stores = [copy]
     end = chunks
     for k, piece in enumerate(pieces_of(chunks)):
         loads[k].wait()
@@ -339,32 +356,49 @@
     msg, first_f, last_a, first_d, last_d = lax.optimization_barrier(
         (msg, first_f, last_a, first_d, last_d)
     )
-    for index, hop in enumerate(hops):
-        if index == 0:
-            continue
+    for index, hop in list(enumerate(hops))[1:-2]:
         upper = uppers[index]
         mine_f, mine_a, mine_d = msg[:half], msg[half : 2 * half], msg[2 * half :]
-        part = index - len(hops) + parts
-        final = index == len(hops) - 1
-        sent = jnp.where(upper, mine_a, mine_f) if final else msg
-        sent = run_part.gate(part, sent)
-        got = lax.ppermute(sent, "tm", [(i, i ^ hop) for i in range(n)])
+        part = index - len(hops) + 2 + parts - 1
+        msg = run_part.gate(part, msg)
+        got = lax.ppermute(msg, "tm", [(i, i ^ hop) for i in range(n)])
         got = run_part(part, got)
-        if final:
-            before = jnp.where(upper, d_before * got + before, before)
-            after = jnp.where(upper, after, d_after * got + after)
-        else:
-            got_f, got_a, got_d = got[:half], got[half : 2 * half], got[2 * half :]
-            next_f = jnp.where(upper, mine_d * got_f + mine_f, got_d * mine_f + got_f)
-            next_a = jnp.where(upper, got_d * mine_a + got_a, mine_d * got_a + mine_a)
-            msg = jnp.concatenate([next_f, next_a, mine_d * got_d], axis=0)
-            before = jnp.where(upper, d_before * got_f + before, before)
-            after = jnp.where(upper, after, d_after * got_a + after)
-            d_before = jnp.where(upper, d_before * got_d, d_before)
-            d_after = jnp.where(upper, d_after, d_after * got_d)
-            msg, before, after, d_before, d_after = lax.optimization_barrier(
-                (msg, before, after, d_before, d_after)
-            )
+        got_f, got_a, got_d = got[:half], got[half : 2 * half], got[2 * half :]
+        next_f = jnp.where(upper, mine_d * got_f + mine_f, got_d * mine_f + got_f)
+        next_a = jnp.where(upper, got_d * mine_a + got_a, mine_d * got_a + mine_a)
+        msg = jnp.concatenate([next_f, next_a, mine_d * got_d], axis=0)
+        before = jnp.where(upper, d_before * got_f + before, before)
+        after = jnp.where(upper, after, d_after * got_a + after)
+        d_before = jnp.where(upper, d_before * got_d, d_before)
+        d_after = jnp.where(upper, d_after, d_after * got_d)
+        msg, before, after, d_before, d_after = lax.optimization_barrier(
+            (msg, before, after, d_before, d_after)
+        )
+    near, far = uppers[-2], uppers[-1]
+    mine_f, mine_a, mine_d = msg[:half], msg[half : 2 * half], msg[2 * half :]
+    to_near = jnp.concatenate([jnp.where(near, mine_a, mine_f), mine_d], axis=0)
+    to_far = jnp.concatenate([jnp.where(far, mine_a, mine_f), mine_d], axis=0)
+    to_near, to_far = lax.optimization_barrier((to_near, to_far))
+    to_near = run_part.gate(parts - 1, to_near)
+    quarter = hops[-2]
+    got = [
+        lax.ppermute(sent, "tm", [(i, i ^ hop) for i in range(n)])
+        for sent, hop in ((to_far, 2 * quarter), (to_near, quarter), (to_far, 3 * quarter))
+    ]
+    got = run_part(parts - 1, tuple(got))
+    (x2, d2), (x1, d1), (x3, d3) = [(g[:half], g[half:]) for g in got]
+    others_f = jnp.where(
+        far,
+        jnp.where(near, (x3 * d2 + x2) * d1 + x1, d3 * x2 + x3),
+        jnp.where(near, x1, 0.0),
+    )
+    others_a = jnp.where(
+        far,
+        jnp.where(near, 0.0, x1),
+        jnp.where(near, x3 + d3 * x2, x1 + d1 * (x2 + d2 * x3)),
+    )
+    before = d_before * others_f + before
+    after = d_after * others_a + after
     second_f = first_d * before + first_f
     first_a = last_d * after + last_a
     mine_f, mine_a = jnp.where(late, second_f, before), jnp.where(late, after, first_a)
@@ -471,21 +505,23 @@
     )
 
     groups = chunks * modes // CHUNK
-    parts = 3
-    shares = [groups * (k + 1) // parts - groups * k // parts for k in range(parts)]
+    parts = 2
+    shares = [groups - groups // 3, groups // 3]
     covered = KernelParts(split, gains, sums, modes, shares, params)
     before, after = scan_devices(msg, uppers, reps, covered, parts)
 
-    tension, lse = pl.pallas_call(
+    pieces = stress_pieces(chunks)
+    early, tail, lse = pl.pallas_call(
         stress_kernel,
         name="stress",
         in_specs=[whole] * (6 + parts),
-        out_specs=[apart, whole],
+        out_specs=[apart, whole, whole],
         out_shape=[
             pltpu.HBM((samples, wires), BF16),
+            pltpu.VMEM((pieces[-1] * CHUNK, wires), BF16),
             pltpu.HBM((devices, 1, wires), F32),
         ],
-        scratch_shapes=[pltpu.VMEM((samples, wires), BF16), pltpu.SemaphoreType.DMA((copies,))],
+        scratch_shapes=[pltpu.VMEM((samples, wires), BF16), pltpu.SemaphoreType.DMA((len(pieces),))],
         compiler_params=params,
         cost_estimate=pl.CostEstimate(
             flops=2 * CHUNK * flops, bytes_accessed=10 << 20, transcendentals=0
@@ -494,17 +530,19 @@
 
     all_lse = lax.all_to_all(lse, "tm", 0, 0, tiled=True)
 
-    gradient = pl.pallas_call(
+    gradient, tension = pl.pallas_call(
         adjoint_kernel,
         name="adjoint",
-        in_specs=[apart] + [whole] * (5 + parts),
-        out_specs=apart,
-        out_shape=pltpu.HBM((samples, wires), BF16),
+        in_specs=[apart] * 2 + [whole] * (6 + parts),
+        out_specs=[apart] * 2,
+        out_shape=[pltpu.HBM((samples, wires), BF16)] * 2,
+        input_output_aliases={1: 1},
         scratch_shapes=[
             pltpu.VMEM((samples, wires), BF16),
             pltpu.VMEM((samples, wires), BF16),
             pltpu.SemaphoreType.DMA((copies,)),
             pltpu.SemaphoreType.DMA((copies,)),
+            pltpu.SemaphoreType.DMA,
         ],
         compiler_params=params,
         cost_estimate=pl.CostEstimate(
@@ -512,6 +550,8 @@
         ),
     )(
         on_hbm(seed_on_tension),
+        on_hbm(early),
+        on_vmem(tail),
         *map(on_vmem, (back, fresh_a, decay, after, counts, *covered.ka)),
     )
 

time: 40.6 us -> 38.2 us (0.941)
  starting transfers between devices: 14.7 us -> 11.9 us
  waiting for transfers between devices: 8.24 us -> 8.87 us
    all_to_all x1, starting transfers between devices: 6.42 us -> 3.96 us  [body(): all_lse = lax.all_to_all(lse, 'tm', 0, 0, tiled=True)]
    ppermute x3 -> x4, waiting for transfers between devices: 3.96 us -> 4.91 us  [the longest x3 4.24 us: scan_devices(): lax.ppermute(sent, 'tm', [(i, i ^ hop) for i in range(n)])]
    pallas_call x1, Pallas kernels: 3.36 us -> 2.9 us  [body(): pl.pallas_call(stress_kernel, name='stress', in_specs=[whole] * (6 + part...]
    ppermute x3 -> x4, starting transfers between devices: 7.68 us -> 7.39 us  [the longest x3 4.46 us: scan_devices(): lax.ppermute(sent, 'tm', [(i, i ^ hop) for i in range(n)])]
    pallas_call x3 -> x2, Pallas kernels: 3.41 us -> 3.23 us  [__call__(): pl.pallas_call(functools.partial(kernels_kernel, self.modes, sum(self.cou...]
  transfers between devices with their start and end apart: 6 -> 7, of which waited for: 6 -> 6; matrix products, arithmetic and copies ran while one was open for 0% -> 0% of each run, Pallas kernels for 20% -> 21%
where the time goes in v5:
time: 38.2 us; the launch traced here: 38 us
  Pallas kernels  15.4 us (40%)
  starting transfers between devices  11.9 us (31%)
  waiting for transfers between devices  8.87 us (23%)
  other arithmetic  0.91 us (2%)
  between operations  0.84 us (2%)
    pallas_call x1, Pallas kernels, body(): pl.pallas_call(adjoint_kernel, name='adjoint', in_specs=[apart] * 2 + [wh...  4.81 us
    pallas_call x1, Pallas kernels, body(): pl.pallas_call(totals_kernel, name='totals', in_specs=[apart] * 5, out_sp...  4.49 us
    ppermute x3, starting transfers between devices, scan_devices(): lax.ppermute(sent, 'tm', [(i, i ^ hop) for i in range(n)])  4.46 us
    ppermute x3, waiting for transfers between devices, scan_devices(): lax.ppermute(sent, 'tm', [(i, i ^ hop) for i in range(n)])  4.24 us
    all_to_all x1, starting transfers between devices, body(): all_lse = lax.all_to_all(lse, 'tm', 0, 0, tiled=True)  3.96 us
    pallas_call x2, Pallas kernels, __call__(): pl.pallas_call(functools.partial(kernels_kernel, self.modes, sum(self.cou...  3.23 us
    ppermute x1, starting transfers between devices, scan_devices(): got = lax.ppermute(msg, 'tm', [(i, i ^ hop) for i in range(n)])  2.93 us
    pallas_call x1, Pallas kernels, body(): pl.pallas_call(stress_kernel, name='stress', in_specs=[whole] * (6 + part...  2.9 us
  transfers between devices with their start and end apart: 7, of which 6 were waited for; matrix products, arithmetic and copies ran while one was open for 0% of the time, Pallas kernels for 21%

profile of v5, /device:TPU:0, one launch (start us, length us, event | category | flops | bytes accessed | tf_op | source)
XLA Modules:
  0.0 38.0 jit_solution(15519782429816197694)
XLA Ops:
  0.6 4.5 %totals.1 = (bf16[3072,512]{1,0:T(8,128)(2,1)S(1)}, f32[768,512]{1,0:T(8,128)S(1)}, bf16[768,512]{1,0:T(8,128)(2,1)S(1)}, f32[768,128]{1,0:T(8,128)S(1)}, f32[9,...) custom-call(f32[32,3072]{1,0:T(8,128)} %heat_hbm.1, ...), custom_call_target="tpu_custom_call" | custom-call | flops 201326592 | bytes 14680064 | tf_op jit(solution)/shard_map/totals/pallas_call | solution.py:469
  5.2 0.5 %collective-permute-start = (f32[5,32,128]{2,1,0:T(8,128)S(1)}, f32[5,32,128]{2,1,0:T(8,128)S(1)}, u32[]{:S(2)}, u32[]{:S(2)}) collective-permute-start(f32[5,32,128]{2,1,0:T(8,128)S(1)} %pad_maximum_fusion), channel_id=1, source_target_pairs={{0,1},{1,0},{2,3},{3,2},{4,5},{5,4},{6,7},{7,6},{8,9},{9,8},{10,11... | collective-permute-start | bytes 245768 | tf_op jit(solution)/shard_map/ppermute | solution.py:340
  5.7 0.9 %collective-permute-done = f32[5,32,128]{2,1,0:T(8,128)S(1)} collective-permute-done((f32[5,32,128]{2,1,0:T(8,128)S(1)}, f32[5,32,128]{2,1,0:T(8,128)S(1)}, u32[]{:S(2)}, u32[]{:S(2)}) %collective-permute-start) | collective-permute-done | bytes 81952 | tf_op jit(solution)/shard_map/ppermute | solution.py:340
  6.7 0.0 copy-start
  6.7 2.9 %collective-permute-start.1 = (f32[5,32,128]{2,1,0:T(8,128)S(1)}, f32[5,32,128]{2,1,0:T(8,128)S(1)}, u32[]{:S(2)}, u32[]{:S(2)}) collective-permute-start(f32[5,32,128]{2,1,0:T(8,128)S(1)} %pad_maximum_fusion.1), channel_id=1, source_target_pairs={{0,2},{1,3},{2,0},{3,1},{4,6},{5,7},{6,4},{7,5},{8,10},{9,11},{10,... | collective-permute-start | bytes 245768 | tf_op jit(solution)/shard_map/ppermute | solution.py:364
  9.6 2.1 %kernels.2 = (bf16[2048,128]{1,0:T(8,128)(2,1)S(1)}, bf16[2048,128]{1,0:T(8,128)(2,1)S(1)}) custom-call(bf16[768,256]{1,0:T(8,128)(2,1)S(1)} %get-tuple-element.62.split_ref, f32[128,128]{1,0:T(8,128)S(1)} %get-tuple-element.75.gains_ref, bf16[128,896]{1,0:T(8,128)(2,1)S(1)} %get-tuple-element.64.sums_ref), custom_call_target="tpu_custom_call" | custom-call | flops 671088640 | bytes 8388608 | tf_op jit(solution)/shard_map/kernels/pallas_call | solution.py:435
  11.7 0.7 %collective-permute-done.1 = f32[5,32,128]{2,1,0:T(8,128)S(1)} collective-permute-done((f32[5,32,128]{2,1,0:T(8,128)S(1)}, f32[5,32,128]{2,1,0:T(8,128)S(1)}, u32[]{:S(2)}, u32[]{:S(2)}) %collective-permute-start.1) | collective-permute-done | bytes 81952 | tf_op jit(solution)/shard_map/ppermute | solution.py:364
  12.5 1.9 %collective-permute-start.3 = (f32[3,32,128]{2,1,0:T(8,128)S(1)}, f32[3,32,128]{2,1,0:T(8,128)S(1)}, u32[]{:S(2)}, u32[]{:S(2)}) collective-permute-start(f32[3,32,128]{2,1,0:T(8,128)S(1)} %get-tuple-element.74), channel_id=1, source_target_pairs={{0,4},{1,5},{2,6},{3,7},{4,0},{5,1},{6,2},{7,3},{8,12},{9,13},{10,... | collective-permute-start | bytes 147464 | tf_op jit(solution)/shard_map/ppermute | solution.py:385
  14.3 2.5 %collective-permute-start.4 = (f32[3,32,128]{2,1,0:T(8,128)S(1)}, f32[3,32,128]{2,1,0:T(8,128)S(1)}, u32[]{:S(2)}, u32[]{:S(2)}) collective-permute-start(f32[3,32,128]{2,1,0:T(8,128)S(1)} %get-tuple-element.72), channel_id=1, source_target_pairs={{0,12},{1,13},{2,14},{3,15},{4,8},{5,9},{6,10},{7,11},{8,4},{9,5},... | collective-permute-start | bytes 147464 | tf_op jit(solution)/shard_map/ppermute | solution.py:385
  16.8 0.1 collective-permute-start.2
  16.9 1.1 %kernels.3 = (bf16[1024,128]{1,0:T(8,128)(2,1)S(1)}, bf16[1024,128]{1,0:T(8,128)(2,1)S(1)}) custom-call(bf16[768,256]{1,0:T(8,128)(2,1)S(1)} %get-tuple-element.62.split_ref, f32[128,128]{1,0:T(8,128)S(1)} %get-tuple-element.75.gains_ref, bf16[128,896]{1,0:T(8,128)(2,1)S(1)} %get-tuple-element.64.sums_ref), custom_call_target="tpu_custom_call" | custom-call | flops 335544320 | bytes 8388608 | tf_op jit(solution)/shard_map/kernels/pallas_call | solution.py:435
  18.1 0.0 collective-permute-done.3
  18.1 2.3 %collective-permute-done.4 = f32[3,32,128]{2,1,0:T(8,128)S(1)} collective-permute-done((f32[3,32,128]{2,1,0:T(8,128)S(1)}, f32[3,32,128]{2,1,0:T(8,128)S(1)}, u32[]{:S(2)}, u32[]{:S(2)}) %collective-permute-start.4) | collective-permute-done | bytes 49184 | tf_op jit(solution)/shard_map/ppermute | solution.py:385
  20.3 2.0 %collective-permute-done.2 = f32[3,32,128]{2,1,0:T(8,128)S(1)} collective-permute-done((f32[3,32,128]{2,1,0:T(8,128)S(1)}, f32[3,32,128]{2,1,0:T(8,128)S(1)}, u32[]{:S(2)}, u32[]{:S(2)}) %collective-permute-start.2) | collective-permute-done | bytes 49184 | tf_op jit(solution)/shard_map/ppermute | solution.py:385
  22.4 0.1 collective-permute-start.5
  22.5 1.2 %collective-permute-done.5 = f32[4,32,128]{2,1,0:T(8,128)S(1)} collective-permute-done((f32[4,32,128]{2,1,0:T(8,128)S(1)}, f32[4,32,128]{2,1,0:T(8,128)S(1)}, u32[]{:S(2)}, u32[]{:S(2)}) %collective-permute-start.5) | collective-permute-done | bytes 65568 | tf_op jit(solution)/shard_map/ppermute | solution.py:408
  23.8 0.0 copy-done
  23.8 2.9 %stress.1 = (bf16[3072,512]{1,0:T(8,128)(2,1)}, bf16[768,512]{1,0:T(8,128)(2,1)S(1)}, f32[16,1,512]{2,1,0:T(1,128)}) custom-call(bf16[3072,512]{1,0:T(8,128)(2,1)S(1)} %get-tuple-element.52.cur_ref, bf16[768,128]{1,0:T(8,128)(2,1)S(1)} %get-tuple-element.53.start_ref, f32[768,512]{1,0:T(8,128)S(1)} %get-tuple-element.54.fresh_ref, ...), custom_call_target="tpu_custom_call" | custom-call | flops 805306368 | bytes 10485760 | tf_op jit(solution)/shard_map/stress/pallas_call | solution.py:514
  26.7 4.0 %all-to-all-start = ((f32[16,1,512]{2,1,0:T(1,128)}), f32[16,1,512]{2,1,0:T(1,128)S(1)}, u32[]{:S(2)}, u32[]{:S(2)}) async-start(f32[16,1,512]{2,1,0:T(1,128)} %get-tuple-element.98), calls=%async_computation | async-start | bytes 65536 | tf_op jit(solution)/shard_map/all_to_all | solution.py:531
  30.7 4.8 %adjoint.1 = (bf16[3072,512]{1,0:T(8,128)(2,1)}, bf16[3072,512]{1,0:T(8,128)(2,1)}) custom-call(bf16[3072,512]{1,0:T(8,128)(2,1)} %cot_hbm.3, bf16[3072,512]{1,0:T(8,128)(2,1)} %get-tuple-element.90.early_hbm, bf16[768,512]{1,0:T(8,128)(2,1)S(1)} %get-tuple-element.91.tail_ref, ...), custom_call_target="tpu_custom_call", output_to_operand_aliasing={{1}: (1, {})} | custom-call | flops 805306368 | bytes 10485760 | tf_op jit(solution)/shard_map/adjoint/pallas_call | solution.py:533
  35.5 1.8 %all-to-all-done = f32[16,1,512]{2,1,0:T(1,128)S(1)} async-done(((f32[16,1,512]{2,1,0:T(1,128)}), f32[16,1,512]{2,1,0:T(1,128)S(1)}, u32[]{:S(2)}, u32[]{:S(2)}) %all-to-all-start) | async-done | bytes 32800 | tf_op jit(solution)/shard_map/all_to_all | solution.py:531
  37.3 0.1 exponential_reduce_fusion
  37.4 0.6 %add_multiply_fusion = f32[512]{0:T(512)} fusion(f32[512]{0:T(512)S(1)} %exponential_reduce_fusion, f32[512]{0:T(512)S(1)} %reduce_max.9), kind=kLoop, calls=%fused_computation.49 | loop fusion | flops 1536 | bytes 6144 | tf_op jit(solution)/shard_map/div | solution.py:560
  (21 shorter events, 0.2 us)
Async XLA Ops:
  5.2 1.4 %collective-permute-start = (f32[5,32,128]{2,1,0:T(8,128)S(1)}, f32[5,32,128]{2,1,0:T(8,128)S(1)}, u32[]{:S(2)}, u32[]{:S(2)}) collective-permute-start(f32[5,32,128]{2,1,0:T(8,128)S(1)} %pad_maximum_fusion), channel_id=1, source_target_pairs={{0,1},{1,0},{2,3},{3,2},{4,5},{5,4},{6,7},{7,6},{8,9},{9,8},{10,11... | collective-permute-start | bytes 245768 | tf_op jit(solution)/shard_map/ppermute | solution.py:340
  6.7 17.1 %copy-start = (s32[512]{0:T(512)S(1)}, s32[512]{0:T(512)}, u32[]{:S(2)}) copy-start(s32[512]{0:T(512)} %param.11) | copy-start | bytes 6148
  6.7 5.7 %collective-permute-start.1 = (f32[5,32,128]{2,1,0:T(8,128)S(1)}, f32[5,32,128]{2,1,0:T(8,128)S(1)}, u32[]{:S(2)}, u32[]{:S(2)}) collective-permute-start(f32[5,32,128]{2,1,0:T(8,128)S(1)} %pad_maximum_fusion.1), channel_id=1, source_target_pairs={{0,2},{1,3},{2,0},{3,1},{4,6},{5,7},{6,4},{7,5},{8,10},{9,11},{10,... | collective-permute-start | bytes 245768 | tf_op jit(solution)/shard_map/ppermute | solution.py:364
  12.5 5.6 %collective-permute-start.3 = (f32[3,32,128]{2,1,0:T(8,128)S(1)}, f32[3,32,128]{2,1,0:T(8,128)S(1)}, u32[]{:S(2)}, u32[]{:S(2)}) collective-permute-start(f32[3,32,128]{2,1,0:T(8,128)S(1)} %get-tuple-element.74), channel_id=1, source_target_pairs={{0,4},{1,5},{2,6},{3,7},{4,0},{5,1},{6,2},{7,3},{8,12},{9,13},{10,... | collective-permute-start | bytes 147464 | tf_op jit(solution)/shard_map/ppermute | solution.py:385
  14.3 6.0 %collective-permute-start.4 = (f32[3,32,128]{2,1,0:T(8,128)S(1)}, f32[3,32,128]{2,1,0:T(8,128)S(1)}, u32[]{:S(2)}, u32[]{:S(2)}) collective-permute-start(f32[3,32,128]{2,1,0:T(8,128)S(1)} %get-tuple-element.72), channel_id=1, source_target_pairs={{0,12},{1,13},{2,14},{3,15},{4,8},{5,9},{6,10},{7,11},{8,4},{9,5},... | collective-permute-start | bytes 147464 | tf_op jit(solution)/shard_map/ppermute | solution.py:385
  16.8 5.5 %collective-permute-start.2 = (f32[3,32,128]{2,1,0:T(8,128)S(1)}, f32[3,32,128]{2,1,0:T(8,128)S(1)}, u32[]{:S(2)}, u32[]{:S(2)}) collective-permute-start(f32[3,32,128]{2,1,0:T(8,128)S(1)} %get-tuple-element.72), channel_id=1, source_target_pairs={{0,8},{1,9},{2,10},{3,11},{4,12},{5,13},{6,14},{7,15},{8,0},{9,1},... | collective-permute-start | bytes 147464 | tf_op jit(solution)/shard_map/ppermute | solution.py:385
  22.4 1.3 %collective-permute-start.5 = (f32[4,32,128]{2,1,0:T(8,128)S(1)}, f32[4,32,128]{2,1,0:T(8,128)S(1)}, u32[]{:S(2)}, u32[]{:S(2)}) collective-permute-start(f32[4,32,128]{2,1,0:T(8,128)S(1)} %pad_maximum_fusion.3), channel_id=1, source_target_pairs={{0,1},{1,0},{2,3},{3,2},{4,5},{5,4},{6,7},{7,6},{8,9},{9,8},{10,11... | collective-permute-start | bytes 196616 | tf_op jit(solution)/shard_map/ppermute | solution.py:408
  26.7 10.6 %all-to-all-start = ((f32[16,1,512]{2,1,0:T(1,128)}), f32[16,1,512]{2,1,0:T(1,128)S(1)}, u32[]{:S(2)}, u32[]{:S(2)}) async-start(f32[16,1,512]{2,1,0:T(1,128)} %get-tuple-element.98), calls=%async_computation | async-start | bytes 65536 | tf_op jit(solution)/shard_map/all_to_all | solution.py:531

commit v6 on v5

--- a/solution.py
+++ b/solution.py
@@ -106,18 +106,10 @@
     ]
     for copy in small:
         copy.start()
-    loads = []
-    at = 0
-    for k, piece in enumerate(pieces_of(chunks)):
-        rows = pl.ds(at * CHUNK, piece * CHUNK)
-        pair = (
-            pltpu.make_async_copy(cur_hbm.at[rows], cur_ref.at[rows], cur_sem.at[k]),
-            pltpu.make_async_copy(cot_hbm.at[rows], cot_ref.at[rows], cot_sem.at[k]),
-        )
-        for copy in pair:
-            copy.start()
-        loads.append((at, piece, pair))
-        at += piece
+    load_cur = pltpu.make_async_copy(cur_hbm, cur_ref, cur_sem)
+    load_cot = pltpu.make_async_copy(cot_hbm, cot_ref, cot_sem)
+    load_cur.start()
+    load_cot.start()
     sums_ref[...] = level_sums()
     for copy in small:
         copy.wait()
@@ -138,20 +130,21 @@
     tf = jnp.zeros((modes, wires), F32)
     ta = jnp.zeros((modes, wires), F32)
     dc = jnp.ones((modes, CHUNK), F32)
-    for first, piece, pair in loads:
-        for copy in pair:
-            copy.wait()
-        for c in range(first, first + piece):
-            span = slice(c * CHUNK, (c + 1) * CHUNK)
-            rows = slice(c * modes, (c + 1) * modes)
-            decay = decay_ref[rows, :]
-            fresh_f = jnp.dot(back_ref[rows, :], cur_ref[span, :], preferred_element_type=F32)
-            fresh_a = jnp.dot(start_ref[rows, :], cot_ref[span, :], preferred_element_type=F32)
-            fresh_f_ref[rows, :] = fresh_f
-            fresh_a_ref[rows, :] = fresh_a.astype(BF16)
-            tf = wide(decay, reps) * tf + fresh_f
-            ta = ta + wide(dc, reps) * fresh_a
-            dc = dc * decay
+    load_cur.wait()
+    for c in range(chunks):
+        span = slice(c * CHUNK, (c + 1) * CHUNK)
+        rows = slice(c * modes, (c + 1) * modes)
+        fresh_f = jnp.dot(back_ref[rows, :], cur_ref[span, :], preferred_element_type=F32)
+        fresh_f_ref[rows, :] = fresh_f
+        tf = wide(decay_ref[rows, :], reps) * tf + fresh_f
+    load_cot.wait()
+    for c in range(chunks):
+        span = slice(c * CHUNK, (c + 1) * CHUNK)
+        rows = slice(c * modes, (c + 1) * modes)
+        fresh_a = jnp.dot(start_ref[rows, :], cot_ref[span, :], preferred_element_type=F32)
+        fresh_a_ref[rows, :] = fresh_a.astype(BF16)
+        ta = ta + wide(dc, reps) * fresh_a
+        dc = dc * decay_ref[rows, :]
     for k in range(reps):
         lanes = slice(k * CHUNK, (k + 1) * CHUNK)
         msg_ref[k] = tf[:, lanes]
@@ -489,8 +482,8 @@
             pltpu.VMEM((1, modes), F32),
             pltpu.VMEM((1, modes), F32),
             pltpu.SemaphoreType.DMA((3,)),
-            pltpu.SemaphoreType.DMA((copies,)),
-            pltpu.SemaphoreType.DMA((copies,)),
+            pltpu.SemaphoreType.DMA,
+            pltpu.SemaphoreType.DMA,
         ],
         compiler_params=params,
         cost_estimate=pl.CostEstimate(

time: 38.2 us -> 37.3 us (0.976)
  Pallas kernels: 15.4 us -> 14.5 us
    pallas_call x1, Pallas kernels: 4.49 us -> 3.61 us  [body(): pl.pallas_call(totals_kernel, name='totals', in_specs=[apart] * 5, out_sp...]
  transfers between devices with their start and end apart: 7 -> 7, of which waited for: 6 -> 6; matrix products, arithmetic and copies ran while one was open for 0% -> 0% of each run, Pallas kernels for 21% -> 22%
where the time goes in v6:
time: 37.3 us; the launch traced here: 37.1 us
  Pallas kernels  14.5 us (39%)
  starting transfers between devices  11.9 us (32%)
  waiting for transfers between devices  8.89 us (24%)
  other arithmetic  0.91 us (2%)
  between operations  0.84 us (2%)
    pallas_call x1, Pallas kernels, body(): pl.pallas_call(adjoint_kernel, name='adjoint', in_specs=[apart] * 2 + [wh...  4.79 us
    ppermute x3, starting transfers between devices, scan_devices(): lax.ppermute(sent, 'tm', [(i, i ^ hop) for i in range(n)])  4.46 us
    ppermute x3, waiting for transfers between devices, scan_devices(): lax.ppermute(sent, 'tm', [(i, i ^ hop) for i in range(n)])  4.25 us
    all_to_all x1, starting transfers between devices, body(): all_lse = lax.all_to_all(lse, 'tm', 0, 0, tiled=True)  3.96 us
    pallas_call x1, Pallas kernels, body(): pl.pallas_call(totals_kernel, name='totals', in_specs=[apart] * 5, out_sp...  3.61 us
    pallas_call x2, Pallas kernels, __call__(): pl.pallas_call(functools.partial(kernels_kernel, self.modes, sum(self.cou...  3.23 us
    ppermute x1, starting transfers between devices, scan_devices(): got = lax.ppermute(msg, 'tm', [(i, i ^ hop) for i in range(n)])  2.93 us
    pallas_call x1, Pallas kernels, body(): pl.pallas_call(stress_kernel, name='stress', in_specs=[whole] * (6 + part...  2.9 us
  transfers between devices with their start and end apart: 7, of which 6 were waited for; matrix products, arithmetic and copies ran while one was open for 0% of the time, Pallas kernels for 22%

profile of v6, /device:TPU:0, one launch (start us, length us, event | category | flops | bytes accessed | tf_op | source)
XLA Modules:
  0.0 37.1 jit_solution(14129862724997093499)
XLA Ops:
  0.6 3.6 %totals.1 = (bf16[3072,512]{1,0:T(8,128)(2,1)S(1)}, f32[768,512]{1,0:T(8,128)S(1)}, bf16[768,512]{1,0:T(8,128)(2,1)S(1)}, f32[768,128]{1,0:T(8,128)S(1)}, f32[9,...) custom-call(f32[32,3072]{1,0:T(8,128)} %heat_hbm.1, ...), custom_call_target="tpu_custom_call" | custom-call | flops 201326592 | bytes 14680064 | tf_op jit(solution)/shard_map/totals/pallas_call | solution.py:462
  4.3 0.5 %collective-permute-start = (f32[5,32,128]{2,1,0:T(8,128)S(1)}, f32[5,32,128]{2,1,0:T(8,128)S(1)}, u32[]{:S(2)}, u32[]{:S(2)}) collective-permute-start(f32[5,32,128]{2,1,0:T(8,128)S(1)} %pad_maximum_fusion), channel_id=1, source_target_pairs={{0,1},{1,0},{2,3},{3,2},{4,5},{5,4},{6,7},{7,6},{8,9},{9,8},{10,11... | collective-permute-start | bytes 245768 | tf_op jit(solution)/shard_map/ppermute | solution.py:333
  4.8 0.9 %collective-permute-done = f32[5,32,128]{2,1,0:T(8,128)S(1)} collective-permute-done((f32[5,32,128]{2,1,0:T(8,128)S(1)}, f32[5,32,128]{2,1,0:T(8,128)S(1)}, u32[]{:S(2)}, u32[]{:S(2)}) %collective-permute-start) | collective-permute-done | bytes 81952 | tf_op jit(solution)/shard_map/ppermute | solution.py:333
  5.8 0.0 copy-start
  5.8 2.9 %collective-permute-start.1 = (f32[5,32,128]{2,1,0:T(8,128)S(1)}, f32[5,32,128]{2,1,0:T(8,128)S(1)}, u32[]{:S(2)}, u32[]{:S(2)}) collective-permute-start(f32[5,32,128]{2,1,0:T(8,128)S(1)} %pad_maximum_fusion.1), channel_id=1, source_target_pairs={{0,2},{1,3},{2,0},{3,1},{4,6},{5,7},{6,4},{7,5},{8,10},{9,11},{10,... | collective-permute-start | bytes 245768 | tf_op jit(solution)/shard_map/ppermute | solution.py:357
  8.7 2.1 %kernels.2 = (bf16[2048,128]{1,0:T(8,128)(2,1)S(1)}, bf16[2048,128]{1,0:T(8,128)(2,1)S(1)}) custom-call(bf16[768,256]{1,0:T(8,128)(2,1)S(1)} %get-tuple-element.62.split_ref, f32[128,128]{1,0:T(8,128)S(1)} %get-tuple-element.75.gains_ref, bf16[128,896]{1,0:T(8,128)(2,1)S(1)} %get-tuple-element.64.sums_ref), custom_call_target="tpu_custom_call" | custom-call | flops 671088640 | bytes 8388608 | tf_op jit(solution)/shard_map/kernels/pallas_call | solution.py:428
  10.8 0.7 %collective-permute-done.1 = f32[5,32,128]{2,1,0:T(8,128)S(1)} collective-permute-done((f32[5,32,128]{2,1,0:T(8,128)S(1)}, f32[5,32,128]{2,1,0:T(8,128)S(1)}, u32[]{:S(2)}, u32[]{:S(2)}) %collective-permute-start.1) | collective-permute-done | bytes 81952 | tf_op jit(solution)/shard_map/ppermute | solution.py:357
  11.6 1.9 %collective-permute-start.3 = (f32[3,32,128]{2,1,0:T(8,128)S(1)}, f32[3,32,128]{2,1,0:T(8,128)S(1)}, u32[]{:S(2)}, u32[]{:S(2)}) collective-permute-start(f32[3,32,128]{2,1,0:T(8,128)S(1)} %get-tuple-element.74), channel_id=1, source_target_pairs={{0,4},{1,5},{2,6},{3,7},{4,0},{5,1},{6,2},{7,3},{8,12},{9,13},{10,... | collective-permute-start | bytes 147464 | tf_op jit(solution)/shard_map/ppermute | solution.py:378
  13.5 2.5 %collective-permute-start.4 = (f32[3,32,128]{2,1,0:T(8,128)S(1)}, f32[3,32,128]{2,1,0:T(8,128)S(1)}, u32[]{:S(2)}, u32[]{:S(2)}) collective-permute-start(f32[3,32,128]{2,1,0:T(8,128)S(1)} %get-tuple-element.72), channel_id=1, source_target_pairs={{0,12},{1,13},{2,14},{3,15},{4,8},{5,9},{6,10},{7,11},{8,4},{9,5},... | collective-permute-start | bytes 147464 | tf_op jit(solution)/shard_map/ppermute | solution.py:378
  15.9 0.1 collective-permute-start.2
  16.1 1.1 %kernels.3 = (bf16[1024,128]{1,0:T(8,128)(2,1)S(1)}, bf16[1024,128]{1,0:T(8,128)(2,1)S(1)}) custom-call(bf16[768,256]{1,0:T(8,128)(2,1)S(1)} %get-tuple-element.62.split_ref, f32[128,128]{1,0:T(8,128)S(1)} %get-tuple-element.75.gains_ref, bf16[128,896]{1,0:T(8,128)(2,1)S(1)} %get-tuple-element.64.sums_ref), custom_call_target="tpu_custom_call" | custom-call | flops 335544320 | bytes 8388608 | tf_op jit(solution)/shard_map/kernels/pallas_call | solution.py:428
  17.2 0.0 collective-permute-done.3
  17.2 2.3 %collective-permute-done.4 = f32[3,32,128]{2,1,0:T(8,128)S(1)} collective-permute-done((f32[3,32,128]{2,1,0:T(8,128)S(1)}, f32[3,32,128]{2,1,0:T(8,128)S(1)}, u32[]{:S(2)}, u32[]{:S(2)}) %collective-permute-start.4) | collective-permute-done | bytes 49184 | tf_op jit(solution)/shard_map/ppermute | solution.py:378
  19.5 2.0 %collective-permute-done.2 = f32[3,32,128]{2,1,0:T(8,128)S(1)} collective-permute-done((f32[3,32,128]{2,1,0:T(8,128)S(1)}, f32[3,32,128]{2,1,0:T(8,128)S(1)}, u32[]{:S(2)}, u32[]{:S(2)}) %collective-permute-start.2) | collective-permute-done | bytes 49184 | tf_op jit(solution)/shard_map/ppermute | solution.py:378
  21.5 0.1 collective-permute-start.5
  21.6 1.2 %collective-permute-done.5 = f32[4,32,128]{2,1,0:T(8,128)S(1)} collective-permute-done((f32[4,32,128]{2,1,0:T(8,128)S(1)}, f32[4,32,128]{2,1,0:T(8,128)S(1)}, u32[]{:S(2)}, u32[]{:S(2)}) %collective-permute-start.5) | collective-permute-done | bytes 65568 | tf_op jit(solution)/shard_map/ppermute | solution.py:401
  22.9 0.0 copy-done
  22.9 2.9 %stress.1 = (bf16[3072,512]{1,0:T(8,128)(2,1)}, bf16[768,512]{1,0:T(8,128)(2,1)S(1)}, f32[16,1,512]{2,1,0:T(1,128)}) custom-call(bf16[3072,512]{1,0:T(8,128)(2,1)S(1)} %get-tuple-element.52.cur_ref, bf16[768,128]{1,0:T(8,128)(2,1)S(1)} %get-tuple-element.53.start_ref, f32[768,512]{1,0:T(8,128)S(1)} %get-tuple-element.54.fresh_ref, ...), custom_call_target="tpu_custom_call" | custom-call | flops 805306368 | bytes 10485760 | tf_op jit(solution)/shard_map/stress/pallas_call | solution.py:507
  25.8 4.0 %all-to-all-start = ((f32[16,1,512]{2,1,0:T(1,128)}), f32[16,1,512]{2,1,0:T(1,128)S(1)}, u32[]{:S(2)}, u32[]{:S(2)}) async-start(f32[16,1,512]{2,1,0:T(1,128)} %get-tuple-element.98), calls=%async_computation | async-start | bytes 65536 | tf_op jit(solution)/shard_map/all_to_all | solution.py:524
  29.8 4.8 %adjoint.1 = (bf16[3072,512]{1,0:T(8,128)(2,1)}, bf16[3072,512]{1,0:T(8,128)(2,1)}) custom-call(bf16[3072,512]{1,0:T(8,128)(2,1)} %cot_hbm.3, bf16[3072,512]{1,0:T(8,128)(2,1)} %get-tuple-element.90.early_hbm, bf16[768,512]{1,0:T(8,128)(2,1)S(1)} %get-tuple-element.91.tail_ref, ...), custom_call_target="tpu_custom_call", output_to_operand_aliasing={{1}: (1, {})} | custom-call | flops 805306368 | bytes 10485760 | tf_op jit(solution)/shard_map/adjoint/pallas_call | solution.py:526
  34.6 1.8 %all-to-all-done = f32[16,1,512]{2,1,0:T(1,128)S(1)} async-done(((f32[16,1,512]{2,1,0:T(1,128)}), f32[16,1,512]{2,1,0:T(1,128)S(1)}, u32[]{:S(2)}, u32[]{:S(2)}) %all-to-all-start) | async-done | bytes 32800 | tf_op jit(solution)/shard_map/all_to_all | solution.py:524
  36.4 0.1 exponential_reduce_fusion
  36.5 0.6 %add_multiply_fusion = f32[512]{0:T(512)} fusion(f32[512]{0:T(512)S(1)} %exponential_reduce_fusion, f32[512]{0:T(512)S(1)} %reduce_max.9), kind=kLoop, calls=%fused_computation.49 | loop fusion | flops 1536 | bytes 6144 | tf_op jit(solution)/shard_map/div | solution.py:553
  (21 shorter events, 0.2 us)
Async XLA Ops:
  4.3 1.4 %collective-permute-start = (f32[5,32,128]{2,1,0:T(8,128)S(1)}, f32[5,32,128]{2,1,0:T(8,128)S(1)}, u32[]{:S(2)}, u32[]{:S(2)}) collective-permute-start(f32[5,32,128]{2,1,0:T(8,128)S(1)} %pad_maximum_fusion), channel_id=1, source_target_pairs={{0,1},{1,0},{2,3},{3,2},{4,5},{5,4},{6,7},{7,6},{8,9},{9,8},{10,11... | collective-permute-start | bytes 245768 | tf_op jit(solution)/shard_map/ppermute | solution.py:333
  5.8 17.1 %copy-start = (s32[512]{0:T(512)S(1)}, s32[512]{0:T(512)}, u32[]{:S(2)}) copy-start(s32[512]{0:T(512)} %param.11) | copy-start | bytes 6148
  5.8 5.7 %collective-permute-start.1 = (f32[5,32,128]{2,1,0:T(8,128)S(1)}, f32[5,32,128]{2,1,0:T(8,128)S(1)}, u32[]{:S(2)}, u32[]{:S(2)}) collective-permute-start(f32[5,32,128]{2,1,0:T(8,128)S(1)} %pad_maximum_fusion.1), channel_id=1, source_target_pairs={{0,2},{1,3},{2,0},{3,1},{4,6},{5,7},{6,4},{7,5},{8,10},{9,11},{10,... | collective-permute-start | bytes 245768 | tf_op jit(solution)/shard_map/ppermute | solution.py:357
  11.6 5.6 %collective-permute-start.3 = (f32[3,32,128]{2,1,0:T(8,128)S(1)}, f32[3,32,128]{2,1,0:T(8,128)S(1)}, u32[]{:S(2)}, u32[]{:S(2)}) collective-permute-start(f32[3,32,128]{2,1,0:T(8,128)S(1)} %get-tuple-element.74), channel_id=1, source_target_pairs={{0,4},{1,5},{2,6},{3,7},{4,0},{5,1},{6,2},{7,3},{8,12},{9,13},{10,... | collective-permute-start | bytes 147464 | tf_op jit(solution)/shard_map/ppermute | solution.py:378
  13.5 6.0 %collective-permute-start.4 = (f32[3,32,128]{2,1,0:T(8,128)S(1)}, f32[3,32,128]{2,1,0:T(8,128)S(1)}, u32[]{:S(2)}, u32[]{:S(2)}) collective-permute-start(f32[3,32,128]{2,1,0:T(8,128)S(1)} %get-tuple-element.72), channel_id=1, source_target_pairs={{0,12},{1,13},{2,14},{3,15},{4,8},{5,9},{6,10},{7,11},{8,4},{9,5},... | collective-permute-start | bytes 147464 | tf_op jit(solution)/shard_map/ppermute | solution.py:378
  15.9 5.5 %collective-permute-start.2 = (f32[3,32,128]{2,1,0:T(8,128)S(1)}, f32[3,32,128]{2,1,0:T(8,128)S(1)}, u32[]{:S(2)}, u32[]{:S(2)}) collective-permute-start(f32[3,32,128]{2,1,0:T(8,128)S(1)} %get-tuple-element.72), channel_id=1, source_target_pairs={{0,8},{1,9},{2,10},{3,11},{4,12},{5,13},{6,14},{7,15},{8,0},{9,1},... | collective-permute-start | bytes 147464 | tf_op jit(solution)/shard_map/ppermute | solution.py:378
  21.5 1.3 %collective-permute-start.5 = (f32[4,32,128]{2,1,0:T(8,128)S(1)}, f32[4,32,128]{2,1,0:T(8,128)S(1)}, u32[]{:S(2)}, u32[]{:S(2)}) collective-permute-start(f32[4,32,128]{2,1,0:T(8,128)S(1)} %pad_maximum_fusion.3), channel_id=1, source_target_pairs={{0,1},{1,0},{2,3},{3,2},{4,5},{5,4},{6,7},{7,6},{8,9},{9,8},{10,11... | collective-permute-start | bytes 196616 | tf_op jit(solution)/shard_map/ppermute | solution.py:401
  25.8 10.6 %all-to-all-start = ((f32[16,1,512]{2,1,0:T(1,128)}), f32[16,1,512]{2,1,0:T(1,128)S(1)}, u32[]{:S(2)}, u32[]{:S(2)}) async-start(f32[16,1,512]{2,1,0:T(1,128)} %get-tuple-element.98), calls=%async_computation | async-start | bytes 65536 | tf_op jit(solution)/shard_map/all_to_all | solution.py:524

commit v7 on v6

--- a/solution.py
+++ b/solution.py
@@ -212,7 +212,7 @@
     if chunks % 8:
         return [1] * chunks
     unit = chunks // 8
-    return [2 * unit, 2 * unit, unit, unit, 2 * unit]
+    return [2 * unit, unit, unit, unit, 3 * unit]
 
 
 def stress_kernel(
@@ -498,8 +498,8 @@
     )
 
     groups = chunks * modes // CHUNK
-    parts = 2
-    shares = [groups - groups // 3, groups // 3]
+    parts = 1
+    shares = [groups]
     covered = KernelParts(split, gains, sums, modes, shares, params)
     before, after = scan_devices(msg, uppers, reps, covered, parts)
 

time: 37.3 us -> 36.5 us (0.979)
  waiting for transfers between devices: 8.89 us -> 7.95 us
  starting transfers between devices: 11.9 us -> 12.3 us
    ppermute x3, waiting for transfers between devices: 4.25 us -> 1.35 us  [scan_devices(): lax.ppermute(sent, 'tm', [(i, i ^ hop) for i in range(n)])]
    ppermute x1, waiting for transfers between devices: 0.66 us -> 2.76 us  [scan_devices(): got = lax.ppermute(msg, 'tm', [(i, i ^ hop) for i in range(n)])]
    all_to_all x1, starting transfers between devices: 3.96 us -> 4.34 us  [body(): all_lse = lax.all_to_all(lse, 'tm', 0, 0, tiled=True)]
    pallas_call x2 -> x1, Pallas kernels: 3.23 us -> 3.03 us  [__call__(): pl.pallas_call(functools.partial(kernels_kernel, self.modes, sum(self.cou...]
where the time goes in v7:
time: 36.5 us; the launch traced here: 36.3 us
  Pallas kernels  14.3 us (39%)
  starting transfers between devices  12.3 us (34%)
  waiting for transfers between devices  7.95 us (22%)
  other arithmetic  0.91 us (2%)
  between operations  0.82 us (2%)
    pallas_call x1, Pallas kernels, body(): pl.pallas_call(adjoint_kernel, name='adjoint', in_specs=[apart] * 2 + [wh...  4.93 us
    ppermute x3, starting transfers between devices, scan_devices(): lax.ppermute(sent, 'tm', [(i, i ^ hop) for i in range(n)])  4.46 us
    all_to_all x1, starting transfers between devices, body(): all_lse = lax.all_to_all(lse, 'tm', 0, 0, tiled=True)  4.34 us
    pallas_call x1, Pallas kernels, body(): pl.pallas_call(totals_kernel, name='totals', in_specs=[apart] * 5, out_sp...  3.61 us
    pallas_call x1, Pallas kernels, __call__(): pl.pallas_call(functools.partial(kernels_kernel, self.modes, sum(self.cou...  3.03 us
    ppermute x1, starting transfers between devices, scan_devices(): got = lax.ppermute(msg, 'tm', [(i, i ^ hop) for i in range(n)])  2.93 us
    ppermute x1, waiting for transfers between devices, scan_devices(): got = lax.ppermute(msg, 'tm', [(i, i ^ hop) for i in range(n)])  2.76 us
    pallas_call x1, Pallas kernels, body(): pl.pallas_call(stress_kernel, name='stress', in_specs=[whole] * (6 + part...  2.68 us
  transfers between devices with their start and end apart: 7, of which 6 were waited for; matrix products, arithmetic and copies ran while one was open for 0% of the time, Pallas kernels for 22%

profile of v7, /device:TPU:0, one launch (start us, length us, event | category | flops | bytes accessed | tf_op | source)
XLA Modules:
  0.0 36.3 jit_solution(16953305865783296421)
XLA Ops:
  0.6 3.6 %totals.1 = (bf16[3072,512]{1,0:T(8,128)(2,1)S(1)}, f32[768,512]{1,0:T(8,128)S(1)}, bf16[768,512]{1,0:T(8,128)(2,1)S(1)}, f32[768,128]{1,0:T(8,128)S(1)}, f32[9,...) custom-call(f32[32,3072]{1,0:T(8,128)} %heat_hbm.1, ...), custom_call_target="tpu_custom_call" | custom-call | flops 201326592 | bytes 14680064 | tf_op jit(solution)/shard_map/totals/pallas_call | solution.py:462
  4.3 0.5 %collective-permute-start = (f32[5,32,128]{2,1,0:T(8,128)S(1)}, f32[5,32,128]{2,1,0:T(8,128)S(1)}, u32[]{:S(2)}, u32[]{:S(2)}) collective-permute-start(f32[5,32,128]{2,1,0:T(8,128)S(1)} %pad_maximum_fusion), channel_id=1, source_target_pairs={{0,1},{1,0},{2,3},{3,2},{4,5},{5,4},{6,7},{7,6},{8,9},{9,8},{10,11... | collective-permute-start | bytes 245768 | tf_op jit(solution)/shard_map/ppermute | solution.py:333
  4.8 0.9 %collective-permute-done = f32[5,32,128]{2,1,0:T(8,128)S(1)} collective-permute-done((f32[5,32,128]{2,1,0:T(8,128)S(1)}, f32[5,32,128]{2,1,0:T(8,128)S(1)}, u32[]{:S(2)}, u32[]{:S(2)}) %collective-permute-start) | collective-permute-done | bytes 81952 | tf_op jit(solution)/shard_map/ppermute | solution.py:333
  5.8 0.0 copy-start
  5.8 2.9 %collective-permute-start.1 = (f32[5,32,128]{2,1,0:T(8,128)S(1)}, f32[5,32,128]{2,1,0:T(8,128)S(1)}, u32[]{:S(2)}, u32[]{:S(2)}) collective-permute-start(f32[5,32,128]{2,1,0:T(8,128)S(1)} %pad_maximum_fusion.1), channel_id=1, source_target_pairs={{0,2},{1,3},{2,0},{3,1},{4,6},{5,7},{6,4},{7,5},{8,10},{9,11},{10,... | collective-permute-start | bytes 245768 | tf_op jit(solution)/shard_map/ppermute | solution.py:357
  8.7 2.8 %collective-permute-done.1 = f32[5,32,128]{2,1,0:T(8,128)S(1)} collective-permute-done((f32[5,32,128]{2,1,0:T(8,128)S(1)}, f32[5,32,128]{2,1,0:T(8,128)S(1)}, u32[]{:S(2)}, u32[]{:S(2)}) %collective-permute-start.1) | collective-permute-done | bytes 81952 | tf_op jit(solution)/shard_map/ppermute | solution.py:357
  11.6 2.9 %collective-permute-start.2 = (f32[3,32,128]{2,1,0:T(8,128)S(1)}, f32[3,32,128]{2,1,0:T(8,128)S(1)}, u32[]{:S(2)}, u32[]{:S(2)}) collective-permute-start(f32[3,32,128]{2,1,0:T(8,128)S(1)} %get-tuple-element.57), channel_id=1, source_target_pairs={{0,8},{1,9},{2,10},{3,11},{4,12},{5,13},{6,14},{7,15},{8,0},{9,1},... | collective-permute-start | bytes 147464 | tf_op jit(solution)/shard_map/ppermute | solution.py:378
  14.5 1.3 %collective-permute-start.4 = (f32[3,32,128]{2,1,0:T(8,128)S(1)}, f32[3,32,128]{2,1,0:T(8,128)S(1)}, u32[]{:S(2)}, u32[]{:S(2)}) collective-permute-start(f32[3,32,128]{2,1,0:T(8,128)S(1)} %get-tuple-element.57), channel_id=1, source_target_pairs={{0,12},{1,13},{2,14},{3,15},{4,8},{5,9},{6,10},{7,11},{8,4},{9,5},... | collective-permute-start | bytes 147464 | tf_op jit(solution)/shard_map/ppermute | solution.py:378
  15.8 0.2 collective-permute-start.3
  16.1 3.0 %kernels.1 = (bf16[3072,128]{1,0:T(8,128)(2,1)S(1)}, bf16[3072,128]{1,0:T(8,128)(2,1)S(1)}) custom-call(bf16[768,256]{1,0:T(8,128)(2,1)S(1)} %get-tuple-element.61.split_ref, f32[128,128]{1,0:T(8,128)S(1)} %get-tuple-element.62.gains_ref, bf16[128,896]{1,0:T(8,128)(2,1)S(1)} %get-tuple-element.63.sums_ref), custom_call_target="tpu_custom_call" | custom-call | flops 1006632960 | bytes 8388608 | tf_op jit(solution)/shard_map/kernels/pallas_call | solution.py:428
  19.1 0.8 %collective-permute-done.3 = f32[3,32,128]{2,1,0:T(8,128)S(1)} collective-permute-done((f32[3,32,128]{2,1,0:T(8,128)S(1)}, f32[3,32,128]{2,1,0:T(8,128)S(1)}, u32[]{:S(2)}, u32[]{:S(2)}) %collective-permute-start.3) | collective-permute-done | bytes 49184 | tf_op jit(solution)/shard_map/ppermute | solution.py:378
  19.9 0.0 collective-permute-done.2
  19.9 0.5 %collective-permute-done.4 = f32[3,32,128]{2,1,0:T(8,128)S(1)} collective-permute-done((f32[3,32,128]{2,1,0:T(8,128)S(1)}, f32[3,32,128]{2,1,0:T(8,128)S(1)}, u32[]{:S(2)}, u32[]{:S(2)}) %collective-permute-start.4) | collective-permute-done | bytes 49184 | tf_op jit(solution)/shard_map/ppermute | solution.py:378
  20.5 0.1 collective-permute-start.5
  20.6 1.2 %collective-permute-done.5 = f32[4,32,128]{2,1,0:T(8,128)S(1)} collective-permute-done((f32[4,32,128]{2,1,0:T(8,128)S(1)}, f32[4,32,128]{2,1,0:T(8,128)S(1)}, u32[]{:S(2)}, u32[]{:S(2)}) %collective-permute-start.5) | collective-permute-done | bytes 65568 | tf_op jit(solution)/shard_map/ppermute | solution.py:401
  21.9 0.0 copy-done
  21.9 2.7 %stress.1 = (bf16[3072,512]{1,0:T(8,128)(2,1)}, bf16[1152,512]{1,0:T(8,128)(2,1)S(1)}, f32[16,1,512]{2,1,0:T(1,128)}) custom-call(bf16[3072,512]{1,0:T(8,128)(2,1)S(1)} %get-tuple-element.45.cur_ref, bf16[768,128]{1,0:T(8,128)(2,1)S(1)} %get-tuple-element.46.start_ref, f32[768,512]{1,0:T(8,128)S(1)} %get-tuple-element.47.fresh_ref, ...), custom_call_target="tpu_custom_call" | custom-call | flops 805306368 | bytes 10485760 | tf_op jit(solution)/shard_map/stress/pallas_call | solution.py:507
  24.6 4.3 %all-to-all-start = ((f32[16,1,512]{2,1,0:T(1,128)}), f32[16,1,512]{2,1,0:T(1,128)S(1)}, u32[]{:S(2)}, u32[]{:S(2)}) async-start(f32[16,1,512]{2,1,0:T(1,128)} %get-tuple-element.84), calls=%async_computation | async-start | bytes 65536 | tf_op jit(solution)/shard_map/all_to_all | solution.py:524
  28.9 4.9 %adjoint.1 = (bf16[3072,512]{1,0:T(8,128)(2,1)}, bf16[3072,512]{1,0:T(8,128)(2,1)}) custom-call(bf16[3072,512]{1,0:T(8,128)(2,1)} %cot_hbm.3, bf16[3072,512]{1,0:T(8,128)(2,1)} %get-tuple-element.77.early_hbm, bf16[1152,512]{1,0:T(8,128)(2,1)S(1)} %get-tuple-element.78.tail_ref, ...), custom_call_target="tpu_custom_call", output_to_operand_aliasing={{1}: (1, {})} | custom-call | flops 805306368 | bytes 10485760 | tf_op jit(solution)/shard_map/adjoint/pallas_call | solution.py:526
  33.9 1.7 %all-to-all-done = f32[16,1,512]{2,1,0:T(1,128)S(1)} async-done(((f32[16,1,512]{2,1,0:T(1,128)}), f32[16,1,512]{2,1,0:T(1,128)S(1)}, u32[]{:S(2)}, u32[]{:S(2)}) %all-to-all-start) | async-done | bytes 32800 | tf_op jit(solution)/shard_map/all_to_all | solution.py:524
  35.6 0.1 exponential_reduce_fusion
  35.7 0.6 %add_multiply_fusion = f32[512]{0:T(512)} fusion(f32[512]{0:T(512)S(1)} %exponential_reduce_fusion, f32[512]{0:T(512)S(1)} %reduce_max.9), kind=kLoop, calls=%fused_computation.49 | loop fusion | flops 1536 | bytes 6144 | tf_op jit(solution)/shard_map/div | solution.py:553
  (21 shorter events, 0.2 us)
Async XLA Ops:
  4.3 1.4 %collective-permute-start = (f32[5,32,128]{2,1,0:T(8,128)S(1)}, f32[5,32,128]{2,1,0:T(8,128)S(1)}, u32[]{:S(2)}, u32[]{:S(2)}) collective-permute-start(f32[5,32,128]{2,1,0:T(8,128)S(1)} %pad_maximum_fusion), channel_id=1, source_target_pairs={{0,1},{1,0},{2,3},{3,2},{4,5},{5,4},{6,7},{7,6},{8,9},{9,8},{10,11... | collective-permute-start | bytes 245768 | tf_op jit(solution)/shard_map/ppermute | solution.py:333
  5.8 16.1 %copy-start = (s32[512]{0:T(512)S(1)}, s32[512]{0:T(512)}, u32[]{:S(2)}) copy-start(s32[512]{0:T(512)} %param.11) | copy-start | bytes 6148
  5.8 5.7 %collective-permute-start.1 = (f32[5,32,128]{2,1,0:T(8,128)S(1)}, f32[5,32,128]{2,1,0:T(8,128)S(1)}, u32[]{:S(2)}, u32[]{:S(2)}) collective-permute-start(f32[5,32,128]{2,1,0:T(8,128)S(1)} %pad_maximum_fusion.1), channel_id=1, source_target_pairs={{0,2},{1,3},{2,0},{3,1},{4,6},{5,7},{6,4},{7,5},{8,10},{9,11},{10,... | collective-permute-start | bytes 245768 | tf_op jit(solution)/shard_map/ppermute | solution.py:357
  11.6 8.3 %collective-permute-start.2 = (f32[3,32,128]{2,1,0:T(8,128)S(1)}, f32[3,32,128]{2,1,0:T(8,128)S(1)}, u32[]{:S(2)}, u32[]{:S(2)}) collective-permute-start(f32[3,32,128]{2,1,0:T(8,128)S(1)} %get-tuple-element.57), channel_id=1, source_target_pairs={{0,8},{1,9},{2,10},{3,11},{4,12},{5,13},{6,14},{7,15},{8,0},{9,1},... | collective-permute-start | bytes 147464 | tf_op jit(solution)/shard_map/ppermute | solution.py:378
  14.5 6.0 %collective-permute-start.4 = (f32[3,32,128]{2,1,0:T(8,128)S(1)}, f32[3,32,128]{2,1,0:T(8,128)S(1)}, u32[]{:S(2)}, u32[]{:S(2)}) collective-permute-start(f32[3,32,128]{2,1,0:T(8,128)S(1)} %get-tuple-element.57), channel_id=1, source_target_pairs={{0,12},{1,13},{2,14},{3,15},{4,8},{5,9},{6,10},{7,11},{8,4},{9,5},... | collective-permute-start | bytes 147464 | tf_op jit(solution)/shard_map/ppermute | solution.py:378
  15.8 4.1 %collective-permute-start.3 = (f32[3,32,128]{2,1,0:T(8,128)S(1)}, f32[3,32,128]{2,1,0:T(8,128)S(1)}, u32[]{:S(2)}, u32[]{:S(2)}) collective-permute-start(f32[3,32,128]{2,1,0:T(8,128)S(1)} %get-tuple-element.60), channel_id=1, source_target_pairs={{0,4},{1,5},{2,6},{3,7},{4,0},{5,1},{6,2},{7,3},{8,12},{9,13},{10,... | collective-permute-start | bytes 147464 | tf_op jit(solution)/shard_map/ppermute | solution.py:378
  20.5 1.3 %collective-permute-start.5 = (f32[4,32,128]{2,1,0:T(8,128)S(1)}, f32[4,32,128]{2,1,0:T(8,128)S(1)}, u32[]{:S(2)}, u32[]{:S(2)}) collective-permute-start(f32[4,32,128]{2,1,0:T(8,128)S(1)} %pad_maximum_fusion.3), channel_id=1, source_target_pairs={{0,1},{1,0},{2,3},{3,2},{4,5},{5,4},{6,7},{7,6},{8,9},{9,8},{10,11... | collective-permute-start | bytes 196616 | tf_op jit(solution)/shard_map/ppermute | solution.py:401
  24.6 11.0 %all-to-all-start = ((f32[16,1,512]{2,1,0:T(1,128)}), f32[16,1,512]{2,1,0:T(1,128)S(1)}, u32[]{:S(2)}, u32[]{:S(2)}) async-start(f32[16,1,512]{2,1,0:T(1,128)} %get-tuple-element.84), calls=%async_computation | async-start | bytes 65536 | tf_op jit(solution)/shard_map/all_to_all | solution.py:524

commit v8 on v7

--- a/solution.py
+++ b/solution.py
@@ -97,7 +97,7 @@
     samples, wires = cur_ref.shape
     reps = wires // CHUNK
     chunks = samples // CHUNK
-    group = group_of(chunks, 3)
+    group = group_of(chunks, 4)
 
     small = [
         pltpu.make_async_copy(heat_hbm, heat_ref, small_sem.at[0]),
@@ -273,21 +273,15 @@
     modes = in_ref.shape[1]
     scale = counts_ref[...].astype(F32) * 0.25
     state = jnp.concatenate([in_ref[k] for k in range(reps)], axis=1)
-    loads = []
-    end = chunks
-    for k, piece in enumerate(pieces_of(chunks)):
-        rows = pl.ds((end - piece) * CHUNK, piece * CHUNK)
-        copy = pltpu.make_async_copy(cot_hbm.at[rows], cot_ref.at[rows], load_sem.at[k])
-        copy.start()
-        loads.append(copy)
-        end -= piece
+    load = pltpu.make_async_copy(cot_hbm, cot_ref, load_sem)
+    load.start()
     tail = tail_ref.shape[0]
     copy = pltpu.make_async_copy(tail_ref, stress_hbm.at[pl.ds(samples - tail, tail)], tail_sem)
     copy.start()
     stores = [copy]
+    load.wait()
     end = chunks
     for k, piece in enumerate(pieces_of(chunks)):
-        loads[k].wait()
         for c in reversed(range(end - piece, end)):
             span = slice(c * CHUNK, (c + 1) * CHUNK)
             rows = slice(c * modes, (c + 1) * modes)
@@ -533,7 +527,7 @@
         scratch_shapes=[
             pltpu.VMEM((samples, wires), BF16),
             pltpu.VMEM((samples, wires), BF16),
-            pltpu.SemaphoreType.DMA((copies,)),
+            pltpu.SemaphoreType.DMA,
             pltpu.SemaphoreType.DMA((copies,)),
             pltpu.SemaphoreType.DMA,
         ],

time: 36.5 us -> 36.5 us (level)
  no operation moved by 1% of the time
where the time goes in v8:
time: 36.5 us; the launch traced here: 36.3 us
  Pallas kernels  14.3 us (39%)
  starting transfers between devices  12.3 us (34%)
  waiting for transfers between devices  7.89 us (22%)
  other arithmetic  0.91 us (2%)
  between operations  0.82 us (2%)
    pallas_call x1, Pallas kernels, body(): pl.pallas_call(adjoint_kernel, name='adjoint', in_specs=[apart] * 2 + [wh...  4.99 us
    ppermute x3, starting transfers between devices, scan_devices(): lax.ppermute(sent, 'tm', [(i, i ^ hop) for i in range(n)])  4.46 us
    all_to_all x1, starting transfers between devices, body(): all_lse = lax.all_to_all(lse, 'tm', 0, 0, tiled=True)  4.34 us
    pallas_call x1, Pallas kernels, body(): pl.pallas_call(totals_kernel, name='totals', in_specs=[apart] * 5, out_sp...  3.61 us
    pallas_call x1, Pallas kernels, __call__(): pl.pallas_call(functools.partial(kernels_kernel, self.modes, sum(self.cou...  3.03 us
    ppermute x1, starting transfers between devices, scan_devices(): got = lax.ppermute(msg, 'tm', [(i, i ^ hop) for i in range(n)])  2.93 us
    ppermute x1, waiting for transfers between devices, scan_devices(): got = lax.ppermute(msg, 'tm', [(i, i ^ hop) for i in range(n)])  2.76 us
    pallas_call x1, Pallas kernels, body(): pl.pallas_call(stress_kernel, name='stress', in_specs=[whole] * (6 + part...  2.68 us
  transfers between devices with their start and end apart: 7, of which 6 were waited for; matrix products, arithmetic and copies ran while one was open for 0% of the time, Pallas kernels for 22%

profile of v8, /device:TPU:0, one launch (start us, length us, event | category | flops | bytes accessed | tf_op | source)
XLA Modules:
  0.0 36.3 jit_solution(11219197039711940899)
XLA Ops:
  0.6 3.6 %totals.1 = (bf16[3072,512]{1,0:T(8,128)(2,1)S(1)}, f32[768,512]{1,0:T(8,128)S(1)}, bf16[768,512]{1,0:T(8,128)(2,1)S(1)}, f32[768,128]{1,0:T(8,128)S(1)}, f32[9,...) custom-call(f32[32,3072]{1,0:T(8,128)} %heat_hbm.1, ...), custom_call_target="tpu_custom_call" | custom-call | flops 201326592 | bytes 14680064 | tf_op jit(solution)/shard_map/totals/pallas_call | solution.py:456
  4.3 0.5 %collective-permute-start = (f32[5,32,128]{2,1,0:T(8,128)S(1)}, f32[5,32,128]{2,1,0:T(8,128)S(1)}, u32[]{:S(2)}, u32[]{:S(2)}) collective-permute-start(f32[5,32,128]{2,1,0:T(8,128)S(1)} %pad_maximum_fusion), channel_id=1, source_target_pairs={{0,1},{1,0},{2,3},{3,2},{4,5},{5,4},{6,7},{7,6},{8,9},{9,8},{10,11... | collective-permute-start | bytes 245768 | tf_op jit(solution)/shard_map/ppermute | solution.py:327
  4.8 0.9 %collective-permute-done = f32[5,32,128]{2,1,0:T(8,128)S(1)} collective-permute-done((f32[5,32,128]{2,1,0:T(8,128)S(1)}, f32[5,32,128]{2,1,0:T(8,128)S(1)}, u32[]{:S(2)}, u32[]{:S(2)}) %collective-permute-start) | collective-permute-done | bytes 81952 | tf_op jit(solution)/shard_map/ppermute | solution.py:327
  5.8 0.0 copy-start
  5.8 2.9 %collective-permute-start.1 = (f32[5,32,128]{2,1,0:T(8,128)S(1)}, f32[5,32,128]{2,1,0:T(8,128)S(1)}, u32[]{:S(2)}, u32[]{:S(2)}) collective-permute-start(f32[5,32,128]{2,1,0:T(8,128)S(1)} %pad_maximum_fusion.1), channel_id=1, source_target_pairs={{0,2},{1,3},{2,0},{3,1},{4,6},{5,7},{6,4},{7,5},{8,10},{9,11},{10,... | collective-permute-start | bytes 245768 | tf_op jit(solution)/shard_map/ppermute | solution.py:351
  8.7 2.8 %collective-permute-done.1 = f32[5,32,128]{2,1,0:T(8,128)S(1)} collective-permute-done((f32[5,32,128]{2,1,0:T(8,128)S(1)}, f32[5,32,128]{2,1,0:T(8,128)S(1)}, u32[]{:S(2)}, u32[]{:S(2)}) %collective-permute-start.1) | collective-permute-done | bytes 81952 | tf_op jit(solution)/shard_map/ppermute | solution.py:351
  11.6 2.9 %collective-permute-start.2 = (f32[3,32,128]{2,1,0:T(8,128)S(1)}, f32[3,32,128]{2,1,0:T(8,128)S(1)}, u32[]{:S(2)}, u32[]{:S(2)}) collective-permute-start(f32[3,32,128]{2,1,0:T(8,128)S(1)} %get-tuple-element.57), channel_id=1, source_target_pairs={{0,8},{1,9},{2,10},{3,11},{4,12},{5,13},{6,14},{7,15},{8,0},{9,1},... | collective-permute-start | bytes 147464 | tf_op jit(solution)/shard_map/ppermute | solution.py:372
  14.5 1.3 %collective-permute-start.4 = (f32[3,32,128]{2,1,0:T(8,128)S(1)}, f32[3,32,128]{2,1,0:T(8,128)S(1)}, u32[]{:S(2)}, u32[]{:S(2)}) collective-permute-start(f32[3,32,128]{2,1,0:T(8,128)S(1)} %get-tuple-element.57), channel_id=1, source_target_pairs={{0,12},{1,13},{2,14},{3,15},{4,8},{5,9},{6,10},{7,11},{8,4},{9,5},... | collective-permute-start | bytes 147464 | tf_op jit(solution)/shard_map/ppermute | solution.py:372
  15.8 0.2 collective-permute-start.3
  16.1 3.0 %kernels.1 = (bf16[3072,128]{1,0:T(8,128)(2,1)S(1)}, bf16[3072,128]{1,0:T(8,128)(2,1)S(1)}) custom-call(bf16[768,256]{1,0:T(8,128)(2,1)S(1)} %get-tuple-element.61.split_ref, f32[128,128]{1,0:T(8,128)S(1)} %get-tuple-element.62.gains_ref, bf16[128,896]{1,0:T(8,128)(2,1)S(1)} %get-tuple-element.63.sums_ref), custom_call_target="tpu_custom_call" | custom-call | flops 1006632960 | bytes 8388608 | tf_op jit(solution)/shard_map/kernels/pallas_call | solution.py:422
  19.1 0.8 %collective-permute-done.3 = f32[3,32,128]{2,1,0:T(8,128)S(1)} collective-permute-done((f32[3,32,128]{2,1,0:T(8,128)S(1)}, f32[3,32,128]{2,1,0:T(8,128)S(1)}, u32[]{:S(2)}, u32[]{:S(2)}) %collective-permute-start.3) | collective-permute-done | bytes 49184 | tf_op jit(solution)/shard_map/ppermute | solution.py:372
  19.9 0.0 collective-permute-done.2
  19.9 0.5 %collective-permute-done.4 = f32[3,32,128]{2,1,0:T(8,128)S(1)} collective-permute-done((f32[3,32,128]{2,1,0:T(8,128)S(1)}, f32[3,32,128]{2,1,0:T(8,128)S(1)}, u32[]{:S(2)}, u32[]{:S(2)}) %collective-permute-start.4) | collective-permute-done | bytes 49184 | tf_op jit(solution)/shard_map/ppermute | solution.py:372
  20.5 0.1 collective-permute-start.5
  20.6 1.2 %collective-permute-done.5 = f32[4,32,128]{2,1,0:T(8,128)S(1)} collective-permute-done((f32[4,32,128]{2,1,0:T(8,128)S(1)}, f32[4,32,128]{2,1,0:T(8,128)S(1)}, u32[]{:S(2)}, u32[]{:S(2)}) %collective-permute-start.5) | collective-permute-done | bytes 65568 | tf_op jit(solution)/shard_map/ppermute | solution.py:395
  21.9 0.0 copy-done
  21.9 2.7 %stress.1 = (bf16[3072,512]{1,0:T(8,128)(2,1)}, bf16[1152,512]{1,0:T(8,128)(2,1)S(1)}, f32[16,1,512]{2,1,0:T(1,128)}) custom-call(bf16[3072,512]{1,0:T(8,128)(2,1)S(1)} %get-tuple-element.45.cur_ref, bf16[768,128]{1,0:T(8,128)(2,1)S(1)} %get-tuple-element.46.start_ref, f32[768,512]{1,0:T(8,128)S(1)} %get-tuple-element.47.fresh_ref, ...), custom_call_target="tpu_custom_call" | custom-call | flops 805306368 | bytes 10485760 | tf_op jit(solution)/shard_map/stress/pallas_call | solution.py:501
  24.6 4.3 %all-to-all-start = ((f32[16,1,512]{2,1,0:T(1,128)}), f32[16,1,512]{2,1,0:T(1,128)S(1)}, u32[]{:S(2)}, u32[]{:S(2)}) async-start(f32[16,1,512]{2,1,0:T(1,128)} %get-tuple-element.84), calls=%async_computation | async-start | bytes 65536 | tf_op jit(solution)/shard_map/all_to_all | solution.py:518
  28.9 5.0 %adjoint.1 = (bf16[3072,512]{1,0:T(8,128)(2,1)}, bf16[3072,512]{1,0:T(8,128)(2,1)}) custom-call(bf16[3072,512]{1,0:T(8,128)(2,1)} %cot_hbm.3, bf16[3072,512]{1,0:T(8,128)(2,1)} %get-tuple-element.77.early_hbm, bf16[1152,512]{1,0:T(8,128)(2,1)S(1)} %get-tuple-element.78.tail_ref, ...), custom_call_target="tpu_custom_call", output_to_operand_aliasing={{1}: (1, {})} | custom-call | flops 805306368 | bytes 10485760 | tf_op jit(solution)/shard_map/adjoint/pallas_call | solution.py:520
  33.9 1.6 %all-to-all-done = f32[16,1,512]{2,1,0:T(1,128)S(1)} async-done(((f32[16,1,512]{2,1,0:T(1,128)}), f32[16,1,512]{2,1,0:T(1,128)S(1)}, u32[]{:S(2)}, u32[]{:S(2)}) %all-to-all-start) | async-done | bytes 32800 | tf_op jit(solution)/shard_map/all_to_all | solution.py:518
  35.6 0.1 exponential_reduce_fusion
  35.7 0.6 %add_multiply_fusion = f32[512]{0:T(512)} fusion(f32[512]{0:T(512)S(1)} %exponential_reduce_fusion, f32[512]{0:T(512)S(1)} %reduce_max.9), kind=kLoop, calls=%fused_computation.49 | loop fusion | flops 1536 | bytes 6144 | tf_op jit(solution)/shard_map/div | solution.py:547
  (21 shorter events, 0.2 us)
Async XLA Ops:
  4.3 1.4 %collective-permute-start = (f32[5,32,128]{2,1,0:T(8,128)S(1)}, f32[5,32,128]{2,1,0:T(8,128)S(1)}, u32[]{:S(2)}, u32[]{:S(2)}) collective-permute-start(f32[5,32,128]{2,1,0:T(8,128)S(1)} %pad_maximum_fusion), channel_id=1, source_target_pairs={{0,1},{1,0},{2,3},{3,2},{4,5},{5,4},{6,7},{7,6},{8,9},{9,8},{10,11... | collective-permute-start | bytes 245768 | tf_op jit(solution)/shard_map/ppermute | solution.py:327
  5.8 16.1 %copy-start = (s32[512]{0:T(512)S(1)}, s32[512]{0:T(512)}, u32[]{:S(2)}) copy-start(s32[512]{0:T(512)} %param.11) | copy-start | bytes 6148
  5.8 5.7 %collective-permute-start.1 = (f32[5,32,128]{2,1,0:T(8,128)S(1)}, f32[5,32,128]{2,1,0:T(8,128)S(1)}, u32[]{:S(2)}, u32[]{:S(2)}) collective-permute-start(f32[5,32,128]{2,1,0:T(8,128)S(1)} %pad_maximum_fusion.1), channel_id=1, source_target_pairs={{0,2},{1,3},{2,0},{3,1},{4,6},{5,7},{6,4},{7,5},{8,10},{9,11},{10,... | collective-permute-start | bytes 245768 | tf_op jit(solution)/shard_map/ppermute | solution.py:351
  11.6 8.3 %collective-permute-start.2 = (f32[3,32,128]{2,1,0:T(8,128)S(1)}, f32[3,32,128]{2,1,0:T(8,128)S(1)}, u32[]{:S(2)}, u32[]{:S(2)}) collective-permute-start(f32[3,32,128]{2,1,0:T(8,128)S(1)} %get-tuple-element.57), channel_id=1, source_target_pairs={{0,8},{1,9},{2,10},{3,11},{4,12},{5,13},{6,14},{7,15},{8,0},{9,1},... | collective-permute-start | bytes 147464 | tf_op jit(solution)/shard_map/ppermute | solution.py:372
  14.5 6.0 %collective-permute-start.4 = (f32[3,32,128]{2,1,0:T(8,128)S(1)}, f32[3,32,128]{2,1,0:T(8,128)S(1)}, u32[]{:S(2)}, u32[]{:S(2)}) collective-permute-start(f32[3,32,128]{2,1,0:T(8,128)S(1)} %get-tuple-element.57), channel_id=1, source_target_pairs={{0,12},{1,13},{2,14},{3,15},{4,8},{5,9},{6,10},{7,11},{8,4},{9,5},... | collective-permute-start | bytes 147464 | tf_op jit(solution)/shard_map/ppermute | solution.py:372
  15.8 4.1 %collective-permute-start.3 = (f32[3,32,128]{2,1,0:T(8,128)S(1)}, f32[3,32,128]{2,1,0:T(8,128)S(1)}, u32[]{:S(2)}, u32[]{:S(2)}) collective-permute-start(f32[3,32,128]{2,1,0:T(8,128)S(1)} %get-tuple-element.60), channel_id=1, source_target_pairs={{0,4},{1,5},{2,6},{3,7},{4,0},{5,1},{6,2},{7,3},{8,12},{9,13},{10,... | collective-permute-start | bytes 147464 | tf_op jit(solution)/shard_map/ppermute | solution.py:372
  20.5 1.3 %collective-permute-start.5 = (f32[4,32,128]{2,1,0:T(8,128)S(1)}, f32[4,32,128]{2,1,0:T(8,128)S(1)}, u32[]{:S(2)}, u32[]{:S(2)}) collective-permute-start(f32[4,32,128]{2,1,0:T(8,128)S(1)} %pad_maximum_fusion.3), channel_id=1, source_target_pairs={{0,1},{1,0},{2,3},{3,2},{4,5},{5,4},{6,7},{7,6},{8,9},{9,8},{10,11... | collective-permute-start | bytes 196616 | tf_op jit(solution)/shard_map/ppermute | solution.py:395
  24.6 11.0 %all-to-all-start = ((f32[16,1,512]{2,1,0:T(1,128)}), f32[16,1,512]{2,1,0:T(1,128)S(1)}, u32[]{:S(2)}, u32[]{:S(2)}) async-start(f32[16,1,512]{2,1,0:T(1,128)} %get-tuple-element.84), calls=%async_computation | async-start | bytes 65536 | tf_op jit(solution)/shard_map/all_to_all | solution.py:518

commit v9 on v7

--- a/solution.py
+++ b/solution.py
@@ -376,10 +376,10 @@
     quarter = hops[-2]
     got = [
         lax.ppermute(sent, "tm", [(i, i ^ hop) for i in range(n)])
-        for sent, hop in ((to_far, 2 * quarter), (to_near, quarter), (to_far, 3 * quarter))
+        for sent, hop in ((to_near, quarter), (to_far, 2 * quarter), (to_far, 3 * quarter))
     ]
     got = run_part(parts - 1, tuple(got))
-    (x2, d2), (x1, d1), (x3, d3) = [(g[:half], g[half:]) for g in got]
+    (x1, d1), (x2, d2), (x3, d3) = [(g[:half], g[half:]) for g in got]
     others_f = jnp.where(
         far,
         jnp.where(near, (x3 * d2 + x2) * d1 + x1, d3 * x2 + x3),

time: 36.5 us -> 36.5 us (level)
  no operation moved by 1% of the time
where the time goes in v9:
time: 36.5 us; the launch traced here: 36.3 us
  Pallas kernels  14.3 us (39%)
  starting transfers between devices  12.3 us (34%)
  waiting for transfers between devices  7.95 us (22%)
  other arithmetic  0.91 us (2%)
  between operations  0.82 us (2%)
    pallas_call x1, Pallas kernels, body(): pl.pallas_call(adjoint_kernel, name='adjoint', in_specs=[apart] * 2 + [wh...  4.93 us
    ppermute x3, starting transfers between devices, scan_devices(): lax.ppermute(sent, 'tm', [(i, i ^ hop) for i in range(n)])  4.46 us
    all_to_all x1, starting transfers between devices, body(): all_lse = lax.all_to_all(lse, 'tm', 0, 0, tiled=True)  4.34 us
    pallas_call x1, Pallas kernels, body(): pl.pallas_call(totals_kernel, name='totals', in_specs=[apart] * 5, out_sp...  3.61 us
    pallas_call x1, Pallas kernels, __call__(): pl.pallas_call(functools.partial(kernels_kernel, self.modes, sum(self.cou...  3.03 us
    ppermute x1, starting transfers between devices, scan_devices(): got = lax.ppermute(msg, 'tm', [(i, i ^ hop) for i in range(n)])  2.93 us
    ppermute x1, waiting for transfers between devices, scan_devices(): got = lax.ppermute(msg, 'tm', [(i, i ^ hop) for i in range(n)])  2.76 us
    pallas_call x1, Pallas kernels, body(): pl.pallas_call(stress_kernel, name='stress', in_specs=[whole] * (6 + part...  2.68 us
  transfers between devices with their start and end apart: 7, of which 6 were waited for; matrix products, arithmetic and copies ran while one was open for 0% of the time, Pallas kernels for 22%

profile of v9, /device:TPU:0, one launch (start us, length us, event | category | flops | bytes accessed | tf_op | source)
XLA Modules:
  0.0 36.3 jit_solution(16953305865783296421)
XLA Ops:
  0.6 3.6 %totals.1 = (bf16[3072,512]{1,0:T(8,128)(2,1)S(1)}, f32[768,512]{1,0:T(8,128)S(1)}, bf16[768,512]{1,0:T(8,128)(2,1)S(1)}, f32[768,128]{1,0:T(8,128)S(1)}, f32[9,...) custom-call(f32[32,3072]{1,0:T(8,128)} %heat_hbm.1, ...), custom_call_target="tpu_custom_call" | custom-call | flops 201326592 | bytes 14680064 | tf_op jit(solution)/shard_map/totals/pallas_call | solution.py:462
  4.3 0.5 %collective-permute-start = (f32[5,32,128]{2,1,0:T(8,128)S(1)}, f32[5,32,128]{2,1,0:T(8,128)S(1)}, u32[]{:S(2)}, u32[]{:S(2)}) collective-permute-start(f32[5,32,128]{2,1,0:T(8,128)S(1)} %pad_maximum_fusion), channel_id=1, source_target_pairs={{0,1},{1,0},{2,3},{3,2},{4,5},{5,4},{6,7},{7,6},{8,9},{9,8},{10,11... | collective-permute-start | bytes 245768 | tf_op jit(solution)/shard_map/ppermute | solution.py:333
  4.8 0.9 %collective-permute-done = f32[5,32,128]{2,1,0:T(8,128)S(1)} collective-permute-done((f32[5,32,128]{2,1,0:T(8,128)S(1)}, f32[5,32,128]{2,1,0:T(8,128)S(1)}, u32[]{:S(2)}, u32[]{:S(2)}) %collective-permute-start) | collective-permute-done | bytes 81952 | tf_op jit(solution)/shard_map/ppermute | solution.py:333
  5.8 0.0 copy-start
  5.8 2.9 %collective-permute-start.1 = (f32[5,32,128]{2,1,0:T(8,128)S(1)}, f32[5,32,128]{2,1,0:T(8,128)S(1)}, u32[]{:S(2)}, u32[]{:S(2)}) collective-permute-start(f32[5,32,128]{2,1,0:T(8,128)S(1)} %pad_maximum_fusion.1), channel_id=1, source_target_pairs={{0,2},{1,3},{2,0},{3,1},{4,6},{5,7},{6,4},{7,5},{8,10},{9,11},{10,... | collective-permute-start | bytes 245768 | tf_op jit(solution)/shard_map/ppermute | solution.py:357
  8.7 2.8 %collective-permute-done.1 = f32[5,32,128]{2,1,0:T(8,128)S(1)} collective-permute-done((f32[5,32,128]{2,1,0:T(8,128)S(1)}, f32[5,32,128]{2,1,0:T(8,128)S(1)}, u32[]{:S(2)}, u32[]{:S(2)}) %collective-permute-start.1) | collective-permute-done | bytes 81952 | tf_op jit(solution)/shard_map/ppermute | solution.py:357
  11.6 2.9 %collective-permute-start.3 = (f32[3,32,128]{2,1,0:T(8,128)S(1)}, f32[3,32,128]{2,1,0:T(8,128)S(1)}, u32[]{:S(2)}, u32[]{:S(2)}) collective-permute-start(f32[3,32,128]{2,1,0:T(8,128)S(1)} %get-tuple-element.60), channel_id=1, source_target_pairs={{0,8},{1,9},{2,10},{3,11},{4,12},{5,13},{6,14},{7,15},{8,0},{9,1},... | collective-permute-start | bytes 147464 | tf_op jit(solution)/shard_map/ppermute | solution.py:378
  14.5 1.3 %collective-permute-start.4 = (f32[3,32,128]{2,1,0:T(8,128)S(1)}, f32[3,32,128]{2,1,0:T(8,128)S(1)}, u32[]{:S(2)}, u32[]{:S(2)}) collective-permute-start(f32[3,32,128]{2,1,0:T(8,128)S(1)} %get-tuple-element.60), channel_id=1, source_target_pairs={{0,12},{1,13},{2,14},{3,15},{4,8},{5,9},{6,10},{7,11},{8,4},{9,5},... | collective-permute-start | bytes 147464 | tf_op jit(solution)/shard_map/ppermute | solution.py:378
  15.8 0.2 collective-permute-start.2
  16.1 3.0 %kernels.1 = (bf16[3072,128]{1,0:T(8,128)(2,1)S(1)}, bf16[3072,128]{1,0:T(8,128)(2,1)S(1)}) custom-call(bf16[768,256]{1,0:T(8,128)(2,1)S(1)} %get-tuple-element.61.split_ref, f32[128,128]{1,0:T(8,128)S(1)} %get-tuple-element.62.gains_ref, bf16[128,896]{1,0:T(8,128)(2,1)S(1)} %get-tuple-element.63.sums_ref), custom_call_target="tpu_custom_call" | custom-call | flops 1006632960 | bytes 8388608 | tf_op jit(solution)/shard_map/kernels/pallas_call | solution.py:428
  19.1 0.8 %collective-permute-done.2 = f32[3,32,128]{2,1,0:T(8,128)S(1)} collective-permute-done((f32[3,32,128]{2,1,0:T(8,128)S(1)}, f32[3,32,128]{2,1,0:T(8,128)S(1)}, u32[]{:S(2)}, u32[]{:S(2)}) %collective-permute-start.2) | collective-permute-done | bytes 49184 | tf_op jit(solution)/shard_map/ppermute | solution.py:378
  19.9 0.0 collective-permute-done.3
  19.9 0.5 %collective-permute-done.4 = f32[3,32,128]{2,1,0:T(8,128)S(1)} collective-permute-done((f32[3,32,128]{2,1,0:T(8,128)S(1)}, f32[3,32,128]{2,1,0:T(8,128)S(1)}, u32[]{:S(2)}, u32[]{:S(2)}) %collective-permute-start.4) | collective-permute-done | bytes 49184 | tf_op jit(solution)/shard_map/ppermute | solution.py:378
  20.5 0.1 collective-permute-start.5
  20.6 1.2 %collective-permute-done.5 = f32[4,32,128]{2,1,0:T(8,128)S(1)} collective-permute-done((f32[4,32,128]{2,1,0:T(8,128)S(1)}, f32[4,32,128]{2,1,0:T(8,128)S(1)}, u32[]{:S(2)}, u32[]{:S(2)}) %collective-permute-start.5) | collective-permute-done | bytes 65568 | tf_op jit(solution)/shard_map/ppermute | solution.py:401
  21.9 0.0 copy-done
  21.9 2.7 %stress.1 = (bf16[3072,512]{1,0:T(8,128)(2,1)}, bf16[1152,512]{1,0:T(8,128)(2,1)S(1)}, f32[16,1,512]{2,1,0:T(1,128)}) custom-call(bf16[3072,512]{1,0:T(8,128)(2,1)S(1)} %get-tuple-element.45.cur_ref, bf16[768,128]{1,0:T(8,128)(2,1)S(1)} %get-tuple-element.46.start_ref, f32[768,512]{1,0:T(8,128)S(1)} %get-tuple-element.47.fresh_ref, ...), custom_call_target="tpu_custom_call" | custom-call | flops 805306368 | bytes 10485760 | tf_op jit(solution)/shard_map/stress/pallas_call | solution.py:507
  24.6 4.3 %all-to-all-start = ((f32[16,1,512]{2,1,0:T(1,128)}), f32[16,1,512]{2,1,0:T(1,128)S(1)}, u32[]{:S(2)}, u32[]{:S(2)}) async-start(f32[16,1,512]{2,1,0:T(1,128)} %get-tuple-element.84), calls=%async_computation | async-start | bytes 65536 | tf_op jit(solution)/shard_map/all_to_all | solution.py:524
  28.9 4.9 %adjoint.1 = (bf16[3072,512]{1,0:T(8,128)(2,1)}, bf16[3072,512]{1,0:T(8,128)(2,1)}) custom-call(bf16[3072,512]{1,0:T(8,128)(2,1)} %cot_hbm.3, bf16[3072,512]{1,0:T(8,128)(2,1)} %get-tuple-element.77.early_hbm, bf16[1152,512]{1,0:T(8,128)(2,1)S(1)} %get-tuple-element.78.tail_ref, ...), custom_call_target="tpu_custom_call", output_to_operand_aliasing={{1}: (1, {})} | custom-call | flops 805306368 | bytes 10485760 | tf_op jit(solution)/shard_map/adjoint/pallas_call | solution.py:526
  33.9 1.7 %all-to-all-done = f32[16,1,512]{2,1,0:T(1,128)S(1)} async-done(((f32[16,1,512]{2,1,0:T(1,128)}), f32[16,1,512]{2,1,0:T(1,128)S(1)}, u32[]{:S(2)}, u32[]{:S(2)}) %all-to-all-start) | async-done | bytes 32800 | tf_op jit(solution)/shard_map/all_to_all | solution.py:524
  35.6 0.1 exponential_reduce_fusion
  35.7 0.6 %add_multiply_fusion = f32[512]{0:T(512)} fusion(f32[512]{0:T(512)S(1)} %exponential_reduce_fusion, f32[512]{0:T(512)S(1)} %reduce_max.9), kind=kLoop, calls=%fused_computation.49 | loop fusion | flops 1536 | bytes 6144 | tf_op jit(solution)/shard_map/div | solution.py:553
  (21 shorter events, 0.2 us)
Async XLA Ops:
  4.3 1.4 %collective-permute-start = (f32[5,32,128]{2,1,0:T(8,128)S(1)}, f32[5,32,128]{2,1,0:T(8,128)S(1)}, u32[]{:S(2)}, u32[]{:S(2)}) collective-permute-start(f32[5,32,128]{2,1,0:T(8,128)S(1)} %pad_maximum_fusion), channel_id=1, source_target_pairs={{0,1},{1,0},{2,3},{3,2},{4,5},{5,4},{6,7},{7,6},{8,9},{9,8},{10,11... | collective-permute-start | bytes 245768 | tf_op jit(solution)/shard_map/ppermute | solution.py:333
  5.8 16.1 %copy-start = (s32[512]{0:T(512)S(1)}, s32[512]{0:T(512)}, u32[]{:S(2)}) copy-start(s32[512]{0:T(512)} %param.11) | copy-start | bytes 6148
  5.8 5.7 %collective-permute-start.1 = (f32[5,32,128]{2,1,0:T(8,128)S(1)}, f32[5,32,128]{2,1,0:T(8,128)S(1)}, u32[]{:S(2)}, u32[]{:S(2)}) collective-permute-start(f32[5,32,128]{2,1,0:T(8,128)S(1)} %pad_maximum_fusion.1), channel_id=1, source_target_pairs={{0,2},{1,3},{2,0},{3,1},{4,6},{5,7},{6,4},{7,5},{8,10},{9,11},{10,... | collective-permute-start | bytes 245768 | tf_op jit(solution)/shard_map/ppermute | solution.py:357
  11.6 8.3 %collective-permute-start.3 = (f32[3,32,128]{2,1,0:T(8,128)S(1)}, f32[3,32,128]{2,1,0:T(8,128)S(1)}, u32[]{:S(2)}, u32[]{:S(2)}) collective-permute-start(f32[3,32,128]{2,1,0:T(8,128)S(1)} %get-tuple-element.60), channel_id=1, source_target_pairs={{0,8},{1,9},{2,10},{3,11},{4,12},{5,13},{6,14},{7,15},{8,0},{9,1},... | collective-permute-start | bytes 147464 | tf_op jit(solution)/shard_map/ppermute | solution.py:378
  14.5 6.0 %collective-permute-start.4 = (f32[3,32,128]{2,1,0:T(8,128)S(1)}, f32[3,32,128]{2,1,0:T(8,128)S(1)}, u32[]{:S(2)}, u32[]{:S(2)}) collective-permute-start(f32[3,32,128]{2,1,0:T(8,128)S(1)} %get-tuple-element.60), channel_id=1, source_target_pairs={{0,12},{1,13},{2,14},{3,15},{4,8},{5,9},{6,10},{7,11},{8,4},{9,5},... | collective-permute-start | bytes 147464 | tf_op jit(solution)/shard_map/ppermute | solution.py:378
  15.8 4.1 %collective-permute-start.2 = (f32[3,32,128]{2,1,0:T(8,128)S(1)}, f32[3,32,128]{2,1,0:T(8,128)S(1)}, u32[]{:S(2)}, u32[]{:S(2)}) collective-permute-start(f32[3,32,128]{2,1,0:T(8,128)S(1)} %get-tuple-element.59), channel_id=1, source_target_pairs={{0,4},{1,5},{2,6},{3,7},{4,0},{5,1},{6,2},{7,3},{8,12},{9,13},{10,... | collective-permute-start | bytes 147464 | tf_op jit(solution)/shard_map/ppermute | solution.py:378
  20.5 1.3 %collective-permute-start.5 = (f32[4,32,128]{2,1,0:T(8,128)S(1)}, f32[4,32,128]{2,1,0:T(8,128)S(1)}, u32[]{:S(2)}, u32[]{:S(2)}) collective-permute-start(f32[4,32,128]{2,1,0:T(8,128)S(1)} %pad_maximum_fusion.3), channel_id=1, source_target_pairs={{0,1},{1,0},{2,3},{3,2},{4,5},{5,4},{6,7},{7,6},{8,9},{9,8},{10,11... | collective-permute-start | bytes 196616 | tf_op jit(solution)/shard_map/ppermute | solution.py:401
  24.6 11.0 %all-to-all-start = ((f32[16,1,512]{2,1,0:T(1,128)}), f32[16,1,512]{2,1,0:T(1,128)S(1)}, u32[]{:S(2)}, u32[]{:S(2)}) async-start(f32[16,1,512]{2,1,0:T(1,128)} %get-tuple-element.84), calls=%async_computation | async-start | bytes 65536 | tf_op jit(solution)/shard_map/all_to_all | solution.py:524
